TPU v7x, 512 devices: a whole 4x8x8 slice. The times are simulated.
512 devices in a mesh: ctx: 128 (over y, z, core), head: 4 (over x).
Axes of the slice: x: 4, y: 8, z: 8, core: 2. Of those that a mesh axis runs over, the one named last changes fastest.
Arguments:
- queries: bfloat16 [65536, 8192], P(('ctx', 'head')), may hold values from -6 to 6
- key_rows: bfloat16 [65536, 1024], P(('ctx', 'head')), may hold values from -6 to 6
- value_rows: bfloat16 [65536, 1024], P(('ctx', 'head')), may hold values from -6 to 6
- doc_lengths: int32 [128], replicated, may hold values from 1 to 384, 32768 in all
Outputs:
- attended: bfloat16 [65536, 8192], P('ctx', 'head')
All inputs are finite; a program needn't handle non-finite values.
Results may differ from a plain program's by a relative error of at most 0.0036.
Values may be sent and summed in bfloat16 or wider, within the bound.
No kernel may reach another device: no remote copies, remote signals or barrier semaphores. Data moves between devices by JAX's collectives and lax.ppermute only.
A program may use at most 64 MiB of HBM per device.

v0:
```python
import jax
import jax.numpy as jnp
from jax import lax
from jax.sharding import PartitionSpec as P

HEAD_DIM = 128
REACH = 3


def shifted(block, axis, distance):
    devices = range(lax.axis_size(axis))
    route = [(i - distance, i) for i in devices if i - distance in devices]
    return lax.ppermute(block, axis, route)


def doc_of(positions, starts):
    marks = (starts[None, :] <= positions[:, None]).astype(jnp.int32)
    return jnp.sum(marks, axis=1) - 1


def lane_attention(
    query_lane, key_cat, value_cat, query_pos, query_doc, key_pos, key_doc, key_valid
):
    row_count = query_lane.shape[0]
    key_count = key_cat.shape[0]
    kv_local = key_cat.shape[1] // HEAD_DIM
    group = query_lane.shape[1] // (kv_local * HEAD_DIM)
    scale = HEAD_DIM ** (-0.5)
    query_items = jnp.transpose(
        query_lane.reshape(row_count, kv_local, group, HEAD_DIM), (1, 2, 0, 3)
    )
    key_items = jnp.transpose(key_cat.reshape(key_count, kv_local, HEAD_DIM), (1, 0, 2))
    value_items = jnp.transpose(value_cat.reshape(key_count, kv_local, HEAD_DIM), (1, 0, 2))
    allowed = (
        (key_doc[None, :] == query_doc[:, None])
        & (key_pos[None, :] <= query_pos[:, None])
        & key_valid[None, :]
    )

    def one_group(operands):
        query_group, key_group, value_group = operands
        scores = (
            jnp.einsum("jqd,kd->jqk", query_group, key_group, preferred_element_type=jnp.float32)
            * scale
        )
        scores = jnp.where(allowed[None], scores, -jnp.inf)
        row_max = jnp.max(scores, axis=-1, keepdims=True)
        raised = jnp.exp(scores - row_max)
        denominator = jnp.sum(raised, axis=-1, keepdims=True)
        weights = raised.astype(jnp.bfloat16)
        mixed_values = jnp.einsum(
            "jqk,kd->jqd", weights, value_group, preferred_element_type=jnp.float32
        )
        return (mixed_values / denominator).astype(jnp.bfloat16)

    results = lax.map(one_group, (query_items, key_items, value_items))
    return jnp.transpose(results, (2, 0, 1, 3)).reshape(row_count, kv_local * group * HEAD_DIM)


def run_lane(
    block_total,
    query_lane,
    key_blocks,
    value_blocks,
    pos_blocks,
    valid_blocks,
    query_pos,
    query_doc,
    starts,
):
    key_cat = jnp.concatenate(key_blocks[:block_total], axis=0)
    value_cat = jnp.concatenate(value_blocks[:block_total], axis=0)
    key_pos = jnp.concatenate(pos_blocks[:block_total], axis=0)
    key_valid = jnp.concatenate(valid_blocks[:block_total], axis=0)
    key_doc = doc_of(key_pos, starts)
    return lane_attention(
        query_lane, key_cat, value_cat, query_pos, query_doc, key_pos, key_doc, key_valid
    )


def body(queries, key_rows, value_rows, doc_lengths):
    query_all, key_all, value_all = (
        lax.all_to_all(queries, "head", split_axis=1, concat_axis=0, tiled=True),
        lax.all_to_all(key_rows, "head", split_axis=1, concat_axis=0, tiled=True),
        lax.all_to_all(value_rows, "head", split_axis=1, concat_axis=0, tiled=True),
    )
    row_count = query_all.shape[0]
    half_rows = row_count // 2
    width = key_all.shape[1]
    own_pair = jnp.stack([key_all, value_all]).reshape(2, 2, half_rows, width)
    device_count = lax.axis_size("ctx")
    own_index = lax.axis_index("ctx")
    lower_list = []
    upper_list = []
    for offset in range(1, REACH + 1):
        lower_list.append(shifted(own_pair, "ctx", offset))
        upper_list.append(shifted(own_pair, "ctx", -offset))
    table = jnp.stack(lower_list[::-1] + [own_pair] + upper_list)
    sizes = doc_lengths * 2
    starts = jnp.cumsum(sizes) - sizes
    stretch_total = 2 * device_count
    span = jnp.arange(half_rows, dtype=jnp.int32)
    outputs = []
    for lane_index in range(2):
        if lane_index == 0:
            first_stretch = own_index
        else:
            first_stretch = stretch_total - 1 - own_index
        query_lane = query_all[lane_index * half_rows : (lane_index + 1) * half_rows]
        query_pos = first_stretch * half_rows + span
        query_doc = doc_of(query_pos, starts)
        key_blocks = []
        value_blocks = []
        pos_blocks = []
        valid_blocks = []
        for back in range(REACH + 1):
            stretch_id = first_stretch - back
            holder = jnp.where(
                stretch_id < device_count, stretch_id, stretch_total - 1 - stretch_id
            )
            side_index = jnp.where(stretch_id < device_count, 0, 1).astype(jnp.int32)
            slot_index = jnp.clip(holder - own_index + REACH, 0, 2 * REACH)
            picked = lax.dynamic_index_in_dim(table, slot_index, 0, keepdims=False)
            picked = lax.dynamic_index_in_dim(picked, side_index, 1, keepdims=False)
            key_blocks.append(picked[0])
            value_blocks.append(picked[1])
            pos_blocks.append(stretch_id * half_rows + span)
            valid_blocks.append(jnp.broadcast_to(stretch_id >= 0, (half_rows,)))
        lane_out = run_lane(
            REACH + 1,
            query_lane,
            key_blocks,
            value_blocks,
            pos_blocks,
            valid_blocks,
            query_pos,
            query_doc,
            starts,
        )
        outputs.append(lane_out)
    return jnp.concatenate(outputs, axis=0)


def solution(mesh):
    placed = (P(("ctx", "head"), None), P(("ctx", "head"), None), P(("ctx", "head"), None), P())
    return jax.shard_map(
        body, mesh=mesh, in_specs=placed, out_specs=P("ctx", "head"), check_vma=False
    )
```

profile of v0, /device:TPU:1, one launch (start us, length us, event | category | flops | bytes accessed | tf_op | source)
XLA Modules:
  0.0 141.3 jit_solution(9283019938555628155)
XLA Ops:
  0.0 1.8 %copy.67 = bf16[128,1024]{0,1:T(8,128)(2,1)} copy(bf16[128,1024]{1,0:T(8,128)(2,1)} %param.9) | data formatting | bytes 524288 | tf_op args[1]
  1.8 4.8 %all-to-all-start.1 = ((bf16[128,4,256]{0,2,1:T(8,128)(2,1)}), bf16[128,4,256]{0,2,1:T(8,128)(2,1)S(1)}, u32[]{:S(2)}, u32[]{:S(2)}) async-start(bf16[128,4,256]{0,2,1:T(8,128)(2,1)} %bitcast.2), calls=%async_computation.1 | async-start | bytes 524288 | tf_op jit(solution)/shard_map/all_to_all | solution.py:84
  6.6 1.8 %copy.69 = bf16[128,1024]{0,1:T(8,128)(2,1)} copy(bf16[128,1024]{1,0:T(8,128)(2,1)} %param.10) | data formatting | bytes 524288 | tf_op args[2]
  10.2 3.2 %copy.120 = bf16[16,4,8,2048]{3,2,0,1:T(8,128)(2,1)} copy(bf16[16,4,8,2048]{3,2,1,0:T(8,128)(2,1)} %bitcast.148) | data formatting | bytes 4194304 | tf_op jit(solution)/shard_map/all_to_all | solution.py:83
  14.0 4.2 %all-to-all-start.2 = ((bf16[128,4,256]{0,2,1:T(8,128)(2,1)}), bf16[128,4,256]{0,2,1:T(8,128)(2,1)S(1)}, u32[]{:S(2)}, u32[]{:S(2)}) async-start(bf16[128,4,256]{0,2,1:T(8,128)(2,1)} %bitcast.5), calls=%async_computation.2 | async-start | bytes 524288 | tf_op jit(solution)/shard_map/all_to_all | solution.py:85
  18.4 5.4 %all-to-all-done.2 = bf16[128,4,256]{0,2,1:T(8,128)(2,1)S(1)} async-done(((bf16[128,4,256]{0,2,1:T(8,128)(2,1)}), bf16[128,4,256]{0,2,1:T(8,128)(2,1)S(1)}, u32[]{:S(2)}, u32[]{:S(2)}) %all-to-all-start.2) | async-done | bytes 262176 | tf_op jit(solution)/shard_map/all_to_all | solution.py:85
  23.8 3.6 %all-to-all-start = ((bf16[128,4,2048]{2,0,1:T(8,128)(2,1)}), bf16[128,4,2048]{2,0,1:T(8,128)(2,1)S(1)}, u32[]{:S(2)}, u32[]{:S(2)}) async-start(bf16[128,4,2048]{2,0,1:T(8,128)(2,1)} %bitcast.114), calls=%async_computation | async-start | bytes 4194304 | tf_op jit(solution)/shard_map/all_to_all | solution.py:83
  27.6 9.2 %collective-permute-start = (bf16[2,2,256,256]{3,2,1,0:T(8,128)(2,1)S(1)}, bf16[2,2,256,256]{3,2,1,0:T(8,128)(2,1)}, u32[]{:S(2)}, u32[]{:S(2)}) collective-permute-start(bf16[2,2,256,256]{3,2,1,0:T(8,128)(2,1)S(1)} %pad_maximum_fusion.1), channel_id=1, source_target_pairs={{0,12},{4,16},{8,20},{12,24},{16,28},{20,32},{24,36},{28,40},{32,4... | collective-permute-start | bytes 1572872 | tf_op jit(solution)/shard_map/ppermute | solution.py:13
  37.1 4.0 %collective-permute-start.1 = (bf16[2,2,256,256]{3,2,1,0:T(8,128)(2,1)S(1)}, bf16[2,2,256,256]{3,2,1,0:T(8,128)(2,1)}, u32[]{:S(2)}, u32[]{:S(2)}) collective-permute-start(bf16[2,2,256,256]{3,2,1,0:T(8,128)(2,1)S(1)} %pad_maximum_fusion.1), channel_id=1, source_target_pairs={{0,8},{4,12},{8,16},{12,20},{16,24},{20,28},{24,32},{28,36},{32,40... | collective-permute-start | bytes 1572872 | tf_op jit(solution)/shard_map/ppermute | solution.py:13
  42.2 1.9 %collective-permute-start.2 = (bf16[2,2,256,256]{3,2,1,0:T(8,128)(2,1)S(1)}, bf16[2,2,256,256]{3,2,1,0:T(8,128)(2,1)}, u32[]{:S(2)}, u32[]{:S(2)}) collective-permute-start(bf16[2,2,256,256]{3,2,1,0:T(8,128)(2,1)S(1)} %pad_maximum_fusion.1), channel_id=1, source_target_pairs={{0,4},{4,8},{8,12},{12,16},{16,20},{20,24},{24,28},{28,32},{32,36}... | collective-permute-start | bytes 1572872 | tf_op jit(solution)/shard_map/ppermute | solution.py:13
  44.8 3.2 %collective-permute-start.3 = (bf16[2,2,256,256]{3,2,1,0:T(8,128)(2,1)S(1)}, bf16[2,2,256,256]{3,2,1,0:T(8,128)(2,1)S(1)}, u32[]{:S(2)}, u32[]{:S(2)}) collective-permute-start(bf16[2,2,256,256]{3,2,1,0:T(8,128)(2,1)S(1)} %pad_maximum_fusion.1), channel_id=1, source_target_pairs={{4,0},{8,4},{12,8},{16,12},{20,16},{24,20},{28,24},{32,28},{36,32}... | collective-permute-start | bytes 1572872 | tf_op jit(solution)/shard_map/ppermute | solution.py:13
  51.7 7.1 %collective-permute-done.1 = bf16[2,2,256,256]{3,2,1,0:T(8,128)(2,1)} collective-permute-done((bf16[2,2,256,256]{3,2,1,0:T(8,128)(2,1)S(1)}, bf16[2,2,256,256]{3,2,1,0:T(8,128)(2,1)}, u32[]{:S(2)}, u32[]{:S(2)}) %collective-permute-start.1) | collective-permute-done | bytes 524320 | tf_op jit(solution)/shard_map/ppermute | solution.py:13
  59.8 4.8 %collective-permute-done.2 = bf16[2,2,256,256]{3,2,1,0:T(8,128)(2,1)} collective-permute-done((bf16[2,2,256,256]{3,2,1,0:T(8,128)(2,1)S(1)}, bf16[2,2,256,256]{3,2,1,0:T(8,128)(2,1)}, u32[]{:S(2)}, u32[]{:S(2)}) %collective-permute-start.2) | collective-permute-done | bytes 524320 | tf_op jit(solution)/shard_map/ppermute | solution.py:13
  65.8 19.7 %collective-permute-done.5 = bf16[2,2,256,256]{3,2,1,0:T(8,128)(2,1)S(1)} collective-permute-done((bf16[2,2,256,256]{3,2,1,0:T(8,128)(2,1)S(1)}, bf16[2,2,256,256]{3,2,1,0:T(8,128)(2,1)S(1)}, u32[]{:S(2)}, u32[]{:S(2)}) %collective-permute-start.5) | collective-permute-done | bytes 524320 | tf_op jit(solution)/shard_map/ppermute | solution.py:13
  86.6 1.7 %copy.73 = bf16[1,1,1,256,256]{3,4,2,1,0:T(8,128)(2,1)} copy(bf16[1,1,1,256,256]{4,3,2,1,0:T(8,128)(2,1)} %get-tuple-element.241) | data formatting | bytes 262144 | tf_op jit(solution)/shard_map/slice | solution.py:125
  88.3 1.7 %copy.74 = bf16[1,1,1,256,256]{3,4,2,1,0:T(8,128)(2,1)} copy(bf16[1,1,1,256,256]{4,3,2,1,0:T(8,128)(2,1)} %get-tuple-element.240) | data formatting | bytes 262144 | tf_op jit(solution)/shard_map/slice | solution.py:125
  89.9 1.7 %copy.75 = bf16[1,1,1,256,256]{3,4,2,1,0:T(8,128)(2,1)} copy(bf16[1,1,1,256,256]{4,3,2,1,0:T(8,128)(2,1)} %get-tuple-element.239) | data formatting | bytes 262144 | tf_op jit(solution)/shard_map/slice | solution.py:125
  91.6 1.7 %copy.76 = bf16[1,1,1,256,256]{3,4,2,1,0:T(8,128)(2,1)} copy(bf16[1,1,1,256,256]{4,3,2,1,0:T(8,128)(2,1)} %get-tuple-element.238) | data formatting | bytes 262144 | tf_op jit(solution)/shard_map/slice | solution.py:125
  93.3 1.7 %copy.77 = bf16[1,1,1,256,256]{3,4,2,1,0:T(8,128)(2,1)} copy(bf16[1,1,1,256,256]{4,3,2,1,0:T(8,128)(2,1)} %get-tuple-element.233) | data formatting | bytes 262144 | tf_op jit(solution)/shard_map/slice | solution.py:126
  101.2 2.2 %maximum_bitcast_fusion = (bf16[2,1024,128]{1,2,0:T(8,128)(2,1)S(1)}, bf16[2,1024,128]{1,2,0:T(8,128)(2,1)}) fusion(bf16[256,2,128]{0,2,1:T(8,128)(2,1)} %bitcast.154, bf16[256,2,128]{0,2,1:T(8,128)(2,1)} %bitcast.153, bf16[256,2,128]{0,2,1:T(8,128)(2,1)} %bitcast.152, bf16[256,2,128]{0,2,1:T(8,128)(2,1)} %bitcast.151, bf16[256,2,128]{0,2,1:T(8,128)(2,1)} %bitcast.160, ...), kind=kLoop, calls=%fused_computation.52 | loop fusion | flops 4194304 | bytes 2097152 | tf_op jit(solution)/shard_map/transpose | solution.py:32
  103.4 2.2 %maximum_bitcast_fusion.2 = (bf16[2,1024,128]{1,2,0:T(8,128)(2,1)S(1)}, bf16[2,1024,128]{1,2,0:T(8,128)(2,1)}) fusion(bf16[256,2,128]{0,2,1:T(8,128)(2,1)} %bitcast.162, bf16[256,2,128]{0,2,1:T(8,128)(2,1)} %bitcast.161, bf16[256,2,128]{0,2,1:T(8,128)(2,1)S(1)} %bitcast.159, bf16[256,2,128]{0,2,1:T(8,128)(2,1)S(1)} %bitcast.157, ...), kind=kLoop, calls=%fused_computation.54 | loop fusion | flops 4194304 | bytes 2097152 | tf_op jit(solution)/shard_map/transpose | solution.py:32
  107.2 13.4 %while.22 = (s32[]{:T(128)}, bf16[2,8,256,128]{3,2,1,0:T(8,128)(2,1)S(1)}, bf16[2,8,256,128]{3,1,0,2:T(8,128)(2,1)S(1)}, bf16[2,1024,128]{1,2,0:T(8,128)(2,1)S(1...) while((s32[]{:T(128)}, ...), condition=%wide.region_6.7_spmd.clone, body=%wide.region_3.6_spmd.clone.sunk | while | flops 1098379264 | bytes 30986384 | solution.py:56
  109.4 2.1 %fusion.64 = f32[8,256]{1,0:T(8,128)S(1)} fusion(f32[8,256,1024]{2,1,0:T(8,128)S(1)} %get-tuple-element.377, f32[8,256]{1,0:T(8,128)S(1)} %get-tuple-element.378, pred[256,1024]{1,0:T(8,128)(4,1)S(1)} %and_and_fusion.4), kind=kLoop, calls=%fused_computation.5.clone.1 | loop fusion | flops 8386560 | bytes 8667136 | tf_op jit(solution)/shard_map/while/body/eval_jaxpr/reduce_sum | solution.py:49
  111.6 2.5 %fusion.65 = bf16[2,8,256,128]{3,2,1,0:T(8,128)(2,1)S(1)} fusion(bf16[2,8,256,128]{3,2,1,0:T(8,128)(2,1)S(1)} %get-tuple-element.436, s32[]{:T(128)} %get-tuple-element.435, f32[8,256,1024]{2,1,0:T(8,128)S(1)} %get-tuple-element.377, f32[8,256]{1,0:T(8,128)S(1)} %get-tuple-element.378, pred[256,1024]{1,0:T(8,128)(4,1)S(1)} %and_and_fusion.4, ...), kind=kOutput, calls=%fused_computation.12.clone.1 | convolution fusion | flops 545783808 | bytes 9454592 | tf_op jit(solution)/shard_map/while/body/eval_jaxpr/jqk,kd->jqd/dot_general | solution.py:51
  116.1 2.1 %fusion.64 = f32[8,256]{1,0:T(8,128)S(1)} fusion(f32[8,256,1024]{2,1,0:T(8,128)S(1)} %get-tuple-element.377, f32[8,256]{1,0:T(8,128)S(1)} %get-tuple-element.378, pred[256,1024]{1,0:T(8,128)(4,1)S(1)} %and_and_fusion.4), kind=kLoop, calls=%fused_computation.5.clone.1 | loop fusion | flops 8386560 | bytes 8667136 | tf_op jit(solution)/shard_map/while/body/eval_jaxpr/reduce_sum | solution.py:49
  118.2 2.5 %fusion.65 = bf16[2,8,256,128]{3,2,1,0:T(8,128)(2,1)S(1)} fusion(bf16[2,8,256,128]{3,2,1,0:T(8,128)(2,1)S(1)} %get-tuple-element.436, s32[]{:T(128)} %get-tuple-element.435, f32[8,256,1024]{2,1,0:T(8,128)S(1)} %get-tuple-element.377, f32[8,256]{1,0:T(8,128)S(1)} %get-tuple-element.378, pred[256,1024]{1,0:T(8,128)(4,1)S(1)} %and_and_fusion.4, ...), kind=kOutput, calls=%fused_computation.12.clone.1 | convolution fusion | flops 545783808 | bytes 9454592 | tf_op jit(solution)/shard_map/while/body/eval_jaxpr/jqk,kd->jqd/dot_general | solution.py:51
  124.3 13.2 %while.23 = (s32[]{:T(128)}, bf16[2,8,256,128]{3,2,1,0:T(8,128)(2,1)S(1)}, bf16[2,8,256,128]{3,1,0,2:T(8,128)(2,1)S(1)}, bf16[2,1024,128]{1,2,0:T(8,128)(2,1)S(1...) while((s32[]{:T(128)}, ...), condition=%wide.region_12.13_spmd.clone, body=%wide.region_9.12_spmd.clone.sunk | while | flops 1098379264 | bytes 30986384 | solution.py:56
  126.3 2.1 %fusion.69 = f32[8,256]{1,0:T(8,128)S(1)} fusion(f32[8,256,1024]{2,1,0:T(8,128)S(1)} %get-tuple-element.389, f32[8,256]{1,0:T(8,128)S(1)} %get-tuple-element.390, pred[256,1024]{1,0:T(8,128)(4,1)S(1)} %and_and_fusion.5), kind=kLoop, calls=%fused_computation.27.clone.1 | loop fusion | flops 8386560 | bytes 8667136 | tf_op jit(solution)/shard_map/while/body/eval_jaxpr/reduce_sum | solution.py:49
  128.5 2.5 %fusion.70 = bf16[2,8,256,128]{3,2,1,0:T(8,128)(2,1)S(1)} fusion(bf16[2,8,256,128]{3,2,1,0:T(8,128)(2,1)S(1)} %get-tuple-element.403, s32[]{:T(128)} %get-tuple-element.402, f32[8,256,1024]{2,1,0:T(8,128)S(1)} %get-tuple-element.389, f32[8,256]{1,0:T(8,128)S(1)} %get-tuple-element.390, pred[256,1024]{1,0:T(8,128)(4,1)S(1)} %and_and_fusion.5, ...), kind=kOutput, calls=%fused_computation.34.clone.1 | convolution fusion | flops 545783808 | bytes 9454592 | tf_op jit(solution)/shard_map/while/body/eval_jaxpr/jqk,kd->jqd/dot_general | solution.py:51
  133.0 2.1 %fusion.69 = f32[8,256]{1,0:T(8,128)S(1)} fusion(f32[8,256,1024]{2,1,0:T(8,128)S(1)} %get-tuple-element.389, f32[8,256]{1,0:T(8,128)S(1)} %get-tuple-element.390, pred[256,1024]{1,0:T(8,128)(4,1)S(1)} %and_and_fusion.5), kind=kLoop, calls=%fused_computation.27.clone.1 | loop fusion | flops 8386560 | bytes 8667136 | tf_op jit(solution)/shard_map/while/body/eval_jaxpr/reduce_sum | solution.py:49
  135.1 2.5 %fusion.70 = bf16[2,8,256,128]{3,2,1,0:T(8,128)(2,1)S(1)} fusion(bf16[2,8,256,128]{3,2,1,0:T(8,128)(2,1)S(1)} %get-tuple-element.403, s32[]{:T(128)} %get-tuple-element.402, f32[8,256,1024]{2,1,0:T(8,128)S(1)} %get-tuple-element.389, f32[8,256]{1,0:T(8,128)S(1)} %get-tuple-element.390, pred[256,1024]{1,0:T(8,128)(4,1)S(1)} %and_and_fusion.5, ...), kind=kOutput, calls=%fused_computation.34.clone.1 | convolution fusion | flops 545783808 | bytes 9454592 | tf_op jit(solution)/shard_map/while/body/eval_jaxpr/jqk,kd->jqd/dot_general | solution.py:51
  138.6 2.8 %pad_maximum_fusion = bf16[512,2048]{1,0:T(8,128)(2,1)} fusion(bf16[256,2048]{1,0:T(8,128)(2,1)S(1)} %bitcast.143, bf16[256,2048]{1,0:T(8,128)(2,1)} %bitcast.140), kind=kLoop, calls=%fused_computation.47 | loop fusion | flops 4194304 | bytes 4194304 | tf_op jit(solution)/shard_map/concatenate | solution.py:141
  (102 shorter events, 32.1 us)
Async XLA Ops:
  1.8 12.2 %all-to-all-start.1 = ((bf16[128,4,256]{0,2,1:T(8,128)(2,1)}), bf16[128,4,256]{0,2,1:T(8,128)(2,1)S(1)}, u32[]{:S(2)}, u32[]{:S(2)}) async-start(bf16[128,4,256]{0,2,1:T(8,128)(2,1)} %bitcast.2), calls=%async_computation.1 | async-start | bytes 524288 | tf_op jit(solution)/shard_map/all_to_all | solution.py:84
  8.4 57.3 %copy-start.2 = (s32[256]{0:T(256)}, s32[256]{0:T(256)S(1)}, u32[]{:S(2)}) copy-start(s32[256]{0:T(256)S(1)} %iota_add_fusion.3) | copy-start | bytes 3076
  8.5 57.3 %copy-start.4 = (s32[256]{0:T(256)}, s32[256]{0:T(256)S(1)}, u32[]{:S(2)}) copy-start(s32[256]{0:T(256)S(1)} %iota_add_fusion.7) | copy-start | bytes 3076
  14.0 9.8 %all-to-all-start.2 = ((bf16[128,4,256]{0,2,1:T(8,128)(2,1)}), bf16[128,4,256]{0,2,1:T(8,128)(2,1)S(1)}, u32[]{:S(2)}, u32[]{:S(2)}) async-start(bf16[128,4,256]{0,2,1:T(8,128)(2,1)} %bitcast.5), calls=%async_computation.2 | async-start | bytes 524288 | tf_op jit(solution)/shard_map/all_to_all | solution.py:85
  23.8 81.8 %all-to-all-start = ((bf16[128,4,2048]{2,0,1:T(8,128)(2,1)}), bf16[128,4,2048]{2,0,1:T(8,128)(2,1)S(1)}, u32[]{:S(2)}, u32[]{:S(2)}) async-start(bf16[128,4,2048]{2,0,1:T(8,128)(2,1)} %bitcast.114), calls=%async_computation | async-start | bytes 4194304 | tf_op jit(solution)/shard_map/all_to_all | solution.py:83
  27.6 21.6 %collective-permute-start = (bf16[2,2,256,256]{3,2,1,0:T(8,128)(2,1)S(1)}, bf16[2,2,256,256]{3,2,1,0:T(8,128)(2,1)}, u32[]{:S(2)}, u32[]{:S(2)}) collective-permute-start(bf16[2,2,256,256]{3,2,1,0:T(8,128)(2,1)S(1)} %pad_maximum_fusion.1), channel_id=1, source_target_pairs={{0,12},{4,16},{8,20},{12,24},{16,28},{20,32},{24,36},{28,40},{32,4... | collective-permute-start | bytes 1572872 | tf_op jit(solution)/shard_map/ppermute | solution.py:13
  37.1 21.7 %collective-permute-start.1 = (bf16[2,2,256,256]{3,2,1,0:T(8,128)(2,1)S(1)}, bf16[2,2,256,256]{3,2,1,0:T(8,128)(2,1)}, u32[]{:S(2)}, u32[]{:S(2)}) collective-permute-start(bf16[2,2,256,256]{3,2,1,0:T(8,128)(2,1)S(1)} %pad_maximum_fusion.1), channel_id=1, source_target_pairs={{0,8},{4,12},{8,16},{12,20},{16,24},{20,28},{24,32},{28,36},{32,40... | collective-permute-start | bytes 1572872 | tf_op jit(solution)/shard_map/ppermute | solution.py:13
  42.2 22.4 %collective-permute-start.2 = (bf16[2,2,256,256]{3,2,1,0:T(8,128)(2,1)S(1)}, bf16[2,2,256,256]{3,2,1,0:T(8,128)(2,1)}, u32[]{:S(2)}, u32[]{:S(2)}) collective-permute-start(bf16[2,2,256,256]{3,2,1,0:T(8,128)(2,1)S(1)} %pad_maximum_fusion.1), channel_id=1, source_target_pairs={{0,4},{4,8},{8,12},{12,16},{16,20},{20,24},{24,28},{28,32},{32,36}... | collective-permute-start | bytes 1572872 | tf_op jit(solution)/shard_map/ppermute | solution.py:13
  44.8 20.9 %collective-permute-start.3 = (bf16[2,2,256,256]{3,2,1,0:T(8,128)(2,1)S(1)}, bf16[2,2,256,256]{3,2,1,0:T(8,128)(2,1)S(1)}, u32[]{:S(2)}, u32[]{:S(2)}) collective-permute-start(bf16[2,2,256,256]{3,2,1,0:T(8,128)(2,1)S(1)} %pad_maximum_fusion.1), channel_id=1, source_target_pairs={{4,0},{8,4},{12,8},{16,12},{20,16},{24,20},{28,24},{32,28},{36,32}... | collective-permute-start | bytes 1572872 | tf_op jit(solution)/shard_map/ppermute | solution.py:13
  48.0 17.8 %collective-permute-start.4 = (bf16[2,2,256,256]{3,2,1,0:T(8,128)(2,1)S(1)}, bf16[2,2,256,256]{3,2,1,0:T(8,128)(2,1)S(1)}, u32[]{:S(2)}, u32[]{:S(2)}) collective-permute-start(bf16[2,2,256,256]{3,2,1,0:T(8,128)(2,1)S(1)} %pad_maximum_fusion.1), channel_id=1, source_target_pairs={{8,0},{12,4},{16,8},{20,12},{24,16},{28,20},{32,24},{36,28},{40,32... | collective-permute-start | bytes 1572872 | tf_op jit(solution)/shard_map/ppermute | solution.py:13
  49.3 36.3 %collective-permute-start.5 = (bf16[2,2,256,256]{3,2,1,0:T(8,128)(2,1)S(1)}, bf16[2,2,256,256]{3,2,1,0:T(8,128)(2,1)S(1)}, u32[]{:S(2)}, u32[]{:S(2)}) collective-permute-start(bf16[2,2,256,256]{3,2,1,0:T(8,128)(2,1)S(1)} %pad_maximum_fusion.1), channel_id=1, source_target_pairs={{12,0},{16,4},{20,8},{24,12},{28,16},{32,20},{36,24},{40,28},{44,3... | collective-permute-start | bytes 1572872 | tf_op jit(solution)/shard_map/ppermute | solution.py:13
  103.4 3.8 %copy-start.5 = (s32[256]{0:T(256)S(1)}, s32[256]{0:T(256)}, u32[]{:S(2)}) copy-start(s32[256]{0:T(256)} %copy-done.4) | copy-start | bytes 3076
  103.4 3.8 %copy-start.7 = (pred[1024]{0:T(1024)(128)(4,1)S(1)}, pred[1024]{0:T(1024)(128)(4,1)}, u32[]{:S(2)}) copy-start(pred[1024]{0:T(1024)(128)(4,1)} %pad_add_fusion.2) | copy-start | bytes 3076
  103.4 3.8 %copy-start.9 = (s32[256]{0:T(256)S(1)}, s32[256]{0:T(256)}, u32[]{:S(2)}) copy-start(s32[256]{0:T(256)} %get-tuple-element.429) | copy-start | bytes 3076
  107.2 17.1 %copy-start.3 = (s32[256]{0:T(256)S(1)}, s32[256]{0:T(256)}, u32[]{:S(2)}) copy-start(s32[256]{0:T(256)} %copy-done.2) | copy-start | bytes 3076
  107.2 17.1 %copy-start.6 = (pred[1024]{0:T(1024)(128)(4,1)S(1)}, pred[1024]{0:T(1024)(128)(4,1)}, u32[]{:S(2)}) copy-start(pred[1024]{0:T(1024)(128)(4,1)} %pad_add_fusion.3) | copy-start | bytes 3076
  107.2 17.1 %copy-start.8 = (s32[256]{0:T(256)S(1)}, s32[256]{0:T(256)}, u32[]{:S(2)}) copy-start(s32[256]{0:T(256)} %get-tuple-element.396) | copy-start | bytes 3076
  107.8 3.7 %copy-start.1 = (bf16[2,1024,128]{1,2,0:T(8,128)(2,1)S(1)}, bf16[2,1024,128]{1,2,0:T(8,128)(2,1)}, u32[]{:S(2)}) copy-start(bf16[2,1024,128]{1,2,0:T(8,128)(2,1)} %get-tuple-element.450) | copy-start | bytes 1572868 | tf_op jit(solution)/shard_map/while
  114.4 3.7 %copy-start.1 = (bf16[2,1024,128]{1,2,0:T(8,128)(2,1)S(1)}, bf16[2,1024,128]{1,2,0:T(8,128)(2,1)}, u32[]{:S(2)}) copy-start(bf16[2,1024,128]{1,2,0:T(8,128)(2,1)} %get-tuple-element.450) | copy-start | bytes 1572868 | tf_op jit(solution)/shard_map/while
  124.7 3.8 %copy-start = (bf16[2,1024,128]{1,2,0:T(8,128)(2,1)S(1)}, bf16[2,1024,128]{1,2,0:T(8,128)(2,1)}, u32[]{:S(2)}) copy-start(bf16[2,1024,128]{1,2,0:T(8,128)(2,1)} %get-tuple-element.417) | copy-start | bytes 1572868 | tf_op jit(solution)/shard_map/while
  131.3 3.8 %copy-start = (bf16[2,1024,128]{1,2,0:T(8,128)(2,1)S(1)}, bf16[2,1024,128]{1,2,0:T(8,128)(2,1)}, u32[]{:S(2)}) copy-start(bf16[2,1024,128]{1,2,0:T(8,128)(2,1)} %get-tuple-element.417) | copy-start | bytes 1572868 | tf_op jit(solution)/shard_map/while
where the time goes:
time: 142 us; the launch traced here: 141 us
  waiting for transfers between devices  37 us (26%)
  starting transfers between devices  33.6 us (24%)
  local copies, waits for them, and re-layouts  32.5 us (23%)
  other arithmetic  21.2 us (15%)
  matrix products  16.4 us (12%)
    ppermute x6, waiting for transfers between devices, shifted(): return lax.ppermute(block, axis, route)  31.6 us
    ppermute x6, starting transfers between devices, shifted(): return lax.ppermute(block, axis, route)  20.9 us
    unnamed x27, local copies, waits for them, and re-layouts  10.1 us
    dot_general x4, matrix products, one_group(): jnp.einsum('jqk,kd->jqd', weights, value_group, preferred_element_type=jn...  9.9 us
    reduce_sum x4, other arithmetic, one_group(): denominator = jnp.sum(raised, axis=-1, keepdims=True)  8.46 us
    slice x8, local copies, waits for them, and re-layouts, body(): key_blocks.append(picked[0])  8.32 us
    slice x9, local copies, waits for them, and re-layouts, body(): value_blocks.append(picked[1])  7.27 us
    dot_general x4, matrix products, one_group(): jnp.einsum('jqd,kd->jqk', query_group, key_group, preferred_element_type=...  6.46 us
  transfers between devices with their start and end apart: 9, of which 4 were waited for; matrix products, arithmetic and copies ran while one was open for 23% of the time, Pallas kernels for 0%

commit v1 on v0

v1 whole, which is shorter than its diff:
```python
import functools
import jax
import jax.numpy as jnp
from jax import lax
from jax.experimental import pallas as pl
from jax.experimental.pallas import tpu as pltpu
from jax.sharding import PartitionSpec as P

HEAD_DIM = 128
REACH = 3
STRETCH = 256
LANES = 2
ROWS = 128
KEYS = REACH * STRETCH + ROWS
WINDOW = (REACH + 1) * STRETCH
SCALE = HEAD_DIM ** (-0.5)
LOG2E = 1.4426950408889634
GROUP = 8


def kv_pack_kernel(key_ref, value_ref, out_ref):
    width = key_ref.shape[1] // 4
    for dest in range(4):
        out_ref[dest, :, :width] = key_ref[:, dest * width : (dest + 1) * width]
        out_ref[dest, :, width:] = value_ref[:, dest * width : (dest + 1) * width]


def kv_pack(key_rows, value_rows):
    rows, width = key_rows.shape
    return pl.pallas_call(
        kv_pack_kernel,
        out_shape=jax.ShapeDtypeStruct((4, rows, width // 2), key_rows.dtype),
        name="kv_pack",
    )(key_rows, value_rows)


def query_pack_kernel(query_ref, *out_refs):
    at = 0
    for out_ref in out_refs:
        width = out_ref.shape[2]
        out_ref[0] = query_ref[:, at : at + width]
        at += width


def query_pack(queries, widths):
    rows, width = queries.shape
    return pl.pallas_call(
        query_pack_kernel,
        grid=(4,),
        in_specs=[pl.BlockSpec((rows, width // 4), lambda d: (0, d))],
        out_specs=[pl.BlockSpec((1, rows, w), lambda d: (d, 0, 0)) for w in widths],
        out_shape=[jax.ShapeDtypeStruct((4, rows, w), queries.dtype) for w in widths],
        name="query_pack",
    )(queries)


def load_windows(kv_head, kv_local, ctx, count, own, up, down, far, mate, keys, values, sems):
    odd = lax.rem(ctx, 2) == 1
    last = ctx == count - 1
    before_last = ctx == count - 2
    key_col = pl.ds(kv_head * HEAD_DIM, HEAD_DIM)
    value_col = pl.ds((kv_local + kv_head) * HEAD_DIM, HEAD_DIM)

    def pair(source, row, lane, slot):
        rows = pl.ds(row, STRETCH)
        place = pl.ds(slot * STRETCH, STRETCH)
        sem = sems.at[lane, slot]
        return (
            pltpu.make_async_copy(source.at[rows, key_col], keys.at[lane, place, :], sem),
            pltpu.make_async_copy(
                source.at[rows, value_col], values.at[lane, place, pl.ds(0, HEAD_DIM)], sem
            ),
        )

    def start(condition, source, row, lane, slot):
        @pl.when(condition)
        def _():
            for copy in pair(source, row, lane, slot):
                copy.start()

    for lane in range(LANES):
        for copy in pair(own, lane * STRETCH, lane, 3):
            copy.start()
    for copy in pair(up, 0, 0, 1):
        copy.start()
    even = jnp.logical_not(odd)
    plain = ctx < count - 2
    start(odd, mate, STRETCH, 0, 0)
    start(even, far, 0, 0, 0)
    start(odd, mate, 0, 0, 2)
    start(even, mate, STRETCH, 0, 2)
    start(jnp.logical_and(even, plain), mate, 2 * STRETCH, 1, 0)
    start(jnp.logical_and(odd, plain), far, 0, 1, 0)
    start(before_last, own, 0, 1, 0)
    start(last, up, 0, 1, 0)
    start(plain, down, 0, 1, 1)
    start(before_last, mate, 2 * STRETCH, 1, 1)
    start(last, mate, 0, 1, 1)
    start(even, mate, 0, 1, 2)
    start(jnp.logical_and(odd, plain), mate, 2 * STRETCH, 1, 2)
    start(last, own, 0, 1, 2)

    def wait(lane):
        for slot in range(REACH + 1):
            for copy in pair(own, 0, lane, slot):
                copy.wait()

    return wait


def attention_kernel(
    kv_head, kv_local, count,
    ctx_ref, starts_ref, query_ref, own, up, down, far, mate, *rest,
):
    out_ref, keys, values, sems = rest[-4:]
    step = pl.program_id(0)
    ctx = ctx_ref[0]
    lane = step // 2
    half = lax.rem(step, 2)

    @pl.when(step == 0)
    def _():
        wait = load_windows(
            kv_head, kv_local, ctx, count, own, up, down, far, mate, keys, values, sems
        )
        values[:, :, HEAD_DIM:] = jnp.ones((LANES, WINDOW, HEAD_DIM), values.dtype)
        wait(0)
        wait(1)

    stretch = jnp.where(lane == 0, ctx, 2 * count - 1 - ctx)
    first = stretch * STRETCH + half * ROWS
    row_pos = first + lax.broadcasted_iota(jnp.int32, (ROWS, 1), 0)
    starts = starts_ref[...]
    row_start = jnp.max(jnp.where(starts <= row_pos, starts, 0), axis=1, keepdims=True)
    key_pos = first - REACH * STRETCH + lax.broadcasted_iota(jnp.int32, (ROWS, KEYS), 1)
    allowed = (key_pos >= row_start) & (key_pos <= row_pos)
    bias = jnp.where(allowed, 0.0, -jnp.inf).astype(jnp.float32)
    window = pl.ds(pl.multiple_of(half * ROWS, ROWS), KEYS)
    key = keys[lane, window, :]
    value = values[lane, window, :]
    heads = query_ref.shape[1] // HEAD_DIM
    for head in range(heads):
        cols = slice(head * HEAD_DIM, (head + 1) * HEAD_DIM)
        scores = lax.dot_general(
            query_ref[:, cols], key, (((1,), (1,)), ((), ())), preferred_element_type=jnp.float32
        )
        scores = scores + bias
        top = jnp.max(scores, axis=1, keepdims=True)
        raised = jnp.exp2((scores - top) * (SCALE * LOG2E)).astype(jnp.bfloat16)
        mixed = jnp.dot(raised, value, preferred_element_type=jnp.float32)
        out_ref[:, cols] = (mixed[:, :HEAD_DIM] / mixed[:, HEAD_DIM:]).astype(out_ref.dtype)


def attention(kv_head, kv_local, count, ctx, starts, query, own, up, down, far, mate, partial):
    rows, width = query.shape
    blocks = rows // ROWS
    any_spec = pl.BlockSpec(memory_space=pl.ANY)
    operands = [ctx, starts, query, own, up, down, far, mate]
    in_specs = [
        pl.BlockSpec(memory_space=pltpu.SMEM),
        pl.BlockSpec(starts.shape, lambda i: (0, 0)),
        pl.BlockSpec((ROWS, width), lambda i: (i, 0)),
        any_spec, any_spec, any_spec, any_spec, any_spec,
    ]
    aliases = {}
    if partial is not None:
        aliases = {len(operands): 0}
        operands.append(partial)
        in_specs.append(any_spec)
    return pl.pallas_call(
        functools.partial(attention_kernel, kv_head, kv_local, count),
        grid=(blocks,),
        in_specs=in_specs,
        out_specs=pl.BlockSpec((ROWS, width), lambda i: (i, kv_head)),
        out_shape=jax.ShapeDtypeStruct((rows, kv_local * width), query.dtype),
        scratch_shapes=[
            pltpu.VMEM((LANES, WINDOW, HEAD_DIM), jnp.bfloat16),
            pltpu.VMEM((LANES, WINDOW, 2 * HEAD_DIM), jnp.bfloat16),
            pltpu.SemaphoreType.DMA((LANES, REACH + 1)),
        ],
        input_output_aliases=aliases,
        name="attention",
    )(*operands)


def body(queries, key_rows, value_rows, doc_lengths):
    count = lax.axis_size("ctx")
    ctx = lax.axis_index("ctx")
    odd = lax.rem(ctx, 2) == 1

    def swap(block):
        return lax.all_to_all(block, "head", split_axis=0, concat_axis=0, tiled=True)

    kv = swap(kv_pack(key_rows, value_rows)).reshape(LANES * STRETCH, -1)
    kv_local = kv.shape[1] // (2 * HEAD_DIM)
    width = queries.shape[1] // (4 * kv_local)
    packed = query_pack(queries, [width] * kv_local)
    query = [swap(part).reshape(LANES * STRETCH, width) for part in packed]

    lane0, lane1 = kv[:STRETCH], kv[STRETCH:]
    up = lax.ppermute(lane0, "ctx", [(i, i + 2) for i in range(count - 2)])
    down = lax.ppermute(lane1, "ctx", [(i + 2, i) for i in range(count - 2)])
    route = [(i, i + 3) for i in range(1, count - 3, 2)]
    route += [(i + 3, i) for i in range(1, count - 3, 2)]
    route += [(count - 1, count - 3)]
    far = lax.ppermute(jnp.where(odd, lane0, lane1), "ctx", route)
    passed = jnp.concatenate(
        [jnp.where(odd, lane1, lane0), up, jnp.where(ctx == count - 1, lane0, down)], axis=0
    )
    mate = lax.ppermute(passed, "ctx", [(i, i ^ 1) for i in range(count)])

    sizes = doc_lengths * 2
    starts = (jnp.cumsum(sizes) - sizes).reshape(1, -1)
    where = ctx.reshape(1)
    out = None
    for kv_head in range(kv_local):
        out = attention(
            kv_head, kv_local, count, where, starts, query[kv_head],
            kv, up, down, far, mate, out,
        )
    return out


def solution(mesh):
    placed = (P(("ctx", "head"), None), P(("ctx", "head"), None), P(("ctx", "head"), None), P())
    return jax.shard_map(
        body, mesh=mesh, in_specs=placed, out_specs=P("ctx", "head"), check_vma=False
    )
```

time: 142 us -> 85.2 us (0.60)
  the two profiles are of different devices: /device:TPU:1 before, /device:TPU:34 now
where the time goes in v1:
time: 85.2 us; the launch traced here: 84.5 us
  starting transfers between devices  31.2 us (37%)
  Pallas kernels  26.2 us (31%)
  waiting for transfers between devices  22.3 us (26%)
  other arithmetic  2.66 us (3%)
  local copies, waits for them, and re-layouts  2.1 us (2%)
    pallas_call x2, Pallas kernels, attention(): pl.pallas_call(functools.partial(attention_kernel, kv_head, kv_local, cou...  20.6 us
    all_to_all x3, starting transfers between devices, swap(): lax.all_to_all(block, 'head', split_axis=0, concat_axis=0, tiled=True)  14.6 us
    ppermute x1, starting transfers between devices, body(): down = lax.ppermute(lane1, 'ctx', [(i + 2, i) for i in range(count - 2)])  10.8 us
    ppermute x1, waiting for transfers between devices, body(): far = lax.ppermute(jnp.where(odd, lane0, lane1), 'ctx', route)  9.17 us
    ppermute x1, waiting for transfers between devices, body(): up = lax.ppermute(lane0, 'ctx', [(i, i + 2) for i in range(count - 2)])  6.92 us
    all_to_all x3, waiting for transfers between devices, swap(): lax.all_to_all(block, 'head', split_axis=0, concat_axis=0, tiled=True)  4.24 us
    pallas_call x1, Pallas kernels, query_pack(): pl.pallas_call(query_pack_kernel, grid=(4,), in_specs=[pl.BlockSpec((rows...  3.78 us
    unnamed x16, local copies, waits for them, and re-layouts  1.96 us
  transfers between devices with their start and end apart: 7, of which 4 were waited for; matrix products, arithmetic and copies ran while one was open for 3% of the time, Pallas kernels for 17%

profile of v1, /device:TPU:34, one launch (start us, length us, event | category | flops | bytes accessed | tf_op | source)
XLA Modules:
  0.0 84.5 jit_solution(1591450101210142220)
XLA Ops:
  0.0 1.9 %kv_pack.1 = bf16[4,128,512]{2,1,0:T(8,128)(2,1)} custom-call(bf16[128,1024]{1,0:T(8,128)(2,1)} %key_ref.1, bf16[128,1024]{1,0:T(8,128)(2,1)} %value_ref.1), custom_call_target="tpu_custom_call" | custom-call | tf_op jit(solution)/shard_map/kv_pack/pallas_call | solution.py:30
  1.9 4.8 %all-to-all-start.1 = ((bf16[4,128,512]{2,1,0:T(8,128)(2,1)}), bf16[4,128,512]{2,1,0:T(8,128)(2,1)S(1)}, u32[]{:S(2)}, u32[]{:S(2)}) async-start(bf16[4,128,512]{2,1,0:T(8,128)(2,1)} %kv_pack.1), calls=%async_computation.1 | async-start | bytes 1048576 | tf_op jit(solution)/shard_map/all_to_all | solution.py:192
  6.7 3.8 %query_pack.1 = (bf16[4,128,1024]{2,1,0:T(8,128)(2,1)}, bf16[4,128,1024]{2,1,0:T(8,128)(2,1)}) custom-call(bf16[128,8192]{1,0:T(8,128)(2,1)} %query_ref.1), custom_call_target="tpu_custom_call" | custom-call | tf_op jit(solution)/shard_map/query_pack/pallas_call | solution.py:47
  10.5 4.2 %all-to-all-done.1 = bf16[4,128,512]{2,1,0:T(8,128)(2,1)S(1)} async-done(((bf16[4,128,512]{2,1,0:T(8,128)(2,1)}), bf16[4,128,512]{2,1,0:T(8,128)(2,1)S(1)}, u32[]{:S(2)}, u32[]{:S(2)}) %all-to-all-start.1) | async-done | bytes 524320 | tf_op jit(solution)/shard_map/all_to_all | solution.py:192
  14.7 4.9 %all-to-all-start.2 = ((bf16[4,128,1024]{2,1,0:T(8,128)(2,1)}), bf16[4,128,1024]{2,1,0:T(8,128)(2,1)S(1)}, u32[]{:S(2)}, u32[]{:S(2)}) async-start(bf16[4,128,1024]{2,1,0:T(8,128)(2,1)} %get-tuple-element.8), calls=%async_computation.2 | async-start | bytes 2097152 | tf_op jit(solution)/shard_map/all_to_all | solution.py:192
  19.7 0.0 copy-done
  19.7 10.8 %collective-permute-start.1 = (bf16[256,512]{1,0:T(8,128)(2,1)S(1)}, bf16[256,512]{1,0:T(8,128)(2,1)S(1)}, u32[]{:S(2)}, u32[]{:S(2)}) collective-permute-start(bf16[256,512]{1,0:T(8,128)(2,1)S(1)} %bitcast.20), channel_id=1, source_target_pairs={{8,0},{12,4},{16,8},{20,12},{24,16},{28,20},{32,24},{36,28},{40,32... | collective-permute-start | bytes 786440 | tf_op jit(solution)/shard_map/ppermute | solution.py:202
  30.6 1.9 %collective-permute-start = (bf16[256,512]{1,0:T(8,128)(2,1)S(1)}, bf16[256,512]{1,0:T(8,128)(2,1)S(1)}, u32[]{:S(2)}, u32[]{:S(2)}) collective-permute-start(bf16[256,512]{1,0:T(8,128)(2,1)S(1)} %bitcast.19), channel_id=1, source_target_pairs={{0,8},{4,12},{8,16},{12,20},{16,24},{20,28},{24,32},{28,36},{32,40... | collective-permute-start | bytes 786440 | tf_op jit(solution)/shard_map/ppermute | solution.py:201
  32.5 1.9 %collective-permute-done.1.down = bf16[256,512]{1,0:T(8,128)(2,1)S(1)} collective-permute-done((bf16[256,512]{1,0:T(8,128)(2,1)S(1)}, bf16[256,512]{1,0:T(8,128)(2,1)S(1)}, u32[]{:S(2)}, u32[]{:S(2)}) %collective-permute-start.1) | collective-permute-done | bytes 262176 | tf_op jit(solution)/shard_map/ppermute | solution.py:202
  34.4 0.8 broadcast_select_fusion.1
  35.2 6.9 %collective-permute-done.up = bf16[256,512]{1,0:T(8,128)(2,1)S(1)} collective-permute-done((bf16[256,512]{1,0:T(8,128)(2,1)S(1)}, bf16[256,512]{1,0:T(8,128)(2,1)S(1)}, u32[]{:S(2)}, u32[]{:S(2)}) %collective-permute-start) | collective-permute-done | bytes 262176 | tf_op jit(solution)/shard_map/ppermute | solution.py:201
  42.2 1.0 %pad_maximum_fusion = bf16[768,512]{1,0:T(8,128)(2,1)} fusion(bf16[256,512]{1,0:T(8,128)(2,1)S(1)} %get-tuple-element.13, bf16[256,512]{1,0:T(8,128)(2,1)S(1)} %collective-permute-done.up, bf16[256,512]{1,0:T(8,128)(2,1)S(1)} %get-tuple-element.9), kind=kLoop, calls=%fused_computation | loop fusion | flops 2359296 | bytes 1572864 | tf_op jit(solution)/shard_map/concatenate | solution.py:207
  43.1 0.0 copy-done.4
  43.1 1.9 %collective-permute-start.3 = (bf16[768,512]{1,0:T(8,128)(2,1)}, bf16[768,512]{1,0:T(8,128)(2,1)S(1)}, u32[]{:S(2)}, u32[]{:S(2)}) collective-permute-start(bf16[768,512]{1,0:T(8,128)(2,1)} %pad_maximum_fusion), channel_id=1, source_target_pairs={{0,4},{4,0},{8,12},{12,8},{16,20},{20,16},{24,28},{28,24},{32,36},... | collective-permute-start | bytes 2359304 | tf_op jit(solution)/shard_map/ppermute | solution.py:210
  45.1 0.0 all-to-all-done.2
  45.1 0.0 copy-start.1
  45.1 0.0 copy-done.5
  45.1 4.8 %all-to-all-start = ((bf16[4,128,1024]{2,1,0:T(8,128)(2,1)}), bf16[4,128,1024]{2,1,0:T(8,128)(2,1)S(1)}, u32[]{:S(2)}, u32[]{:S(2)}) async-start(bf16[4,128,1024]{2,1,0:T(8,128)(2,1)} %get-tuple-element.7), calls=%async_computation | async-start | bytes 2097152 | tf_op jit(solution)/shard_map/all_to_all | solution.py:192
  49.9 1.9 %collective-permute-start.2 = (bf16[256,512]{1,0:T(8,128)(2,1)}, bf16[256,512]{1,0:T(8,128)(2,1)S(1)}, u32[]{:S(2)}, u32[]{:S(2)}) collective-permute-start(bf16[256,512]{1,0:T(8,128)(2,1)} %get-tuple-element.10), channel_id=1, source_target_pairs={{4,16},{12,24},{20,32},{28,40},{36,48},{44,56},{52,64},{60,72},{68... | collective-permute-start | bytes 786440 | tf_op jit(solution)/shard_map/ppermute | solution.py:206
  51.8 0.0 copy-done.7
  51.8 0.1 copy.7
  52.0 0.2 reduce-window.9
  52.1 0.1 reduce
  52.2 0.6 subtract_bitcast_fusion.starts_ref
  52.8 9.2 %collective-permute-done.2.far = bf16[256,512]{1,0:T(8,128)(2,1)S(1)} collective-permute-done((bf16[256,512]{1,0:T(8,128)(2,1)}, bf16[256,512]{1,0:T(8,128)(2,1)S(1)}, u32[]{:S(2)}, u32[]{:S(2)}) %collective-permute-start.2) | collective-permute-done | bytes 262176 | tf_op jit(solution)/shard_map/ppermute | solution.py:206
  62.0 0.0 collective-permute-done.3.mate
  62.0 0.7 copy-done.6
  62.7 0.3 copy-done.3
  63.0 10.3 %attention.2.rest_0_ = bf16[512,2048]{1,0:T(8,128)(2,1)} custom-call(s32[1]{0:T(128)} %bitcast.ctx_ref, s32[1,128]{1,0:T(1,128)} %subtract_bitcast_fusion.starts_ref, bf16[512,1024]{1,0:T(8,128)(2,1)} %bitcast.17, bf16[512,512]{1,0:T(8,128)(2,1)} %bitcast.15, bf16[256,512]{1,0:T(8,128)(2,1)} %copy-done.5, bf16[256,512]{1,0:T(8,128)(2,1)} %copy-done.4, ...), custom_call_target="tpu_custom_call" | custom-call | tf_op jit(solution)/shard_map/attention/pallas_call | solution.py:170
  73.3 0.0 all-to-all-done
  73.3 1.0 %copy-done.2 = bf16[4,128,1024]{2,1,0:T(8,128)(2,1)} copy-done((bf16[4,128,1024]{2,1,0:T(8,128)(2,1)}, bf16[4,128,1024]{2,1,0:T(8,128)(2,1)S(1)}, u32[]{:S(2)}) %copy-start.2) | copy-done | bytes 1048600
  74.3 10.3 %attention.3 = bf16[512,2048]{1,0:T(8,128)(2,1)} custom-call(s32[1]{0:T(128)} %bitcast.ctx_ref, s32[1,128]{1,0:T(1,128)} %subtract_bitcast_fusion.starts_ref, bf16[512,1024]{1,0:T(8,128)(2,1)} %bitcast.18, bf16[512,512]{1,0:T(8,128)(2,1)} %bitcast.16, bf16[256,512]{1,0:T(8,128)(2,1)} %copy-done.5, ...), custom_call_target="tpu_custom_call", output_to_operand_aliasing={{}: (8, {})} | custom-call | tf_op jit(solution)/shard_map/attention/pallas_call | solution.py:170
  (10 shorter events, 0.1 us)
Async XLA Ops:
  1.9 12.8 %all-to-all-start.1 = ((bf16[4,128,512]{2,1,0:T(8,128)(2,1)}), bf16[4,128,512]{2,1,0:T(8,128)(2,1)S(1)}, u32[]{:S(2)}, u32[]{:S(2)}) async-start(bf16[4,128,512]{2,1,0:T(8,128)(2,1)} %kv_pack.1), calls=%async_computation.1 | async-start | bytes 1048576 | tf_op jit(solution)/shard_map/all_to_all | solution.py:192
  14.7 5.0 %copy-start = (bf16[4,128,512]{2,1,0:T(8,128)(2,1)}, bf16[4,128,512]{2,1,0:T(8,128)(2,1)S(1)}, u32[]{:S(2)}) copy-start(bf16[4,128,512]{2,1,0:T(8,128)(2,1)S(1)} %all-to-all-done.1) | copy-start | bytes 1572868
  14.7 30.3 %all-to-all-start.2 = ((bf16[4,128,1024]{2,1,0:T(8,128)(2,1)}), bf16[4,128,1024]{2,1,0:T(8,128)(2,1)S(1)}, u32[]{:S(2)}, u32[]{:S(2)}) async-start(bf16[4,128,1024]{2,1,0:T(8,128)(2,1)} %get-tuple-element.8), calls=%async_computation.2 | async-start | bytes 2097152 | tf_op jit(solution)/shard_map/all_to_all | solution.py:192
  19.7 14.7 %collective-permute-start.1 = (bf16[256,512]{1,0:T(8,128)(2,1)S(1)}, bf16[256,512]{1,0:T(8,128)(2,1)S(1)}, u32[]{:S(2)}, u32[]{:S(2)}) collective-permute-start(bf16[256,512]{1,0:T(8,128)(2,1)S(1)} %bitcast.20), channel_id=1, source_target_pairs={{8,0},{12,4},{16,8},{20,12},{24,16},{28,20},{32,24},{36,28},{40,32... | collective-permute-start | bytes 786440 | tf_op jit(solution)/shard_map/ppermute | solution.py:202
  30.6 11.6 %collective-permute-start = (bf16[256,512]{1,0:T(8,128)(2,1)S(1)}, bf16[256,512]{1,0:T(8,128)(2,1)S(1)}, u32[]{:S(2)}, u32[]{:S(2)}) collective-permute-start(bf16[256,512]{1,0:T(8,128)(2,1)S(1)} %bitcast.19), channel_id=1, source_target_pairs={{0,8},{4,12},{8,16},{12,20},{16,24},{20,28},{24,32},{28,36},{32,40... | collective-permute-start | bytes 786440 | tf_op jit(solution)/shard_map/ppermute | solution.py:201
  34.4 8.7 %copy-start.4 = (bf16[256,512]{1,0:T(8,128)(2,1)}, bf16[256,512]{1,0:T(8,128)(2,1)S(1)}, u32[]{:S(2)}) copy-start(bf16[256,512]{1,0:T(8,128)(2,1)S(1)} %collective-permute-done.1.down) | copy-start | bytes 786436
  42.2 2.9 %copy-start.5 = (bf16[256,512]{1,0:T(8,128)(2,1)}, bf16[256,512]{1,0:T(8,128)(2,1)S(1)}, u32[]{:S(2)}) copy-start(bf16[256,512]{1,0:T(8,128)(2,1)S(1)} %collective-permute-done.up) | copy-start | bytes 786436
  42.2 9.7 %copy-start.7 = (s32[128]{0:T(128)S(1)}, s32[128]{0:T(128)}, u32[]{:S(2)}) copy-start(s32[128]{0:T(128)} %param.7) | copy-start | bytes 1540
  43.1 18.9 %collective-permute-start.3 = (bf16[768,512]{1,0:T(8,128)(2,1)}, bf16[768,512]{1,0:T(8,128)(2,1)S(1)}, u32[]{:S(2)}, u32[]{:S(2)}) collective-permute-start(bf16[768,512]{1,0:T(8,128)(2,1)} %pad_maximum_fusion), channel_id=1, source_target_pairs={{0,4},{4,0},{8,12},{12,8},{16,20},{20,16},{24,28},{28,24},{32,36},... | collective-permute-start | bytes 2359304 | tf_op jit(solution)/shard_map/ppermute | solution.py:210
  45.1 16.9 %copy-start.1 = (bf16[4,128,1024]{2,1,0:T(8,128)(2,1)}, bf16[4,128,1024]{2,1,0:T(8,128)(2,1)S(1)}, u32[]{:S(2)}) copy-start(bf16[4,128,1024]{2,1,0:T(8,128)(2,1)S(1)} %all-to-all-done.2) | copy-start | bytes 3145732
  45.1 28.2 %all-to-all-start = ((bf16[4,128,1024]{2,1,0:T(8,128)(2,1)}), bf16[4,128,1024]{2,1,0:T(8,128)(2,1)S(1)}, u32[]{:S(2)}, u32[]{:S(2)}) async-start(bf16[4,128,1024]{2,1,0:T(8,128)(2,1)} %get-tuple-element.7), calls=%async_computation | async-start | bytes 2097152 | tf_op jit(solution)/shard_map/all_to_all | solution.py:192
  49.9 12.1 %collective-permute-start.2 = (bf16[256,512]{1,0:T(8,128)(2,1)}, bf16[256,512]{1,0:T(8,128)(2,1)S(1)}, u32[]{:S(2)}, u32[]{:S(2)}) collective-permute-start(bf16[256,512]{1,0:T(8,128)(2,1)} %get-tuple-element.10), channel_id=1, source_target_pairs={{4,16},{12,24},{20,32},{28,40},{36,48},{44,56},{52,64},{60,72},{68... | collective-permute-start | bytes 786440 | tf_op jit(solution)/shard_map/ppermute | solution.py:206
  62.0 0.7 copy-start.6
  62.0 1.0 %copy-start.3 = (bf16[768,512]{1,0:T(8,128)(2,1)}, bf16[768,512]{1,0:T(8,128)(2,1)S(1)}, u32[]{:S(2)}) copy-start(bf16[768,512]{1,0:T(8,128)(2,1)S(1)} %collective-permute-done.3.mate) | copy-start | bytes 2359300
  73.3 1.0 %copy-start.2 = (bf16[4,128,1024]{2,1,0:T(8,128)(2,1)}, bf16[4,128,1024]{2,1,0:T(8,128)(2,1)S(1)}, u32[]{:S(2)}) copy-start(bf16[4,128,1024]{2,1,0:T(8,128)(2,1)S(1)} %all-to-all-done) | copy-start | bytes 3145732

commit v2 on v1

v2 whole, which is shorter than its diff:
```python
import functools
import jax
import jax.numpy as jnp
from jax import lax
from jax.experimental import pallas as pl
from jax.experimental.pallas import tpu as pltpu
from jax.sharding import PartitionSpec as P

HEAD_DIM = 128
REACH = 3
STRETCH = 256
LANES = 2
HEADS = 4
ROWS = 128
KEYS = REACH * STRETCH + ROWS
WINDOW = (REACH + 1) * STRETCH
GROUP = 8
PADDED = HEAD_DIM + 16
EXPONENT_SCALE = HEAD_DIM ** (-0.5) * 1.4426950408889634
SMALL, LARGE = 2.0**-60, 2.0**110
VMEM_LIMIT = 24 << 20
VMEM_SPEC = pl.BlockSpec(memory_space=pltpu.VMEM)
ANY_SPEC = pl.BlockSpec(memory_space=pl.ANY)
SMEM_SPEC = pl.BlockSpec(memory_space=pltpu.SMEM)
PARAMS = pltpu.CompilerParams(vmem_limit_bytes=VMEM_LIMIT)


def kv_pack_kernel(key_ref, value_ref, out_ref):
    width = key_ref.shape[1] // HEADS
    for dest in range(HEADS):
        out_ref[dest, :, :width] = key_ref[:, dest * width : (dest + 1) * width]
        out_ref[dest, :, width:] = value_ref[:, dest * width : (dest + 1) * width]


def kv_pack(key_rows, value_rows):
    rows, width = key_rows.shape
    return pl.pallas_call(
        kv_pack_kernel,
        in_specs=[VMEM_SPEC, VMEM_SPEC],
        out_specs=VMEM_SPEC,
        out_shape=jax.ShapeDtypeStruct((HEADS, rows, 2 * width // HEADS), key_rows.dtype),
        compiler_params=PARAMS,
        name="kv_pack",
    )(key_rows, value_rows)


def query_pack_kernel(place_ref, query_ref, *refs):
    out_refs, sems = refs[:-1], refs[-1]
    width = query_ref.shape[1] // HEADS
    copies = []
    for at, (shift, out_ref) in enumerate(zip((1, 3, 2), out_refs)):
        col = pl.multiple_of(lax.rem(place_ref[1] + shift, HEADS) * width, width)
        copies.append(
            pltpu.make_async_copy(query_ref.at[:, pl.ds(col, width)], out_ref, sems.at[at])
        )
    for copy in copies:
        copy.start()
    for copy in copies:
        copy.wait()


def query_pack(place, queries):
    rows, width = queries.shape
    block = jax.ShapeDtypeStruct((rows, width // HEADS), queries.dtype)
    return pl.pallas_call(
        query_pack_kernel,
        in_specs=[SMEM_SPEC, ANY_SPEC],
        out_specs=[ANY_SPEC] * 3,
        out_shape=[block] * 3,
        scratch_shapes=[pltpu.SemaphoreType.DMA((3,))],
        compiler_params=PARAMS,
        name="query_pack",
    )(place, queries)


def load_windows(ctx, count, own, up, down, far, mate, keys, values, sems):
    odd = lax.rem(ctx, 2) == 1
    even = jnp.logical_not(odd)
    last = ctx == count - 1
    before_last = ctx == count - 2
    plain = ctx < count - 2
    width = keys.shape[2]

    def piece(kind, source, row, lane, slot):
        return pltpu.make_async_copy(
            source.at[pl.ds(row, STRETCH), pl.ds((1 - kind) * width, width)],
            (values, keys)[kind].at[lane, pl.ds(slot * STRETCH, STRETCH), :],
            sems.at[kind, lane, slot],
        )

    def start(condition, source, row, lane, slot):
        @pl.when(condition)
        def _():
            for kind in range(2):
                piece(kind, source, row, lane, slot).start()

    for lane in range(LANES):
        for kind in range(2):
            piece(kind, own, lane * STRETCH, lane, 3).start()
    for kind in range(2):
        piece(kind, up, 0, 0, 1).start()
    start(odd, mate, STRETCH, 0, 0)
    start(even, far, 0, 0, 0)
    start(odd, mate, 0, 0, 2)
    start(even, mate, STRETCH, 0, 2)
    start(jnp.logical_and(even, plain), mate, 2 * STRETCH, 1, 0)
    start(jnp.logical_and(odd, plain), far, 0, 1, 0)
    start(before_last, own, 0, 1, 0)
    start(last, up, 0, 1, 0)
    start(plain, down, 0, 1, 1)
    start(before_last, mate, 2 * STRETCH, 1, 1)
    start(last, mate, 0, 1, 1)
    start(even, mate, 0, 1, 2)
    start(jnp.logical_and(odd, plain), mate, 2 * STRETCH, 1, 2)
    start(last, own, 0, 1, 2)

    def wait(kind, lane):
        for slot in range(REACH + 1):
            piece(kind, own, 0, lane, slot).wait()

    return wait


def attend(block, ctx, count, lengths, query, keys, values_t, bias, out):
    lane = block // 2
    half = lax.rem(block, 2)
    stretch = jnp.where(lane == 0, ctx, 2 * count - 1 - ctx)
    first = stretch * STRETCH + half * ROWS
    docs = lengths.shape[1]
    earlier = lax.broadcasted_iota(jnp.int32, (docs, docs), 1) < lax.broadcasted_iota(
        jnp.int32, (docs, docs), 0
    )
    starts = 2 * jnp.sum(jnp.where(earlier, lengths, 0), axis=1, keepdims=True)
    row_pos = first + lax.broadcasted_iota(jnp.int32, (1, ROWS), 1)
    row_start = jnp.max(jnp.where(starts <= row_pos, starts, 0), axis=0, keepdims=True)
    key_pos = first - REACH * STRETCH + lax.broadcasted_iota(jnp.int32, (KEYS, ROWS), 0)
    allowed = (key_pos >= row_start) & (key_pos <= row_pos)
    bias[...] = jnp.where(allowed, 0.0, -jnp.inf).astype(jnp.float32)
    window = pl.ds(pl.multiple_of(half * ROWS, ROWS), KEYS)
    kv_local = keys.shape[2] // HEAD_DIM

    def part(kv_head, base, heads, raise_by):
        cols = [pl.ds(base + at * HEAD_DIM, HEAD_DIM) for at in range(heads)]
        stacked = jnp.concatenate([query[:, col] for col in cols], axis=0)
        key = keys[lane, window, kv_head * HEAD_DIM : (kv_head + 1) * HEAD_DIM]
        scores = lax.dot_general(
            key, stacked, (((1,), (1,)), ((), ())), preferred_element_type=jnp.float32
        )
        masks = jnp.concatenate([bias[...]] * heads, axis=1)
        weights = jnp.exp2(raise_by(scores, masks)).astype(jnp.bfloat16)
        mixed = jnp.dot(
            values_t[lane, kv_head, :, window], weights, preferred_element_type=jnp.float32
        )
        total = mixed[HEAD_DIM : HEAD_DIM + 1]
        result = (mixed[:HEAD_DIM] / total).astype(out.dtype)
        for at, col in enumerate(cols):
            out[:, col] = result[:, at * HEAD_DIM : (at + 1) * HEAD_DIM].T
        return jnp.where((total >= SMALL) & (total <= LARGE), 0, 1)

    outside = [
        part(kv_head, kv_head * GROUP * HEAD_DIM, GROUP, lambda s, m: s * EXPONENT_SCALE + m)
        for kv_head in range(kv_local)
    ]

    @pl.when(jnp.max(functools.reduce(jnp.maximum, outside)) > 0)
    def _():
        def shifted(scores, masks):
            scores = scores + masks
            return (scores - jnp.max(scores, axis=0, keepdims=True)) * EXPONENT_SCALE

        for kv_head in range(kv_local):

            @pl.loop(0, GROUP)
            def _(head):
                base = pl.multiple_of((kv_head * GROUP + head) * HEAD_DIM, HEAD_DIM)
                part(kv_head, base, 1, shifted)


def first_kernel(
    count, place_ref, lengths_ref, own, up, down, far, mate, queries, left, right,
    out_ref, keys, values_t, values, query, result, bias, sems, load_sems, store_sems,
):
    ctx, head = place_ref[0], place_ref[1]
    width = query.shape[2]
    wait = load_windows(ctx, count, own, up, down, far, mate, keys, values, sems)
    own_cols = pl.ds(pl.multiple_of(head * width, width), width)
    sources = (queries.at[:, own_cols], left, right)
    loads = [
        pltpu.make_async_copy(source, query.at[at], load_sems.at[at])
        for at, source in enumerate(sources)
    ]
    for load in loads:
        load.start()
    kv_local = keys.shape[2] // HEAD_DIM
    for lane in range(LANES):
        wait(0, lane)
        for kv_head in range(kv_local):
            values_t[lane, kv_head, :HEAD_DIM, :] = values[
                lane, :, kv_head * HEAD_DIM : (kv_head + 1) * HEAD_DIM
            ].T
            values_t[lane, kv_head, HEAD_DIM:, :] = jnp.ones(
                (PADDED - HEAD_DIM, WINDOW), values_t.dtype
            )
    for lane in range(LANES):
        wait(1, lane)
    for load in loads:
        load.wait()

    def store(at):
        shift = jnp.where(at == 0, 0, jnp.where(at == 1, 3, 1))
        block = lax.rem(head + shift, HEADS)
        rows = pl.ds(pl.multiple_of(block * ROWS, ROWS), ROWS)
        return block, pltpu.make_async_copy(result.at[at], out_ref.at[rows, :], store_sems.at[at])

    @pl.loop(0, 3)
    def _(at):
        block, copy = store(at)
        attend(
            block, ctx, count, lengths_ref[...], query.at[at], keys, values_t, bias, result.at[at]
        )
        copy.start()

    for at in range(3):
        store(at)[1].wait()


def last_kernel(
    count, place_ref, lengths_ref, query, keys, values_t, partial, out_ref, result, bias, sem
):
    ctx, head = place_ref[0], place_ref[1]
    block = lax.rem(head + 2, HEADS)
    attend(block, ctx, count, lengths_ref[...], query, keys, values_t, bias, result)
    rows = pl.ds(pl.multiple_of(block * ROWS, ROWS), ROWS)
    copy = pltpu.make_async_copy(result, out_ref.at[rows, :], sem)
    copy.start()
    copy.wait()


def attention(count, place, lengths, own, up, down, far, mate, queries, left, right, across):
    rows, width = left.shape
    kv_width = own.shape[1] // 2
    kv_local = kv_width // HEAD_DIM
    dtype = queries.dtype
    out_shape = jax.ShapeDtypeStruct((HEADS * rows, width), dtype)
    bias = pltpu.VMEM((KEYS, ROWS), jnp.float32)
    partial, keys, values_t = pl.pallas_call(
        functools.partial(first_kernel, count),
        in_specs=[SMEM_SPEC, VMEM_SPEC] + [VMEM_SPEC] * 5 + [ANY_SPEC] * 3,
        out_specs=[ANY_SPEC, VMEM_SPEC, VMEM_SPEC],
        out_shape=[
            out_shape,
            jax.ShapeDtypeStruct((LANES, WINDOW, kv_width), dtype),
            jax.ShapeDtypeStruct((LANES, kv_local, PADDED, WINDOW), dtype),
        ],
        scratch_shapes=[
            pltpu.VMEM((LANES, WINDOW, kv_width), dtype),
            pltpu.VMEM((3, rows, width), dtype),
            pltpu.VMEM((3, rows, width), dtype),
            bias,
            pltpu.SemaphoreType.DMA((2, LANES, REACH + 1)),
            pltpu.SemaphoreType.DMA((3,)),
            pltpu.SemaphoreType.DMA((3,)),
        ],
        compiler_params=PARAMS,
        name="attention_first",
    )(place, lengths, own, up, down, far, mate, queries, left, right)
    return pl.pallas_call(
        functools.partial(last_kernel, count),
        in_specs=[SMEM_SPEC] + [VMEM_SPEC] * 4 + [ANY_SPEC],
        out_specs=ANY_SPEC,
        out_shape=out_shape,
        scratch_shapes=[pltpu.VMEM((rows, width), dtype), bias, pltpu.SemaphoreType.DMA],
        input_output_aliases={5: 0},
        compiler_params=PARAMS,
        name="attention_last",
    )(place, lengths, across, keys, values_t, partial)


def body(queries, key_rows, value_rows, doc_lengths):
    count = lax.axis_size("ctx")
    ctx = lax.axis_index("ctx")
    odd = lax.rem(ctx, 2) == 1
    place = jnp.stack([ctx, lax.axis_index("head")])

    packed = kv_pack(key_rows, value_rows)
    to_next, to_previous, to_opposite = query_pack(place, queries)
    kv = lax.all_to_all(packed, "head", split_axis=0, concat_axis=0, tiled=True)
    kv = kv.reshape(LANES * STRETCH, -1)

    def rotate(block, shift):
        return lax.ppermute(block, "head", [(i, (i + shift) % HEADS) for i in range(HEADS)])

    kv, to_next, to_previous, to_opposite = lax.optimization_barrier((kv, to_next, to_previous, to_opposite))
    left = rotate(to_next, 1)
    right = rotate(to_previous, 3)
    across = rotate(to_opposite, 2)

    lane0, lane1 = kv[:STRETCH], kv[STRETCH:]
    up = lax.ppermute(lane0, "ctx", [(i, i + 2) for i in range(count - 2)])
    down = lax.ppermute(lane1, "ctx", [(i + 2, i) for i in range(count - 2)])
    route = [(i, i + 3) for i in range(1, count - 3, 2)]
    route += [(i + 3, i) for i in range(1, count - 3, 2)]
    route += [(count - 1, count - 3)]
    far = lax.ppermute(jnp.where(odd, lane0, lane1), "ctx", route)
    up, down, far, left, right = lax.optimization_barrier((up, down, far, left, right))
    passed = jnp.concatenate(
        [jnp.where(odd, lane1, lane0), up, jnp.where(ctx == count - 1, lane0, down)], axis=0
    )
    mate = lax.ppermute(passed, "ctx", [(i, i ^ 1) for i in range(count)])
    lengths = doc_lengths.reshape(1, -1)
    return attention(
        count, place, lengths, kv, up, down, far, mate, queries, left, right, across
    )


def solution(mesh):
    placed = (P(("ctx", "head"), None), P(("ctx", "head"), None), P(("ctx", "head"), None), P())
    return jax.shard_map(
        body, mesh=mesh, in_specs=placed, out_specs=P("ctx", "head"), check_vma=False
    )
```

time: 85.2 us -> 105 us (1.23)
  the two profiles are of different devices: /device:TPU:34 before, /device:TPU:149 now
where the time goes in v2:
time: 105 us; the launch traced here: 104 us
  Pallas kernels  56.6 us (54%)
  starting transfers between devices  33 us (31%)
  waiting for transfers between devices  9.88 us (9%)
  local copies, waits for them, and re-layouts  3.64 us (3%)
  other arithmetic  1.11 us (1%)
    pallas_call x1, Pallas kernels, attention(): pl.pallas_call(functools.partial(first_kernel, count), in_specs=[SMEM_SPE...  41 us
    pallas_call x1, Pallas kernels, attention(): pl.pallas_call(functools.partial(last_kernel, count), in_specs=[SMEM_SPEC...  14 us
    ppermute x3, starting transfers between devices, rotate(): lax.ppermute(block, 'head', [(i, (i + shift) % HEADS) for i in range(HEAD...  11 us
    ppermute x1, starting transfers between devices, body(): far = lax.ppermute(jnp.where(odd, lane0, lane1), 'ctx', route)  9.46 us
    all_to_all x1, starting transfers between devices, body(): kv = lax.all_to_all(packed, 'head', split_axis=0, concat_axis=0, tiled=True)  4.24 us
    unnamed x16, local copies, waits for them, and re-layouts  3.64 us
    all_to_all x1, waiting for transfers between devices, body(): kv = lax.all_to_all(packed, 'head', split_axis=0, concat_axis=0, tiled=True)  3.55 us
    ppermute x1, starting transfers between devices, body(): up = lax.ppermute(lane0, 'ctx', [(i, i + 2) for i in range(count - 2)])  3.36 us
  transfers between devices with their start and end apart: 8, of which 4 were waited for; matrix products, arithmetic and copies ran while one was open for 1% of the time, Pallas kernels for 40%

profile of v2, /device:TPU:149, one launch (start us, length us, event | category | flops | bytes accessed | tf_op | source)
XLA Modules:
  0.0 104.4 jit_solution(12304845643487518555)
XLA Ops:
  0.0 1.1 %copy-done.1 = bf16[128,1024]{1,0:T(8,128)(2,1)S(1)} copy-done((bf16[128,1024]{1,0:T(8,128)(2,1)S(1)}, bf16[128,1024]{1,0:T(8,128)(2,1)}, u32[]{:S(2)}) %copy-start.1) | copy-done | bytes 262168
  1.1 0.9 copy-done.2
  2.1 0.8 kv_pack.1
  2.9 4.2 %all-to-all-start = ((bf16[4,128,512]{2,1,0:T(8,128)(2,1)}), bf16[4,128,512]{2,1,0:T(8,128)(2,1)S(1)}, u32[]{:S(2)}, u32[]{:S(2)}) async-start(bf16[4,128,512]{2,1,0:T(8,128)(2,1)} %kv_pack.1), calls=%async_computation | async-start | bytes 1048576 | tf_op jit(solution)/shard_map/all_to_all | solution.py:287
  7.1 0.1 pad_add_fusion.place_ref
  7.2 0.0 copy-done
  7.2 0.7 query_pack.1
  7.9 0.0 copy-start.6
  7.9 0.8 copy-done.6
  8.7 0.8 copy-done.7
  9.5 3.6 %all-to-all-done = bf16[4,128,512]{2,1,0:T(8,128)(2,1)S(1)} async-done(((bf16[4,128,512]{2,1,0:T(8,128)(2,1)}), bf16[4,128,512]{2,1,0:T(8,128)(2,1)S(1)}, u32[]{:S(2)}, u32[]{:S(2)}) %all-to-all-start) | async-done | bytes 524320 | tf_op jit(solution)/shard_map/all_to_all | solution.py:287
  13.1 3.4 %collective-permute-start.4 = (bf16[128,2048]{1,0:T(8,128)(2,1)}, bf16[128,2048]{1,0:T(8,128)(2,1)}, u32[]{:S(2)}, u32[]{:S(2)}) collective-permute-start(bf16[128,2048]{1,0:T(8,128)(2,1)} %copy-done.7), channel_id=1, source_target_pairs={{0,1},{1,2},{2,3},{3,0},{4,5},{5,6},{6,7},{7,4},{8,9},{9,10},{10,1... | collective-permute-start | bytes 1572872 | tf_op jit(solution)/shard_map/ppermute | solution.py:291
  16.4 1.9 %collective-permute-start.5 = (bf16[128,2048]{1,0:T(8,128)(2,1)}, bf16[128,2048]{1,0:T(8,128)(2,1)}, u32[]{:S(2)}, u32[]{:S(2)}) collective-permute-start(bf16[128,2048]{1,0:T(8,128)(2,1)} %copy-done.6), channel_id=1, source_target_pairs={{0,3},{1,0},{2,1},{3,2},{4,7},{5,4},{6,5},{7,6},{8,11},{9,8},{10,9... | collective-permute-start | bytes 1572872 | tf_op jit(solution)/shard_map/ppermute | solution.py:291
  18.4 0.9 broadcast_select_fusion.2
  19.3 9.5 %collective-permute-start.3 = (bf16[256,512]{1,0:T(8,128)(2,1)}, bf16[256,512]{1,0:T(8,128)(2,1)S(1)}, u32[]{:S(2)}, u32[]{:S(2)}) collective-permute-start(bf16[256,512]{1,0:T(8,128)(2,1)} %get-tuple-element.37), channel_id=1, source_target_pairs={{4,16},{12,24},{20,32},{28,40},{36,48},{44,56},{52,64},{60,72},{68... | collective-permute-start | bytes 786440 | tf_op jit(solution)/shard_map/ppermute | solution.py:304
  28.8 1.9 %collective-permute-start.2 = (bf16[256,512]{1,0:T(8,128)(2,1)}, bf16[256,512]{1,0:T(8,128)(2,1)S(1)}, u32[]{:S(2)}, u32[]{:S(2)}) collective-permute-start(bf16[256,512]{1,0:T(8,128)(2,1)} %get-tuple-element.38), channel_id=1, source_target_pairs={{8,0},{12,4},{16,8},{20,12},{24,16},{28,20},{32,24},{36,28},{40,32... | collective-permute-start | bytes 786440 | tf_op jit(solution)/shard_map/ppermute | solution.py:300
  30.7 3.4 %collective-permute-start.1 = (bf16[256,512]{1,0:T(8,128)(2,1)}, bf16[256,512]{1,0:T(8,128)(2,1)S(1)}, u32[]{:S(2)}, u32[]{:S(2)}) collective-permute-start(bf16[256,512]{1,0:T(8,128)(2,1)} %get-tuple-element.39), channel_id=1, source_target_pairs={{0,8},{4,12},{8,16},{12,20},{16,24},{20,28},{24,32},{28,36},{32,40... | collective-permute-start | bytes 786440 | tf_op jit(solution)/shard_map/ppermute | solution.py:299
  34.1 0.0 copy-start.5
  34.1 1.5 %collective-permute-done.3.far = bf16[256,512]{1,0:T(8,128)(2,1)S(1)} collective-permute-done((bf16[256,512]{1,0:T(8,128)(2,1)}, bf16[256,512]{1,0:T(8,128)(2,1)S(1)}, u32[]{:S(2)}, u32[]{:S(2)}) %collective-permute-start.3) | collective-permute-done | bytes 262176 | tf_op jit(solution)/shard_map/ppermute | solution.py:304
  35.5 3.2 %collective-permute-done.2.down = bf16[256,512]{1,0:T(8,128)(2,1)S(1)} collective-permute-done((bf16[256,512]{1,0:T(8,128)(2,1)}, bf16[256,512]{1,0:T(8,128)(2,1)S(1)}, u32[]{:S(2)}, u32[]{:S(2)}) %collective-permute-start.2) | collective-permute-done | bytes 262176 | tf_op jit(solution)/shard_map/ppermute | solution.py:300
  38.8 1.6 %collective-permute-done.1.up = bf16[256,512]{1,0:T(8,128)(2,1)S(1)} collective-permute-done((bf16[256,512]{1,0:T(8,128)(2,1)}, bf16[256,512]{1,0:T(8,128)(2,1)S(1)}, u32[]{:S(2)}, u32[]{:S(2)}) %collective-permute-start.1) | collective-permute-done | bytes 262176 | tf_op jit(solution)/shard_map/ppermute | solution.py:299
  40.4 0.0 collective-permute-done.4.left
  40.4 0.0 collective-permute-done.5.right
  40.4 0.1 broadcast_select_fusion.1
  40.5 0.1 pad_maximum_fusion
  40.5 3.0 %collective-permute-start.6 = (bf16[768,512]{1,0:T(8,128)(2,1)S(1)}, bf16[768,512]{1,0:T(8,128)(2,1)S(1)}, u32[]{:S(2)}, u32[]{:S(2)}) collective-permute-start(bf16[768,512]{1,0:T(8,128)(2,1)S(1)} %pad_maximum_fusion), channel_id=1, source_target_pairs={{0,4},{4,0},{8,12},{12,8},{16,20},{20,16},{24,28},{28,24},{32,36},... | collective-permute-start | bytes 2359304 | tf_op jit(solution)/shard_map/ppermute | solution.py:309
  43.6 5.8 %collective-permute-start = (bf16[128,2048]{1,0:T(8,128)(2,1)S(1)}, bf16[128,2048]{1,0:T(8,128)(2,1)S(1)}, u32[]{:S(2)}, u32[]{:S(2)}) collective-permute-start(bf16[128,2048]{1,0:T(8,128)(2,1)S(1)} %copy-done.5), channel_id=1, source_target_pairs={{0,2},{1,3},{2,0},{3,1},{4,6},{5,7},{6,4},{7,5},{8,10},{9,11},{10,... | collective-permute-start | bytes 1572872 | tf_op jit(solution)/shard_map/ppermute | solution.py:291
  49.3 0.0 collective-permute-done.6.mate
  49.3 0.0 copy-done.3
  49.4 41.0 %attention_first.1 = (bf16[512,2048]{1,0:T(8,128)(2,1)}, bf16[2,1024,256]{2,1,0:T(8,128)(2,1)S(1)}, bf16[2,2,144,1024]{3,2,1,0:T(8,128)(2,1)S(1)}) custom-call(s32[2]{0:T(128)S(1)} %pad_add_fusion.place_ref, s32[1,128]{1,0:T(1,128)S(1)} %bitcast.7, bf16[512,512]{1,0:T(8,128)(2,1)S(1)} %bitcast.6, bf16[256,512]{1,0:T(8,128)(2,1)S(1)} %collective-permute-done.1.up, ...), custom_call_target="tpu_custom_call" | custom-call | tf_op jit(solution)/shard_map/attention_first/pallas_call | solution.py:246
  90.4 0.0 collective-permute-done.query
  90.4 14.0 %attention_last.1 = bf16[512,2048]{1,0:T(8,128)(2,1)} custom-call(s32[2]{0:T(128)S(1)} %pad_add_fusion.place_ref, s32[1,128]{1,0:T(1,128)S(1)} %bitcast.8, bf16[128,2048]{1,0:T(8,128)(2,1)S(1)} %collective-permute-done.query, bf16[2,1024,256]{2,1,0:T(8,128)(2,1)S(1)} %get-tuple-element.32.keys, ...), custom_call_target="tpu_custom_call", output_to_operand_aliasing={{}: (5, {})} | custom-call | tf_op jit(solution)/shard_map/attention_last/pallas_call | solution.py:267
  (8 shorter events, 0.0 us)
Async XLA Ops:
  0.0 7.2 %copy-start = (bf16[128,8192]{1,0:T(8,128)(2,1)S(1)}, bf16[128,8192]{1,0:T(8,128)(2,1)}, u32[]{:S(2)}) copy-start(bf16[128,8192]{1,0:T(8,128)(2,1)} %queries.1) | copy-start | bytes 6291460
  0.0 1.1 %copy-start.1 = (bf16[128,1024]{1,0:T(8,128)(2,1)S(1)}, bf16[128,1024]{1,0:T(8,128)(2,1)}, u32[]{:S(2)}) copy-start(bf16[128,1024]{1,0:T(8,128)(2,1)} %key_ref.1) | copy-start | bytes 786436
  1.1 0.9 copy-start.2
  2.9 10.2 %all-to-all-start = ((bf16[4,128,512]{2,1,0:T(8,128)(2,1)}), bf16[4,128,512]{2,1,0:T(8,128)(2,1)S(1)}, u32[]{:S(2)}, u32[]{:S(2)}) async-start(bf16[4,128,512]{2,1,0:T(8,128)(2,1)} %kv_pack.1), calls=%async_computation | async-start | bytes 1048576 | tf_op jit(solution)/shard_map/all_to_all | solution.py:287
  7.9 0.8 copy-start.6
  8.7 0.8 copy-start.7
  9.5 19.3 %copy-start.4 = (bf16[128,2048]{1,0:T(8,128)(2,1)}, bf16[128,2048]{1,0:T(8,128)(2,1)S(1)}, u32[]{:S(2)}) copy-start(bf16[128,2048]{1,0:T(8,128)(2,1)S(1)} %get-tuple-element.23) | copy-start | bytes 1572868
  13.1 27.3 %collective-permute-start.4 = (bf16[128,2048]{1,0:T(8,128)(2,1)}, bf16[128,2048]{1,0:T(8,128)(2,1)}, u32[]{:S(2)}, u32[]{:S(2)}) collective-permute-start(bf16[128,2048]{1,0:T(8,128)(2,1)} %copy-done.7), channel_id=1, source_target_pairs={{0,1},{1,2},{2,3},{3,0},{4,5},{5,6},{6,7},{7,4},{8,9},{9,10},{10,1... | collective-permute-start | bytes 1572872 | tf_op jit(solution)/shard_map/ppermute | solution.py:291
  16.4 24.0 %collective-permute-start.5 = (bf16[128,2048]{1,0:T(8,128)(2,1)}, bf16[128,2048]{1,0:T(8,128)(2,1)}, u32[]{:S(2)}, u32[]{:S(2)}) collective-permute-start(bf16[128,2048]{1,0:T(8,128)(2,1)} %copy-done.6), channel_id=1, source_target_pairs={{0,3},{1,0},{2,1},{3,2},{4,7},{5,4},{6,5},{7,6},{8,11},{9,8},{10,9... | collective-permute-start | bytes 1572872 | tf_op jit(solution)/shard_map/ppermute | solution.py:291
  19.3 30.1 %copy-start.3 = (s32[128]{0:T(128)S(1)}, s32[128]{0:T(128)}, u32[]{:S(2)}) copy-start(s32[128]{0:T(128)} %param.7) | copy-start | bytes 1540
  19.3 16.3 %collective-permute-start.3 = (bf16[256,512]{1,0:T(8,128)(2,1)}, bf16[256,512]{1,0:T(8,128)(2,1)S(1)}, u32[]{:S(2)}, u32[]{:S(2)}) collective-permute-start(bf16[256,512]{1,0:T(8,128)(2,1)} %get-tuple-element.37), channel_id=1, source_target_pairs={{4,16},{12,24},{20,32},{28,40},{36,48},{44,56},{52,64},{60,72},{68... | collective-permute-start | bytes 786440 | tf_op jit(solution)/shard_map/ppermute | solution.py:304
  28.8 10.0 %collective-permute-start.2 = (bf16[256,512]{1,0:T(8,128)(2,1)}, bf16[256,512]{1,0:T(8,128)(2,1)S(1)}, u32[]{:S(2)}, u32[]{:S(2)}) collective-permute-start(bf16[256,512]{1,0:T(8,128)(2,1)} %get-tuple-element.38), channel_id=1, source_target_pairs={{8,0},{12,4},{16,8},{20,12},{24,16},{28,20},{32,24},{36,28},{40,32... | collective-permute-start | bytes 786440 | tf_op jit(solution)/shard_map/ppermute | solution.py:300
  30.7 9.7 %collective-permute-start.1 = (bf16[256,512]{1,0:T(8,128)(2,1)}, bf16[256,512]{1,0:T(8,128)(2,1)S(1)}, u32[]{:S(2)}, u32[]{:S(2)}) collective-permute-start(bf16[256,512]{1,0:T(8,128)(2,1)} %get-tuple-element.39), channel_id=1, source_target_pairs={{0,8},{4,12},{8,16},{12,20},{16,24},{20,28},{24,32},{28,36},{32,40... | collective-permute-start | bytes 786440 | tf_op jit(solution)/shard_map/ppermute | solution.py:299
  34.1 9.5 %copy-start.5 = (bf16[128,2048]{1,0:T(8,128)(2,1)S(1)}, bf16[128,2048]{1,0:T(8,128)(2,1)}, u32[]{:S(2)}) copy-start(bf16[128,2048]{1,0:T(8,128)(2,1)} %copy-done.4) | copy-start | bytes 1572868
  40.5 8.8 %collective-permute-start.6 = (bf16[768,512]{1,0:T(8,128)(2,1)S(1)}, bf16[768,512]{1,0:T(8,128)(2,1)S(1)}, u32[]{:S(2)}, u32[]{:S(2)}) collective-permute-start(bf16[768,512]{1,0:T(8,128)(2,1)S(1)} %pad_maximum_fusion), channel_id=1, source_target_pairs={{0,4},{4,0},{8,12},{12,8},{16,20},{20,16},{24,28},{28,24},{32,36},... | collective-permute-start | bytes 2359304 | tf_op jit(solution)/shard_map/ppermute | solution.py:309
  43.6 46.8 %collective-permute-start = (bf16[128,2048]{1,0:T(8,128)(2,1)S(1)}, bf16[128,2048]{1,0:T(8,128)(2,1)S(1)}, u32[]{:S(2)}, u32[]{:S(2)}) collective-permute-start(bf16[128,2048]{1,0:T(8,128)(2,1)S(1)} %copy-done.5), channel_id=1, source_target_pairs={{0,2},{1,3},{2,0},{3,1},{4,6},{5,7},{6,4},{7,5},{8,10},{9,11},{10,... | collective-permute-start | bytes 1572872 | tf_op jit(solution)/shard_map/ppermute | solution.py:291

commit v3 on v2

--- a/solution.py
+++ b/solution.py
@@ -25,27 +25,38 @@
 PARAMS = pltpu.CompilerParams(vmem_limit_bytes=VMEM_LIMIT)
 
 
-def kv_pack_kernel(key_ref, value_ref, out_ref):
+def kv_pack_kernel(key_ref, value_ref, out_ref, sems):
     width = key_ref.shape[1] // HEADS
-    for dest in range(HEADS):
-        out_ref[dest, :, :width] = key_ref[:, dest * width : (dest + 1) * width]
-        out_ref[dest, :, width:] = value_ref[:, dest * width : (dest + 1) * width]
+    copies = [
+        pltpu.make_async_copy(
+            source.at[:, pl.ds(dest * width, width)],
+            out_ref.at[dest, :, pl.ds(kind * width, width)],
+            sems.at[kind, dest],
+        )
+        for kind, source in enumerate((key_ref, value_ref))
+        for dest in range(HEADS)
+    ]
+    for copy in copies:
+        copy.start()
+    for copy in copies:
+        copy.wait()
 
 
 def kv_pack(key_rows, value_rows):
     rows, width = key_rows.shape
     return pl.pallas_call(
         kv_pack_kernel,
-        in_specs=[VMEM_SPEC, VMEM_SPEC],
-        out_specs=VMEM_SPEC,
+        in_specs=[ANY_SPEC, ANY_SPEC],
+        out_specs=ANY_SPEC,
         out_shape=jax.ShapeDtypeStruct((HEADS, rows, 2 * width // HEADS), key_rows.dtype),
-        compiler_params=PARAMS,
+        scratch_shapes=[pltpu.SemaphoreType.DMA((2, HEADS))],
+        compiler_params=pltpu.CompilerParams(vmem_limit_bytes=60 << 20),
         name="kv_pack",
     )(key_rows, value_rows)
 
 
-def query_pack_kernel(place_ref, query_ref, *refs):
-    out_refs, sems = refs[:-1], refs[-1]
+def query_pack_kernel(place_ref, lengths_ref, query_ref, *refs):
+    out_refs, starts_ref, sems = refs[:-2], refs[-2], refs[-1]
     width = query_ref.shape[1] // HEADS
     copies = []
     for at, (shift, out_ref) in enumerate(zip((1, 3, 2), out_refs)):
@@ -55,25 +66,30 @@
         )
     for copy in copies:
         copy.start()
+    docs = lengths_ref.shape[1]
+    earlier = lax.broadcasted_iota(jnp.int32, (docs, docs), 1) < lax.broadcasted_iota(
+        jnp.int32, (docs, docs), 0
+    )
+    starts_ref[...] = 2 * jnp.sum(jnp.where(earlier, lengths_ref[...], 0), axis=1, keepdims=True)
     for copy in copies:
         copy.wait()
 
 
-def query_pack(place, queries):
+def query_pack(place, lengths, queries):
     rows, width = queries.shape
     block = jax.ShapeDtypeStruct((rows, width // HEADS), queries.dtype)
     return pl.pallas_call(
         query_pack_kernel,
-        in_specs=[SMEM_SPEC, ANY_SPEC],
-        out_specs=[ANY_SPEC] * 3,
-        out_shape=[block] * 3,
+        in_specs=[SMEM_SPEC, VMEM_SPEC, ANY_SPEC],
+        out_specs=[VMEM_SPEC] * 4,
+        out_shape=[block] * 3 + [jax.ShapeDtypeStruct((lengths.shape[1], 1), jnp.int32)],
         scratch_shapes=[pltpu.SemaphoreType.DMA((3,))],
         compiler_params=PARAMS,
         name="query_pack",
-    )(place, queries)
-
-
-def load_windows(ctx, count, own, up, down, far, mate, keys, values, sems):
+    )(place, lengths, queries)
+
+
+def load_windows(ctx, count, own, up, down, far, mate, mate_own, keys, values, sems):
     odd = lax.rem(ctx, 2) == 1
     even = jnp.logical_not(odd)
     last = ctx == count - 1
@@ -99,19 +115,19 @@
             piece(kind, own, lane * STRETCH, lane, 3).start()
     for kind in range(2):
         piece(kind, up, 0, 0, 1).start()
-    start(odd, mate, STRETCH, 0, 0)
+    start(odd, mate, 0, 0, 0)
     start(even, far, 0, 0, 0)
-    start(odd, mate, 0, 0, 2)
-    start(even, mate, STRETCH, 0, 2)
-    start(jnp.logical_and(even, plain), mate, 2 * STRETCH, 1, 0)
+    start(odd, mate_own, 0, 0, 2)
+    start(even, mate, 0, 0, 2)
+    start(jnp.logical_and(even, plain), mate, STRETCH, 1, 0)
     start(jnp.logical_and(odd, plain), far, 0, 1, 0)
     start(before_last, own, 0, 1, 0)
     start(last, up, 0, 1, 0)
     start(plain, down, 0, 1, 1)
-    start(before_last, mate, 2 * STRETCH, 1, 1)
-    start(last, mate, 0, 1, 1)
-    start(even, mate, 0, 1, 2)
-    start(jnp.logical_and(odd, plain), mate, 2 * STRETCH, 1, 2)
+    start(before_last, mate, STRETCH, 1, 1)
+    start(last, mate_own, 0, 1, 1)
+    start(even, mate_own, 0, 1, 2)
+    start(jnp.logical_and(odd, plain), mate, STRETCH, 1, 2)
     start(last, own, 0, 1, 2)
 
     def wait(kind, lane):
@@ -121,16 +137,11 @@
     return wait
 
 
-def attend(block, ctx, count, lengths, query, keys, values_t, bias, out):
+def attend(block, ctx, count, starts, query, keys, values_t, bias, out):
     lane = block // 2
     half = lax.rem(block, 2)
     stretch = jnp.where(lane == 0, ctx, 2 * count - 1 - ctx)
     first = stretch * STRETCH + half * ROWS
-    docs = lengths.shape[1]
-    earlier = lax.broadcasted_iota(jnp.int32, (docs, docs), 1) < lax.broadcasted_iota(
-        jnp.int32, (docs, docs), 0
-    )
-    starts = 2 * jnp.sum(jnp.where(earlier, lengths, 0), axis=1, keepdims=True)
     row_pos = first + lax.broadcasted_iota(jnp.int32, (1, ROWS), 1)
     row_start = jnp.max(jnp.where(starts <= row_pos, starts, 0), axis=0, keepdims=True)
     key_pos = first - REACH * STRETCH + lax.broadcasted_iota(jnp.int32, (KEYS, ROWS), 0)
@@ -177,12 +188,12 @@
 
 
 def first_kernel(
-    count, place_ref, lengths_ref, own, up, down, far, mate, queries, left, right,
+    count, place_ref, starts_ref, own, up, down, far, mate, mate_own, queries, left, right,
     out_ref, keys, values_t, values, query, result, bias, sems, load_sems, store_sems,
 ):
     ctx, head = place_ref[0], place_ref[1]
     width = query.shape[2]
-    wait = load_windows(ctx, count, own, up, down, far, mate, keys, values, sems)
+    wait = load_windows(ctx, count, own, up, down, far, mate, mate_own, keys, values, sems)
     own_cols = pl.ds(pl.multiple_of(head * width, width), width)
     sources = (queries.at[:, own_cols], left, right)
     loads = [
@@ -216,7 +227,7 @@
     def _(at):
         block, copy = store(at)
         attend(
-            block, ctx, count, lengths_ref[...], query.at[at], keys, values_t, bias, result.at[at]
+            block, ctx, count, starts_ref[...], query.at[at], keys, values_t, bias, result.at[at]
         )
         copy.start()
 
@@ -225,18 +236,18 @@
 
 
 def last_kernel(
-    count, place_ref, lengths_ref, query, keys, values_t, partial, out_ref, result, bias, sem
+    count, place_ref, starts_ref, query, keys, values_t, partial, out_ref, result, bias, sem
 ):
     ctx, head = place_ref[0], place_ref[1]
     block = lax.rem(head + 2, HEADS)
-    attend(block, ctx, count, lengths_ref[...], query, keys, values_t, bias, result)
+    attend(block, ctx, count, starts_ref[...], query, keys, values_t, bias, result)
     rows = pl.ds(pl.multiple_of(block * ROWS, ROWS), ROWS)
     copy = pltpu.make_async_copy(result, out_ref.at[rows, :], sem)
     copy.start()
     copy.wait()
 
 
-def attention(count, place, lengths, own, up, down, far, mate, queries, left, right, across):
+def attention(count, place, starts, own, up, down, far, mate, mate_own, queries, left, right, across):
     rows, width = left.shape
     kv_width = own.shape[1] // 2
     kv_local = kv_width // HEAD_DIM
@@ -245,7 +256,7 @@
     bias = pltpu.VMEM((KEYS, ROWS), jnp.float32)
     partial, keys, values_t = pl.pallas_call(
         functools.partial(first_kernel, count),
-        in_specs=[SMEM_SPEC, VMEM_SPEC] + [VMEM_SPEC] * 5 + [ANY_SPEC] * 3,
+        in_specs=[SMEM_SPEC, VMEM_SPEC] + [VMEM_SPEC] * 6 + [ANY_SPEC] * 3,
         out_specs=[ANY_SPEC, VMEM_SPEC, VMEM_SPEC],
         out_shape=[
             out_shape,
@@ -263,7 +274,7 @@
         ],
         compiler_params=PARAMS,
         name="attention_first",
-    )(place, lengths, own, up, down, far, mate, queries, left, right)
+    )(place, starts, own, up, down, far, mate, mate_own, queries, left, right)
     return pl.pallas_call(
         functools.partial(last_kernel, count),
         in_specs=[SMEM_SPEC] + [VMEM_SPEC] * 4 + [ANY_SPEC],
@@ -273,7 +284,7 @@
         input_output_aliases={5: 0},
         compiler_params=PARAMS,
         name="attention_last",
-    )(place, lengths, across, keys, values_t, partial)
+    )(place, starts, across, keys, values_t, partial)
 
 
 def body(queries, key_rows, value_rows, doc_lengths):
@@ -283,14 +294,14 @@
     place = jnp.stack([ctx, lax.axis_index("head")])
 
     packed = kv_pack(key_rows, value_rows)
-    to_next, to_previous, to_opposite = query_pack(place, queries)
+    to_next, to_previous, to_opposite, starts = query_pack(place, doc_lengths.reshape(1, -1), queries)
     kv = lax.all_to_all(packed, "head", split_axis=0, concat_axis=0, tiled=True)
     kv = kv.reshape(LANES * STRETCH, -1)
 
     def rotate(block, shift):
         return lax.ppermute(block, "head", [(i, (i + shift) % HEADS) for i in range(HEADS)])
 
-    kv, to_next, to_previous, to_opposite = lax.optimization_barrier((kv, to_next, to_previous, to_opposite))
+    kv, starts = lax.optimization_barrier((kv, starts))
     left = rotate(to_next, 1)
     right = rotate(to_previous, 3)
     across = rotate(to_opposite, 2)
@@ -302,14 +313,14 @@
     route += [(i + 3, i) for i in range(1, count - 3, 2)]
     route += [(count - 1, count - 3)]
     far = lax.ppermute(jnp.where(odd, lane0, lane1), "ctx", route)
-    up, down, far, left, right = lax.optimization_barrier((up, down, far, left, right))
-    passed = jnp.concatenate(
-        [jnp.where(odd, lane1, lane0), up, jnp.where(ctx == count - 1, lane0, down)], axis=0
-    )
-    mate = lax.ppermute(passed, "ctx", [(i, i ^ 1) for i in range(count)])
-    lengths = doc_lengths.reshape(1, -1)
+    up, down, far = lax.optimization_barrier((up, down, far))
+    passed = jnp.concatenate([up, jnp.where(ctx == count - 1, lane0, down)], axis=0)
+    swap = [(i, i ^ 1) for i in range(count)]
+    mate = lax.ppermute(passed, "ctx", swap)
+    inner, left, right = lax.optimization_barrier((jnp.where(odd, lane1, lane0), left, right))
+    mate_own = lax.ppermute(inner, "ctx", swap)
     return attention(
-        count, place, lengths, kv, up, down, far, mate, queries, left, right, across
+        count, place, starts, kv, up, down, far, mate, mate_own, queries, left, right, across
     )
 
 

time: 105 us -> 134 us (1.28)
  the two profiles are of different devices: /device:TPU:149 before, /device:TPU:143 now
where the time goes in v3:
time: 134 us; the launch traced here: 133 us
  Pallas kernels  72.6 us (54%)
  starting transfers between devices  33.1 us (25%)
  waiting for transfers between devices  24.9 us (19%)
  local copies, waits for them, and re-layouts  1.61 us (1%)
    pallas_call x1, Pallas kernels, attention(): pl.pallas_call(functools.partial(first_kernel, count), in_specs=[SMEM_SPE...  40.8 us
    ppermute x3, waiting for transfers between devices, rotate(): lax.ppermute(block, 'head', [(i, (i + shift) % HEADS) for i in range(HEAD...  18.9 us
    pallas_call x1, Pallas kernels, kv_pack(): pl.pallas_call(kv_pack_kernel, in_specs=[ANY_SPEC, ANY_SPEC], out_specs=A...  17.1 us
    pallas_call x1, Pallas kernels, attention(): pl.pallas_call(functools.partial(last_kernel, count), in_specs=[SMEM_SPEC...  14 us
    ppermute x3, starting transfers between devices, rotate(): lax.ppermute(block, 'head', [(i, (i + shift) % HEADS) for i in range(HEAD...  9.32 us
    ppermute x1, starting transfers between devices, body(): far = lax.ppermute(jnp.where(odd, lane0, lane1), 'ctx', route)  9.05 us
    all_to_all x1, starting transfers between devices, body(): kv = lax.all_to_all(packed, 'head', split_axis=0, concat_axis=0, tiled=True)  4.22 us
    all_to_all x1, waiting for transfers between devices, body(): kv = lax.all_to_all(packed, 'head', split_axis=0, concat_axis=0, tiled=True)  3.99 us
  transfers between devices with their start and end apart: 9, of which 5 were waited for; matrix products, arithmetic and copies ran while one was open for 0% of the time, Pallas kernels for 31%

profile of v3, /device:TPU:143, one launch (start us, length us, event | category | flops | bytes accessed | tf_op | source)
XLA Modules:
  0.0 133.4 jit_solution(577668164300253477)
XLA Ops:
  0.0 17.1 %kv_pack.1 = bf16[4,128,512]{2,1,0:T(8,128)(2,1)} custom-call(bf16[128,1024]{1,0:T(8,128)(2,1)} %key_ref.1, bf16[128,1024]{1,0:T(8,128)(2,1)} %value_ref.1), custom_call_target="tpu_custom_call" | custom-call | tf_op jit(solution)/shard_map/kv_pack/pallas_call | solution.py:47
  17.1 4.2 %all-to-all-start = ((bf16[4,128,512]{2,1,0:T(8,128)(2,1)}), bf16[4,128,512]{2,1,0:T(8,128)(2,1)S(1)}, u32[]{:S(2)}, u32[]{:S(2)}) async-start(bf16[4,128,512]{2,1,0:T(8,128)(2,1)} %kv_pack.1), calls=%async_computation | async-start | bytes 1048576 | tf_op jit(solution)/shard_map/all_to_all | solution.py:298
  21.3 0.1 pad_add_fusion.place_ref
  21.4 0.0 copy-done
  21.4 0.0 copy-done.1
  21.4 0.8 query_pack.1
  22.2 0.0 copy-start.4
  22.2 0.8 copy-done.4
  23.0 0.8 copy-done.5
  23.8 4.0 %all-to-all-done = bf16[4,128,512]{2,1,0:T(8,128)(2,1)S(1)} async-done(((bf16[4,128,512]{2,1,0:T(8,128)(2,1)}), bf16[4,128,512]{2,1,0:T(8,128)(2,1)S(1)}, u32[]{:S(2)}, u32[]{:S(2)}) %all-to-all-start) | async-done | bytes 524320 | tf_op jit(solution)/shard_map/all_to_all | solution.py:298
  27.8 0.9 broadcast_select_fusion.2
  28.7 9.1 %collective-permute-start.3 = (bf16[256,512]{1,0:T(8,128)(2,1)}, bf16[256,512]{1,0:T(8,128)(2,1)S(1)}, u32[]{:S(2)}, u32[]{:S(2)}) collective-permute-start(bf16[256,512]{1,0:T(8,128)(2,1)} %get-tuple-element.37), channel_id=1, source_target_pairs={{4,16},{12,24},{20,32},{28,40},{36,48},{44,56},{52,64},{60,72},{68... | collective-permute-start | bytes 786440 | tf_op jit(solution)/shard_map/ppermute | solution.py:315
  37.8 0.0 copy-done.2
  37.8 1.9 %collective-permute-start.2 = (bf16[256,512]{1,0:T(8,128)(2,1)}, bf16[256,512]{1,0:T(8,128)(2,1)S(1)}, u32[]{:S(2)}, u32[]{:S(2)}) collective-permute-start(bf16[256,512]{1,0:T(8,128)(2,1)} %get-tuple-element.38), channel_id=1, source_target_pairs={{8,0},{12,4},{16,8},{20,12},{24,16},{28,20},{32,24},{36,28},{40,32... | collective-permute-start | bytes 786440 | tf_op jit(solution)/shard_map/ppermute | solution.py:311
  39.7 3.4 %collective-permute-start.1 = (bf16[256,512]{1,0:T(8,128)(2,1)}, bf16[256,512]{1,0:T(8,128)(2,1)S(1)}, u32[]{:S(2)}, u32[]{:S(2)}) collective-permute-start(bf16[256,512]{1,0:T(8,128)(2,1)} %get-tuple-element.39), channel_id=1, source_target_pairs={{0,8},{4,12},{8,16},{12,20},{16,24},{20,28},{24,32},{28,36},{32,40... | collective-permute-start | bytes 786440 | tf_op jit(solution)/shard_map/ppermute | solution.py:310
  43.1 3.7 %collective-permute-start.5 = (bf16[128,2048]{1,0:T(8,128)(2,1)}, bf16[128,2048]{1,0:T(8,128)(2,1)}, u32[]{:S(2)}, u32[]{:S(2)}) collective-permute-start(bf16[128,2048]{1,0:T(8,128)(2,1)} %copy-done.5), channel_id=1, source_target_pairs={{0,1},{1,2},{2,3},{3,0},{4,5},{5,6},{6,7},{7,4},{8,9},{9,10},{10,1... | collective-permute-start | bytes 1572872 | tf_op jit(solution)/shard_map/ppermute | solution.py:302
  46.8 1.9 %collective-permute-start.6 = (bf16[128,2048]{1,0:T(8,128)(2,1)}, bf16[128,2048]{1,0:T(8,128)(2,1)}, u32[]{:S(2)}, u32[]{:S(2)}) collective-permute-start(bf16[128,2048]{1,0:T(8,128)(2,1)} %copy-done.4), channel_id=1, source_target_pairs={{0,3},{1,0},{2,1},{3,2},{4,7},{5,4},{6,5},{7,6},{8,11},{9,8},{10,9... | collective-permute-start | bytes 1572872 | tf_op jit(solution)/shard_map/ppermute | solution.py:302
  48.7 0.0 copy-start.3
  48.7 0.0 collective-permute-done.3.far
  48.7 0.0 collective-permute-done.2.down
  48.7 0.8 collective-permute-done.1.up
  49.5 0.1 broadcast_select_fusion.1
  49.7 2.9 %collective-permute-start.4 = (bf16[512,512]{1,0:T(8,128)(2,1)S(1)}, bf16[512,512]{1,0:T(8,128)(2,1)S(1)}, u32[]{:S(2)}, u32[]{:S(2)}) collective-permute-start(bf16[512,512]{1,0:T(8,128)(2,1)S(1)} %pad_maximum_fusion), channel_id=1, source_target_pairs={{0,4},{4,0},{8,12},{12,8},{16,20},{20,16},{24,28},{28,24},{32,36},... | collective-permute-start | bytes 1572872 | tf_op jit(solution)/shard_map/ppermute | solution.py:319
  52.6 3.7 %collective-permute-start = (bf16[128,2048]{1,0:T(8,128)(2,1)S(1)}, bf16[128,2048]{1,0:T(8,128)(2,1)S(1)}, u32[]{:S(2)}, u32[]{:S(2)}) collective-permute-start(bf16[128,2048]{1,0:T(8,128)(2,1)S(1)} %copy-done.3), channel_id=1, source_target_pairs={{0,2},{1,3},{2,0},{3,1},{4,6},{5,7},{6,4},{7,5},{8,10},{9,11},{10,... | collective-permute-start | bytes 1572872 | tf_op jit(solution)/shard_map/ppermute | solution.py:302
  56.3 13.4 %collective-permute-done.5.left = bf16[128,2048]{1,0:T(8,128)(2,1)} collective-permute-done((bf16[128,2048]{1,0:T(8,128)(2,1)}, bf16[128,2048]{1,0:T(8,128)(2,1)}, u32[]{:S(2)}, u32[]{:S(2)}) %collective-permute-start.5) | collective-permute-done | bytes 524320 | tf_op jit(solution)/shard_map/ppermute | solution.py:302
  69.7 5.5 %collective-permute-done.6.right = bf16[128,2048]{1,0:T(8,128)(2,1)} collective-permute-done((bf16[128,2048]{1,0:T(8,128)(2,1)}, bf16[128,2048]{1,0:T(8,128)(2,1)}, u32[]{:S(2)}, u32[]{:S(2)}) %collective-permute-start.6) | collective-permute-done | bytes 524320 | tf_op jit(solution)/shard_map/ppermute | solution.py:302
  75.2 2.3 %collective-permute-start.7 = (bf16[256,512]{1,0:T(8,128)(2,1)S(1)}, bf16[256,512]{1,0:T(8,128)(2,1)S(1)}, u32[]{:S(2)}, u32[]{:S(2)}) collective-permute-start(bf16[256,512]{1,0:T(8,128)(2,1)S(1)} %get-tuple-element.29), channel_id=1, source_target_pairs={{0,4},{4,0},{8,12},{12,8},{16,20},{20,16},{24,28},{28,24},{32,36},... | collective-permute-start | bytes 786440 | tf_op jit(solution)/shard_map/ppermute | solution.py:321
  77.5 1.1 collective-permute-done.7.mate_own
  78.6 0.0 collective-permute-done.4.mate
  78.6 40.8 %attention_first.1 = (bf16[512,2048]{1,0:T(8,128)(2,1)}, bf16[2,1024,256]{2,1,0:T(8,128)(2,1)S(1)}, bf16[2,2,144,1024]{3,2,1,0:T(8,128)(2,1)S(1)}) custom-call(s32[2]{0:T(128)S(1)} %pad_add_fusion.place_ref, s32[128,1]{1,0:T(8,128)S(1)} %get-tuple-element.21.starts_ref, bf16[512,512]{1,0:T(8,128)(2,1)S(1)} %bitcast.6, ...), custom_call_target="tpu_custom_call" | custom-call | tf_op jit(solution)/shard_map/attention_first/pallas_call | solution.py:257
  119.4 0.0 collective-permute-done.query
  119.4 14.0 %attention_last.1 = bf16[512,2048]{1,0:T(8,128)(2,1)} custom-call(s32[2]{0:T(128)S(1)} %pad_add_fusion.place_ref, s32[128,1]{1,0:T(8,128)S(1)} %get-tuple-element.21.starts_ref, bf16[128,2048]{1,0:T(8,128)(2,1)S(1)} %collective-permute-done.query, bf16[2,1024,256]{2,1,0:T(8,128)(2,1)S(1)} %get-tuple-element.32.keys, ...), custom_call_target="tpu_custom_call", output_to_operand_aliasing={{}: (5, {})} | custom-call | tf_op jit(solution)/shard_map/attention_last/pallas_call | solution.py:278
  (6 shorter events, 0.0 us)
Async XLA Ops:
  0.0 21.4 %copy-start = (bf16[128,8192]{1,0:T(8,128)(2,1)S(1)}, bf16[128,8192]{1,0:T(8,128)(2,1)}, u32[]{:S(2)}) copy-start(bf16[128,8192]{1,0:T(8,128)(2,1)} %queries.1) | copy-start | bytes 6291460
  0.0 21.4 %copy-start.1 = (s32[128]{0:T(128)S(1)}, s32[128]{0:T(128)}, u32[]{:S(2)}) copy-start(s32[128]{0:T(128)} %param.7) | copy-start | bytes 1540
  17.1 10.7 %all-to-all-start = ((bf16[4,128,512]{2,1,0:T(8,128)(2,1)}), bf16[4,128,512]{2,1,0:T(8,128)(2,1)S(1)}, u32[]{:S(2)}, u32[]{:S(2)}) async-start(bf16[4,128,512]{2,1,0:T(8,128)(2,1)} %kv_pack.1), calls=%async_computation | async-start | bytes 1048576 | tf_op jit(solution)/shard_map/all_to_all | solution.py:298
  22.2 0.8 copy-start.4
  23.0 0.8 copy-start.5
  23.8 14.0 %copy-start.2 = (bf16[128,2048]{1,0:T(8,128)(2,1)}, bf16[128,2048]{1,0:T(8,128)(2,1)S(1)}, u32[]{:S(2)}) copy-start(bf16[128,2048]{1,0:T(8,128)(2,1)S(1)} %get-tuple-element.22) | copy-start | bytes 1572868
  28.7 20.0 %collective-permute-start.3 = (bf16[256,512]{1,0:T(8,128)(2,1)}, bf16[256,512]{1,0:T(8,128)(2,1)S(1)}, u32[]{:S(2)}, u32[]{:S(2)}) collective-permute-start(bf16[256,512]{1,0:T(8,128)(2,1)} %get-tuple-element.37), channel_id=1, source_target_pairs={{4,16},{12,24},{20,32},{28,40},{36,48},{44,56},{52,64},{60,72},{68... | collective-permute-start | bytes 786440 | tf_op jit(solution)/shard_map/ppermute | solution.py:315
  37.8 11.0 %collective-permute-start.2 = (bf16[256,512]{1,0:T(8,128)(2,1)}, bf16[256,512]{1,0:T(8,128)(2,1)S(1)}, u32[]{:S(2)}, u32[]{:S(2)}) collective-permute-start(bf16[256,512]{1,0:T(8,128)(2,1)} %get-tuple-element.38), channel_id=1, source_target_pairs={{8,0},{12,4},{16,8},{20,12},{24,16},{28,20},{32,24},{36,28},{40,32... | collective-permute-start | bytes 786440 | tf_op jit(solution)/shard_map/ppermute | solution.py:311
  39.7 9.8 %collective-permute-start.1 = (bf16[256,512]{1,0:T(8,128)(2,1)}, bf16[256,512]{1,0:T(8,128)(2,1)S(1)}, u32[]{:S(2)}, u32[]{:S(2)}) collective-permute-start(bf16[256,512]{1,0:T(8,128)(2,1)} %get-tuple-element.39), channel_id=1, source_target_pairs={{0,8},{4,12},{8,16},{12,20},{16,24},{20,28},{24,32},{28,36},{32,40... | collective-permute-start | bytes 786440 | tf_op jit(solution)/shard_map/ppermute | solution.py:310
  43.1 26.6 %collective-permute-start.5 = (bf16[128,2048]{1,0:T(8,128)(2,1)}, bf16[128,2048]{1,0:T(8,128)(2,1)}, u32[]{:S(2)}, u32[]{:S(2)}) collective-permute-start(bf16[128,2048]{1,0:T(8,128)(2,1)} %copy-done.5), channel_id=1, source_target_pairs={{0,1},{1,2},{2,3},{3,0},{4,5},{5,6},{6,7},{7,4},{8,9},{9,10},{10,1... | collective-permute-start | bytes 1572872 | tf_op jit(solution)/shard_map/ppermute | solution.py:302
  46.8 28.4 %collective-permute-start.6 = (bf16[128,2048]{1,0:T(8,128)(2,1)}, bf16[128,2048]{1,0:T(8,128)(2,1)}, u32[]{:S(2)}, u32[]{:S(2)}) collective-permute-start(bf16[128,2048]{1,0:T(8,128)(2,1)} %copy-done.4), channel_id=1, source_target_pairs={{0,3},{1,0},{2,1},{3,2},{4,7},{5,4},{6,5},{7,6},{8,11},{9,8},{10,9... | collective-permute-start | bytes 1572872 | tf_op jit(solution)/shard_map/ppermute | solution.py:302
  48.7 3.8 %copy-start.3 = (bf16[128,2048]{1,0:T(8,128)(2,1)S(1)}, bf16[128,2048]{1,0:T(8,128)(2,1)}, u32[]{:S(2)}) copy-start(bf16[128,2048]{1,0:T(8,128)(2,1)} %copy-done.2) | copy-start | bytes 1572868
  49.7 29.0 %collective-permute-start.4 = (bf16[512,512]{1,0:T(8,128)(2,1)S(1)}, bf16[512,512]{1,0:T(8,128)(2,1)S(1)}, u32[]{:S(2)}, u32[]{:S(2)}) collective-permute-start(bf16[512,512]{1,0:T(8,128)(2,1)S(1)} %pad_maximum_fusion), channel_id=1, source_target_pairs={{0,4},{4,0},{8,12},{12,8},{16,20},{20,16},{24,28},{28,24},{32,36},... | collective-permute-start | bytes 1572872 | tf_op jit(solution)/shard_map/ppermute | solution.py:319
  52.6 66.9 %collective-permute-start = (bf16[128,2048]{1,0:T(8,128)(2,1)S(1)}, bf16[128,2048]{1,0:T(8,128)(2,1)S(1)}, u32[]{:S(2)}, u32[]{:S(2)}) collective-permute-start(bf16[128,2048]{1,0:T(8,128)(2,1)S(1)} %copy-done.3), channel_id=1, source_target_pairs={{0,2},{1,3},{2,0},{3,1},{4,6},{5,7},{6,4},{7,5},{8,10},{9,11},{10,... | collective-permute-start | bytes 1572872 | tf_op jit(solution)/shard_map/ppermute | solution.py:302
  75.2 3.4 %collective-permute-start.7 = (bf16[256,512]{1,0:T(8,128)(2,1)S(1)}, bf16[256,512]{1,0:T(8,128)(2,1)S(1)}, u32[]{:S(2)}, u32[]{:S(2)}) collective-permute-start(bf16[256,512]{1,0:T(8,128)(2,1)S(1)} %get-tuple-element.29), channel_id=1, source_target_pairs={{0,4},{4,0},{8,12},{12,8},{16,20},{20,16},{24,28},{28,24},{32,36},... | collective-permute-start | bytes 786440 | tf_op jit(solution)/shard_map/ppermute | solution.py:321

commit v4 on v3

--- a/solution.py
+++ b/solution.py
@@ -25,21 +25,27 @@
 PARAMS = pltpu.CompilerParams(vmem_limit_bytes=VMEM_LIMIT)
 
 
-def kv_pack_kernel(key_ref, value_ref, out_ref, sems):
+def kv_pack_kernel(key_ref, value_ref, out_ref, stage, sems):
     width = key_ref.shape[1] // HEADS
-    copies = [
-        pltpu.make_async_copy(
-            source.at[:, pl.ds(dest * width, width)],
-            out_ref.at[dest, :, pl.ds(kind * width, width)],
-            sems.at[kind, dest],
-        )
+    loads = [
+        pltpu.make_async_copy(source, stage.at[kind], sems.at[kind, HEADS])
         for kind, source in enumerate((key_ref, value_ref))
-        for dest in range(HEADS)
     ]
-    for copy in copies:
-        copy.start()
-    for copy in copies:
-        copy.wait()
+    for load in loads:
+        load.start()
+    stores = []
+    for kind, load in enumerate(loads):
+        load.wait()
+        for dest in range(HEADS):
+            store = pltpu.make_async_copy(
+                stage.at[kind, :, pl.ds(dest * width, width)],
+                out_ref.at[dest, :, pl.ds(kind * width, width)],
+                sems.at[kind, dest],
+            )
+            store.start()
+            stores.append(store)
+    for store in stores:
+        store.wait()
 
 
 def kv_pack(key_rows, value_rows):
@@ -49,7 +55,10 @@
         in_specs=[ANY_SPEC, ANY_SPEC],
         out_specs=ANY_SPEC,
         out_shape=jax.ShapeDtypeStruct((HEADS, rows, 2 * width // HEADS), key_rows.dtype),
-        scratch_shapes=[pltpu.SemaphoreType.DMA((2, HEADS))],
+        scratch_shapes=[
+            pltpu.VMEM((2, rows, width), key_rows.dtype),
+            pltpu.SemaphoreType.DMA((2, HEADS + 1)),
+        ],
         compiler_params=pltpu.CompilerParams(vmem_limit_bytes=60 << 20),
         name="kv_pack",
     )(key_rows, value_rows)
@@ -89,7 +98,7 @@
     )(place, lengths, queries)
 
 
-def load_windows(ctx, count, own, up, down, far, mate, mate_own, keys, values, sems):
+def load_windows(ctx, count, own, up, down, far, mate, keys, values, sems):
     odd = lax.rem(ctx, 2) == 1
     even = jnp.logical_not(odd)
     last = ctx == count - 1
@@ -117,7 +126,7 @@
         piece(kind, up, 0, 0, 1).start()
     start(odd, mate, 0, 0, 0)
     start(even, far, 0, 0, 0)
-    start(odd, mate_own, 0, 0, 2)
+    start(odd, mate, 2 * STRETCH, 0, 2)
     start(even, mate, 0, 0, 2)
     start(jnp.logical_and(even, plain), mate, STRETCH, 1, 0)
     start(jnp.logical_and(odd, plain), far, 0, 1, 0)
@@ -125,8 +134,8 @@
     start(last, up, 0, 1, 0)
     start(plain, down, 0, 1, 1)
     start(before_last, mate, STRETCH, 1, 1)
-    start(last, mate_own, 0, 1, 1)
-    start(even, mate_own, 0, 1, 2)
+    start(last, mate, 2 * STRETCH, 1, 1)
+    start(even, mate, 2 * STRETCH, 1, 2)
     start(jnp.logical_and(odd, plain), mate, STRETCH, 1, 2)
     start(last, own, 0, 1, 2)
 
@@ -188,12 +197,12 @@
 
 
 def first_kernel(
-    count, place_ref, starts_ref, own, up, down, far, mate, mate_own, queries, left, right,
+    count, place_ref, starts_ref, own, up, down, far, mate, queries, left, right,
     out_ref, keys, values_t, values, query, result, bias, sems, load_sems, store_sems,
 ):
     ctx, head = place_ref[0], place_ref[1]
     width = query.shape[2]
-    wait = load_windows(ctx, count, own, up, down, far, mate, mate_own, keys, values, sems)
+    wait = load_windows(ctx, count, own, up, down, far, mate, keys, values, sems)
     own_cols = pl.ds(pl.multiple_of(head * width, width), width)
     sources = (queries.at[:, own_cols], left, right)
     loads = [
@@ -247,7 +256,7 @@
     copy.wait()
 
 
-def attention(count, place, starts, own, up, down, far, mate, mate_own, queries, left, right, across):
+def attention(count, place, starts, own, up, down, far, mate, queries, left, right, across):
     rows, width = left.shape
     kv_width = own.shape[1] // 2
     kv_local = kv_width // HEAD_DIM
@@ -256,7 +265,7 @@
     bias = pltpu.VMEM((KEYS, ROWS), jnp.float32)
     partial, keys, values_t = pl.pallas_call(
         functools.partial(first_kernel, count),
-        in_specs=[SMEM_SPEC, VMEM_SPEC] + [VMEM_SPEC] * 6 + [ANY_SPEC] * 3,
+        in_specs=[SMEM_SPEC, VMEM_SPEC] + [VMEM_SPEC] * 5 + [ANY_SPEC] * 3,
         out_specs=[ANY_SPEC, VMEM_SPEC, VMEM_SPEC],
         out_shape=[
             out_shape,
@@ -274,7 +283,7 @@
         ],
         compiler_params=PARAMS,
         name="attention_first",
-    )(place, starts, own, up, down, far, mate, mate_own, queries, left, right)
+    )(place, starts, own, up, down, far, mate, queries, left, right)
     return pl.pallas_call(
         functools.partial(last_kernel, count),
         in_specs=[SMEM_SPEC] + [VMEM_SPEC] * 4 + [ANY_SPEC],
@@ -313,14 +322,13 @@
     route += [(i + 3, i) for i in range(1, count - 3, 2)]
     route += [(count - 1, count - 3)]
     far = lax.ppermute(jnp.where(odd, lane0, lane1), "ctx", route)
-    up, down, far = lax.optimization_barrier((up, down, far))
-    passed = jnp.concatenate([up, jnp.where(ctx == count - 1, lane0, down)], axis=0)
-    swap = [(i, i ^ 1) for i in range(count)]
-    mate = lax.ppermute(passed, "ctx", swap)
-    inner, left, right = lax.optimization_barrier((jnp.where(odd, lane1, lane0), left, right))
-    mate_own = lax.ppermute(inner, "ctx", swap)
+    up, down, far, left, right = lax.optimization_barrier((up, down, far, left, right))
+    passed = jnp.concatenate(
+        [up, jnp.where(ctx == count - 1, lane0, down), jnp.where(odd, lane1, lane0)], axis=0
+    )
+    mate = lax.ppermute(passed, "ctx", [(i, i ^ 1) for i in range(count)])
     return attention(
-        count, place, starts, kv, up, down, far, mate, mate_own, queries, left, right, across
+        count, place, starts, kv, up, down, far, mate, queries, left, right, across
     )
 
 

time: 134 us -> 98.3 us (0.73)
  the two profiles are of different devices: /device:TPU:143 before, /device:TPU:4 now
where the time goes in v4:
time: 98.3 us; the launch traced here: 98 us
  Pallas kernels  58.8 us (60%)
  starting transfers between devices  29.3 us (30%)
  waiting for transfers between devices  8.49 us (9%)
  other arithmetic  1.13 us (1%)
    pallas_call x1, Pallas kernels, attention(): pl.pallas_call(functools.partial(first_kernel, count), in_specs=[SMEM_SPE...  41 us
    pallas_call x1, Pallas kernels, attention(): pl.pallas_call(functools.partial(last_kernel, count), in_specs=[SMEM_SPEC...  14 us
    ppermute x3, starting transfers between devices, rotate(): lax.ppermute(block, 'head', [(i, (i + shift) % HEADS) for i in range(HEAD...  11.1 us
    all_to_all x1, starting transfers between devices, body(): kv = lax.all_to_all(packed, 'head', split_axis=0, concat_axis=0, tiled=True)  9.33 us
    ppermute x1, waiting for transfers between devices, body(): down = lax.ppermute(lane1, 'ctx', [(i + 2, i) for i in range(count - 2)])  6.7 us
    ppermute x1, starting transfers between devices, body(): up = lax.ppermute(lane0, 'ctx', [(i, i + 2) for i in range(count - 2)])  4.56 us
    ppermute x1, starting transfers between devices, body(): mate = lax.ppermute(passed, 'ctx', [(i, i ^ 1) for i in range(count)])  2.35 us
    pallas_call x1, Pallas kernels, kv_pack(): pl.pallas_call(kv_pack_kernel, in_specs=[ANY_SPEC, ANY_SPEC], out_specs=A...  2.01 us
  transfers between devices with their start and end apart: 8, of which 3 were waited for; matrix products, arithmetic and copies ran while one was open for 1% of the time, Pallas kernels for 44%

profile of v4, /device:TPU:4, one launch (start us, length us, event | category | flops | bytes accessed | tf_op | source)
XLA Modules:
  0.0 98.0 jit_solution(16262348584569802737)
XLA Ops:
  0.0 0.0 copy-start
  0.0 0.0 copy-start.1
  0.0 2.0 %kv_pack.1 = bf16[4,128,512]{2,1,0:T(8,128)(2,1)} custom-call(bf16[128,1024]{1,0:T(8,128)(2,1)} %key_ref.1, bf16[128,1024]{1,0:T(8,128)(2,1)} %value_ref.1), custom_call_target="tpu_custom_call" | custom-call | tf_op jit(solution)/shard_map/kv_pack/pallas_call | solution.py:53
  2.0 9.3 %all-to-all-start = ((bf16[4,128,512]{2,1,0:T(8,128)(2,1)}), bf16[4,128,512]{2,1,0:T(8,128)(2,1)S(1)}, u32[]{:S(2)}, u32[]{:S(2)}) async-start(bf16[4,128,512]{2,1,0:T(8,128)(2,1)} %kv_pack.1), calls=%async_computation | async-start | bytes 1048576 | tf_op jit(solution)/shard_map/all_to_all | solution.py:307
  11.3 0.1 pad_add_fusion.place_ref
  11.4 0.0 copy-done
  11.4 0.0 copy-done.1
  11.4 1.8 %query_pack.1 = (bf16[128,2048]{1,0:T(8,128)(2,1)}, bf16[128,2048]{1,0:T(8,128)(2,1)}, bf16[128,2048]{1,0:T(8,128)(2,1)S(1)}, s32[128,1]{1,0:T(8,128)S(1)}) custom-call(s32[2]{0:T(128)S(1)} %pad_add_fusion.place_ref, s32[1,128]{1,0:T(1,128)S(1)} %bitcast.7, bf16[128,8192]{1,0:T(8,128)(2,1)S(1)} %copy-done), custom_call_target="tpu_custom_call" | custom-call | tf_op jit(solution)/shard_map/query_pack/pallas_call | solution.py:90
  13.2 0.0 copy-start.2
  13.3 3.1 %collective-permute-start.4 = (bf16[128,2048]{1,0:T(8,128)(2,1)}, bf16[128,2048]{1,0:T(8,128)(2,1)}, u32[]{:S(2)}, u32[]{:S(2)}) collective-permute-start(bf16[128,2048]{1,0:T(8,128)(2,1)} %get-tuple-element.23), channel_id=1, source_target_pairs={{0,1},{1,2},{2,3},{3,0},{4,5},{5,6},{6,7},{7,4},{8,9},{9,10},{10,1... | collective-permute-start | bytes 1572872 | tf_op jit(solution)/shard_map/ppermute | solution.py:311
  16.3 2.8 %collective-permute-start.5 = (bf16[128,2048]{1,0:T(8,128)(2,1)}, bf16[128,2048]{1,0:T(8,128)(2,1)}, u32[]{:S(2)}, u32[]{:S(2)}) collective-permute-start(bf16[128,2048]{1,0:T(8,128)(2,1)} %get-tuple-element.24), channel_id=1, source_target_pairs={{0,3},{1,0},{2,1},{3,2},{4,7},{5,4},{6,5},{7,6},{8,11},{9,8},{10,9... | collective-permute-start | bytes 1572872 | tf_op jit(solution)/shard_map/ppermute | solution.py:311
  19.1 0.0 all-to-all-done
  19.1 0.9 broadcast_select_fusion.2
  20.1 0.7 collective-permute-start.3
  20.7 0.0 copy-done.2
  20.8 1.3 %collective-permute-start.2 = (bf16[256,512]{1,0:T(8,128)(2,1)}, bf16[256,512]{1,0:T(8,128)(2,1)S(1)}, u32[]{:S(2)}, u32[]{:S(2)}) collective-permute-start(bf16[256,512]{1,0:T(8,128)(2,1)} %get-tuple-element.36), channel_id=1, source_target_pairs={{8,0},{12,4},{16,8},{20,12},{24,16},{28,20},{32,24},{36,28},{40,32... | collective-permute-start | bytes 786440 | tf_op jit(solution)/shard_map/ppermute | solution.py:320
  22.1 4.6 %collective-permute-start.1 = (bf16[256,512]{1,0:T(8,128)(2,1)}, bf16[256,512]{1,0:T(8,128)(2,1)S(1)}, u32[]{:S(2)}, u32[]{:S(2)}) collective-permute-start(bf16[256,512]{1,0:T(8,128)(2,1)} %get-tuple-element.37), channel_id=1, source_target_pairs={{0,8},{4,12},{8,16},{12,20},{16,24},{20,28},{24,32},{28,36},{32,40... | collective-permute-start | bytes 786440 | tf_op jit(solution)/shard_map/ppermute | solution.py:319
  26.6 0.0 copy-start.3
  26.6 0.2 collective-permute-done.4.left
  26.9 1.6 %collective-permute-done.5.right = bf16[128,2048]{1,0:T(8,128)(2,1)} collective-permute-done((bf16[128,2048]{1,0:T(8,128)(2,1)}, bf16[128,2048]{1,0:T(8,128)(2,1)}, u32[]{:S(2)}, u32[]{:S(2)}) %collective-permute-start.5) | collective-permute-done | bytes 524320 | tf_op jit(solution)/shard_map/ppermute | solution.py:311
  28.4 0.0 collective-permute-done.3.far
  28.4 6.7 %collective-permute-done.2.down = bf16[256,512]{1,0:T(8,128)(2,1)S(1)} collective-permute-done((bf16[256,512]{1,0:T(8,128)(2,1)}, bf16[256,512]{1,0:T(8,128)(2,1)S(1)}, u32[]{:S(2)}, u32[]{:S(2)}) %collective-permute-start.2) | collective-permute-done | bytes 262176 | tf_op jit(solution)/shard_map/ppermute | solution.py:320
  35.1 0.0 collective-permute-done.1.up
  35.1 0.1 broadcast_select_fusion
  35.2 0.1 pad_maximum_fusion
  35.2 2.4 %collective-permute-start.6 = (bf16[768,512]{1,0:T(8,128)(2,1)S(1)}, bf16[768,512]{1,0:T(8,128)(2,1)S(1)}, u32[]{:S(2)}, u32[]{:S(2)}) collective-permute-start(bf16[768,512]{1,0:T(8,128)(2,1)S(1)} %pad_maximum_fusion), channel_id=1, source_target_pairs={{0,4},{4,0},{8,12},{12,8},{16,20},{20,16},{24,28},{28,24},{32,36},... | collective-permute-start | bytes 2359304 | tf_op jit(solution)/shard_map/ppermute | solution.py:329
  37.6 0.0 copy-done.3
  37.6 5.3 %collective-permute-start = (bf16[128,2048]{1,0:T(8,128)(2,1)S(1)}, bf16[128,2048]{1,0:T(8,128)(2,1)S(1)}, u32[]{:S(2)}, u32[]{:S(2)}) collective-permute-start(bf16[128,2048]{1,0:T(8,128)(2,1)S(1)} %copy-done.3), channel_id=1, source_target_pairs={{0,2},{1,3},{2,0},{3,1},{4,6},{5,7},{6,4},{7,5},{8,10},{9,11},{10,... | collective-permute-start | bytes 1572872 | tf_op jit(solution)/shard_map/ppermute | solution.py:311
  42.9 0.0 collective-permute-done.6.mate
  42.9 41.0 %attention_first.1 = (bf16[512,2048]{1,0:T(8,128)(2,1)}, bf16[2,1024,256]{2,1,0:T(8,128)(2,1)S(1)}, bf16[2,2,144,1024]{3,2,1,0:T(8,128)(2,1)S(1)}) custom-call(s32[2]{0:T(128)S(1)} %pad_add_fusion.place_ref, s32[128,1]{1,0:T(8,128)S(1)} %get-tuple-element.20.starts_ref, bf16[512,512]{1,0:T(8,128)(2,1)S(1)} %bitcast.6, ...), custom_call_target="tpu_custom_call" | custom-call | tf_op jit(solution)/shard_map/attention_first/pallas_call | solution.py:266
  84.0 0.0 collective-permute-done.query
  84.0 14.0 %attention_last.1 = bf16[512,2048]{1,0:T(8,128)(2,1)} custom-call(s32[2]{0:T(128)S(1)} %pad_add_fusion.place_ref, s32[128,1]{1,0:T(8,128)S(1)} %get-tuple-element.20.starts_ref, bf16[128,2048]{1,0:T(8,128)(2,1)S(1)} %collective-permute-done.query, bf16[2,1024,256]{2,1,0:T(8,128)(2,1)S(1)} %get-tuple-element.30.keys, ...), custom_call_target="tpu_custom_call", output_to_operand_aliasing={{}: (5, {})} | custom-call | tf_op jit(solution)/shard_map/attention_last/pallas_call | solution.py:287
Async XLA Ops:
  0.0 11.4 %copy-start = (bf16[128,8192]{1,0:T(8,128)(2,1)S(1)}, bf16[128,8192]{1,0:T(8,128)(2,1)}, u32[]{:S(2)}) copy-start(bf16[128,8192]{1,0:T(8,128)(2,1)} %queries.1) | copy-start | bytes 6291460
  0.0 11.4 %copy-start.1 = (s32[128]{0:T(128)S(1)}, s32[128]{0:T(128)}, u32[]{:S(2)}) copy-start(s32[128]{0:T(128)} %param.7) | copy-start | bytes 1540
  2.0 17.1 %all-to-all-start = ((bf16[4,128,512]{2,1,0:T(8,128)(2,1)}), bf16[4,128,512]{2,1,0:T(8,128)(2,1)S(1)}, u32[]{:S(2)}, u32[]{:S(2)}) async-start(bf16[4,128,512]{2,1,0:T(8,128)(2,1)} %kv_pack.1), calls=%async_computation | async-start | bytes 1048576 | tf_op jit(solution)/shard_map/all_to_all | solution.py:307
  13.2 7.5 %copy-start.2 = (bf16[128,2048]{1,0:T(8,128)(2,1)}, bf16[128,2048]{1,0:T(8,128)(2,1)S(1)}, u32[]{:S(2)}) copy-start(bf16[128,2048]{1,0:T(8,128)(2,1)S(1)} %get-tuple-element.21) | copy-start | bytes 1572868
  13.3 13.6 %collective-permute-start.4 = (bf16[128,2048]{1,0:T(8,128)(2,1)}, bf16[128,2048]{1,0:T(8,128)(2,1)}, u32[]{:S(2)}, u32[]{:S(2)}) collective-permute-start(bf16[128,2048]{1,0:T(8,128)(2,1)} %get-tuple-element.23), channel_id=1, source_target_pairs={{0,1},{1,2},{2,3},{3,0},{4,5},{5,6},{6,7},{7,4},{8,9},{9,10},{10,1... | collective-permute-start | bytes 1572872 | tf_op jit(solution)/shard_map/ppermute | solution.py:311
  16.3 12.1 %collective-permute-start.5 = (bf16[128,2048]{1,0:T(8,128)(2,1)}, bf16[128,2048]{1,0:T(8,128)(2,1)}, u32[]{:S(2)}, u32[]{:S(2)}) collective-permute-start(bf16[128,2048]{1,0:T(8,128)(2,1)} %get-tuple-element.24), channel_id=1, source_target_pairs={{0,3},{1,0},{2,1},{3,2},{4,7},{5,4},{6,5},{7,6},{8,11},{9,8},{10,9... | collective-permute-start | bytes 1572872 | tf_op jit(solution)/shard_map/ppermute | solution.py:311
  20.1 8.3 %collective-permute-start.3 = (bf16[256,512]{1,0:T(8,128)(2,1)}, bf16[256,512]{1,0:T(8,128)(2,1)S(1)}, u32[]{:S(2)}, u32[]{:S(2)}) collective-permute-start(bf16[256,512]{1,0:T(8,128)(2,1)} %get-tuple-element.35), channel_id=1, source_target_pairs={{4,16},{12,24},{20,32},{28,40},{36,48},{44,56},{52,64},{60,72},{68... | collective-permute-start | bytes 786440 | tf_op jit(solution)/shard_map/ppermute | solution.py:324
  20.8 14.4 %collective-permute-start.2 = (bf16[256,512]{1,0:T(8,128)(2,1)}, bf16[256,512]{1,0:T(8,128)(2,1)S(1)}, u32[]{:S(2)}, u32[]{:S(2)}) collective-permute-start(bf16[256,512]{1,0:T(8,128)(2,1)} %get-tuple-element.36), channel_id=1, source_target_pairs={{8,0},{12,4},{16,8},{20,12},{24,16},{28,20},{32,24},{36,28},{40,32... | collective-permute-start | bytes 786440 | tf_op jit(solution)/shard_map/ppermute | solution.py:320
  22.1 13.1 %collective-permute-start.1 = (bf16[256,512]{1,0:T(8,128)(2,1)}, bf16[256,512]{1,0:T(8,128)(2,1)S(1)}, u32[]{:S(2)}, u32[]{:S(2)}) collective-permute-start(bf16[256,512]{1,0:T(8,128)(2,1)} %get-tuple-element.37), channel_id=1, source_target_pairs={{0,8},{4,12},{8,16},{12,20},{16,24},{20,28},{24,32},{28,36},{32,40... | collective-permute-start | bytes 786440 | tf_op jit(solution)/shard_map/ppermute | solution.py:319
  26.6 11.0 %copy-start.3 = (bf16[128,2048]{1,0:T(8,128)(2,1)S(1)}, bf16[128,2048]{1,0:T(8,128)(2,1)}, u32[]{:S(2)}) copy-start(bf16[128,2048]{1,0:T(8,128)(2,1)} %copy-done.2) | copy-start | bytes 1572868
  35.2 7.7 %collective-permute-start.6 = (bf16[768,512]{1,0:T(8,128)(2,1)S(1)}, bf16[768,512]{1,0:T(8,128)(2,1)S(1)}, u32[]{:S(2)}, u32[]{:S(2)}) collective-permute-start(bf16[768,512]{1,0:T(8,128)(2,1)S(1)} %pad_maximum_fusion), channel_id=1, source_target_pairs={{0,4},{4,0},{8,12},{12,8},{16,20},{20,16},{24,28},{28,24},{32,36},... | collective-permute-start | bytes 2359304 | tf_op jit(solution)/shard_map/ppermute | solution.py:329
  37.6 46.3 %collective-permute-start = (bf16[128,2048]{1,0:T(8,128)(2,1)S(1)}, bf16[128,2048]{1,0:T(8,128)(2,1)S(1)}, u32[]{:S(2)}, u32[]{:S(2)}) collective-permute-start(bf16[128,2048]{1,0:T(8,128)(2,1)S(1)} %copy-done.3), channel_id=1, source_target_pairs={{0,2},{1,3},{2,0},{3,1},{4,6},{5,7},{6,4},{7,5},{8,10},{9,11},{10,... | collective-permute-start | bytes 1572872 | tf_op jit(solution)/shard_map/ppermute | solution.py:311

commit v5 on v4

--- a/solution.py
+++ b/solution.py
@@ -98,7 +98,7 @@
     )(place, lengths, queries)
 
 
-def load_windows(ctx, count, own, up, down, far, mate, keys, values, sems):
+def load_windows(ctx, count, own, up, down, far, inner, mate_up, mate_down, keys, values, sems):
     odd = lax.rem(ctx, 2) == 1
     even = jnp.logical_not(odd)
     last = ctx == count - 1
@@ -124,19 +124,19 @@
             piece(kind, own, lane * STRETCH, lane, 3).start()
     for kind in range(2):
         piece(kind, up, 0, 0, 1).start()
-    start(odd, mate, 0, 0, 0)
+    start(odd, mate_up, 0, 0, 0)
     start(even, far, 0, 0, 0)
-    start(odd, mate, 2 * STRETCH, 0, 2)
-    start(even, mate, 0, 0, 2)
-    start(jnp.logical_and(even, plain), mate, STRETCH, 1, 0)
+    start(odd, inner, 0, 0, 2)
+    start(even, mate_up, 0, 0, 2)
+    start(jnp.logical_and(even, plain), mate_down, 0, 1, 0)
     start(jnp.logical_and(odd, plain), far, 0, 1, 0)
     start(before_last, own, 0, 1, 0)
     start(last, up, 0, 1, 0)
     start(plain, down, 0, 1, 1)
-    start(before_last, mate, STRETCH, 1, 1)
-    start(last, mate, 2 * STRETCH, 1, 1)
-    start(even, mate, 2 * STRETCH, 1, 2)
-    start(jnp.logical_and(odd, plain), mate, STRETCH, 1, 2)
+    start(before_last, mate_down, 0, 1, 1)
+    start(last, inner, 0, 1, 1)
+    start(even, inner, 0, 1, 2)
+    start(jnp.logical_and(odd, plain), mate_down, 0, 1, 2)
     start(last, own, 0, 1, 2)
 
     def wait(kind, lane):
@@ -197,12 +197,12 @@
 
 
 def first_kernel(
-    count, place_ref, starts_ref, own, up, down, far, mate, queries, left, right,
+    count, place_ref, starts_ref, own, up, down, far, inner, mate_up, mate_down, queries, left, right,
     out_ref, keys, values_t, values, query, result, bias, sems, load_sems, store_sems,
 ):
     ctx, head = place_ref[0], place_ref[1]
     width = query.shape[2]
-    wait = load_windows(ctx, count, own, up, down, far, mate, keys, values, sems)
+    wait = load_windows(ctx, count, own, up, down, far, inner, mate_up, mate_down, keys, values, sems)
     own_cols = pl.ds(pl.multiple_of(head * width, width), width)
     sources = (queries.at[:, own_cols], left, right)
     loads = [
@@ -256,7 +256,7 @@
     copy.wait()
 
 
-def attention(count, place, starts, own, up, down, far, mate, queries, left, right, across):
+def attention(count, place, starts, own, up, down, far, inner, mate_up, mate_down, queries, left, right, across):
     rows, width = left.shape
     kv_width = own.shape[1] // 2
     kv_local = kv_width // HEAD_DIM
@@ -265,7 +265,7 @@
     bias = pltpu.VMEM((KEYS, ROWS), jnp.float32)
     partial, keys, values_t = pl.pallas_call(
         functools.partial(first_kernel, count),
-        in_specs=[SMEM_SPEC, VMEM_SPEC] + [VMEM_SPEC] * 5 + [ANY_SPEC] * 3,
+        in_specs=[SMEM_SPEC, VMEM_SPEC] + [VMEM_SPEC] * 7 + [ANY_SPEC] * 3,
         out_specs=[ANY_SPEC, VMEM_SPEC, VMEM_SPEC],
         out_shape=[
             out_shape,
@@ -283,7 +283,7 @@
         ],
         compiler_params=PARAMS,
         name="attention_first",
-    )(place, starts, own, up, down, far, mate, queries, left, right)
+    )(place, starts, own, up, down, far, inner, mate_up, mate_down, queries, left, right)
     return pl.pallas_call(
         functools.partial(last_kernel, count),
         in_specs=[SMEM_SPEC] + [VMEM_SPEC] * 4 + [ANY_SPEC],
@@ -316,19 +316,21 @@
     across = rotate(to_opposite, 2)
 
     lane0, lane1 = kv[:STRETCH], kv[STRETCH:]
+    last = ctx == count - 1
     up = lax.ppermute(lane0, "ctx", [(i, i + 2) for i in range(count - 2)])
     down = lax.ppermute(lane1, "ctx", [(i + 2, i) for i in range(count - 2)])
-    route = [(i, i + 3) for i in range(1, count - 3, 2)]
-    route += [(i + 3, i) for i in range(1, count - 3, 2)]
+    swap = [(i, i ^ 1) for i in range(count)]
+    inner = lax.ppermute(jnp.where(odd, lane1, lane0), "ctx", swap)
+    up, down, inner, left, right = lax.optimization_barrier((up, down, inner, left, right))
+    above = jnp.where(last, lane0, down)
+    mate_up = lax.ppermute(up, "ctx", swap)
+    mate_down = lax.ppermute(above, "ctx", swap)
+    route = [(i, i + 1) for i in range(1, count - 1, 2)]
+    route += [(i, i - 1) for i in range(2, count - 2, 2)]
     route += [(count - 1, count - 3)]
-    far = lax.ppermute(jnp.where(odd, lane0, lane1), "ctx", route)
-    up, down, far, left, right = lax.optimization_barrier((up, down, far, left, right))
-    passed = jnp.concatenate(
-        [up, jnp.where(ctx == count - 1, lane0, down), jnp.where(odd, lane1, lane0)], axis=0
-    )
-    mate = lax.ppermute(passed, "ctx", [(i, i ^ 1) for i in range(count)])
+    far = lax.ppermute(jnp.where(odd, jnp.where(last, lane0, up), above), "ctx", route)
     return attention(
-        count, place, starts, kv, up, down, far, mate, queries, left, right, across
+        count, place, starts, kv, up, down, far, inner, mate_up, mate_down, queries, left, right, across
     )
 
 

time: 98.3 us -> 102 us (1.038)
  the two profiles are of different devices: /device:TPU:4 before, /device:TPU:33 now
where the time goes in v5:
time: 102 us; the launch traced here: 101 us
  Pallas kernels  48.8 us (48%)
  starting transfers between devices  37.2 us (36%)
  waiting for transfers between devices  14.2 us (14%)
  other arithmetic  1.06 us (1%)
    pallas_call x1, Pallas kernels, attention(): pl.pallas_call(functools.partial(first_kernel, count), in_specs=[SMEM_SPE...  41 us
    ppermute x1, starting transfers between devices, body(): down = lax.ppermute(lane1, 'ctx', [(i + 2, i) for i in range(count - 2)])  10.6 us
    ppermute x3, starting transfers between devices, rotate(): lax.ppermute(block, 'head', [(i, (i + shift) % HEADS) for i in range(HEAD...  9.09 us
    ppermute x1, waiting for transfers between devices, body(): up = lax.ppermute(lane0, 'ctx', [(i, i + 2) for i in range(count - 2)])  7.01 us
    ppermute x1, waiting for transfers between devices, body(): lax.ppermute(jnp.where(odd, jnp.where(last, lane0, up), above), 'ctx', ro...  5.74 us
    ppermute x1, starting transfers between devices, body(): inner = lax.ppermute(jnp.where(odd, lane1, lane0), 'ctx', swap)  4.77 us
    all_to_all x1, starting transfers between devices, body(): kv = lax.all_to_all(packed, 'head', split_axis=0, concat_axis=0, tiled=True)  4.02 us
    pallas_call x1, Pallas kernels, attention(): pl.pallas_call(functools.partial(last_kernel, count), in_specs=[SMEM_SPEC...  3.98 us
  transfers between devices with their start and end apart: 10, of which 3 were waited for; matrix products, arithmetic and copies ran while one was open for 1% of the time, Pallas kernels for 42%

profile of v5, /device:TPU:33, one launch (start us, length us, event | category | flops | bytes accessed | tf_op | source)
XLA Modules:
  0.0 101.5 jit_solution(6991111953411526387)
XLA Ops:
  0.0 0.0 copy-start
  0.0 2.0 %kv_pack.1 = bf16[4,128,512]{2,1,0:T(8,128)(2,1)} custom-call(bf16[128,1024]{1,0:T(8,128)(2,1)} %key_ref.1, bf16[128,1024]{1,0:T(8,128)(2,1)} %value_ref.1), custom_call_target="tpu_custom_call" | custom-call | tf_op jit(solution)/shard_map/kv_pack/pallas_call | solution.py:53
  2.0 4.0 %all-to-all-start = ((bf16[4,128,512]{2,1,0:T(8,128)(2,1)}), bf16[4,128,512]{2,1,0:T(8,128)(2,1)S(1)}, u32[]{:S(2)}, u32[]{:S(2)}) async-start(bf16[4,128,512]{2,1,0:T(8,128)(2,1)} %kv_pack.1), calls=%async_computation | async-start | bytes 1048576 | tf_op jit(solution)/shard_map/all_to_all | solution.py:307
  6.0 0.1 pad_add_fusion.place_ref
  6.1 0.0 copy-done
  6.1 0.0 copy-done.1
  6.1 1.8 %query_pack.1 = (bf16[128,2048]{1,0:T(8,128)(2,1)}, bf16[128,2048]{1,0:T(8,128)(2,1)}, bf16[128,2048]{1,0:T(8,128)(2,1)S(1)}, s32[128,1]{1,0:T(8,128)S(1)}) custom-call(s32[2]{0:T(128)S(1)} %pad_add_fusion.place_ref, s32[1,128]{1,0:T(1,128)S(1)} %bitcast.7, bf16[128,8192]{1,0:T(8,128)(2,1)S(1)} %copy-done), custom_call_target="tpu_custom_call" | custom-call | tf_op jit(solution)/shard_map/query_pack/pallas_call | solution.py:90
  7.9 0.0 copy-start.2
  7.9 3.4 %collective-permute-start.4 = (bf16[128,2048]{1,0:T(8,128)(2,1)}, bf16[128,2048]{1,0:T(8,128)(2,1)}, u32[]{:S(2)}, u32[]{:S(2)}) collective-permute-start(bf16[128,2048]{1,0:T(8,128)(2,1)} %get-tuple-element.23), channel_id=1, source_target_pairs={{0,1},{1,2},{2,3},{3,0},{4,5},{5,6},{6,7},{7,4},{8,9},{9,10},{10,1... | collective-permute-start | bytes 1572872 | tf_op jit(solution)/shard_map/ppermute | solution.py:311
  11.3 3.1 %collective-permute-start.5 = (bf16[128,2048]{1,0:T(8,128)(2,1)}, bf16[128,2048]{1,0:T(8,128)(2,1)}, u32[]{:S(2)}, u32[]{:S(2)}) collective-permute-start(bf16[128,2048]{1,0:T(8,128)(2,1)} %get-tuple-element.24), channel_id=1, source_target_pairs={{0,3},{1,0},{2,1},{3,2},{4,7},{5,4},{6,5},{7,6},{8,11},{9,8},{10,9... | collective-permute-start | bytes 1572872 | tf_op jit(solution)/shard_map/ppermute | solution.py:311
  14.5 0.0 all-to-all-done
  14.5 0.9 broadcast_select_fusion.1
  15.4 4.8 %collective-permute-start.3 = (bf16[256,512]{1,0:T(8,128)(2,1)}, bf16[256,512]{1,0:T(8,128)(2,1)S(1)}, u32[]{:S(2)}, u32[]{:S(2)}) collective-permute-start(bf16[256,512]{1,0:T(8,128)(2,1)} %get-tuple-element.35), channel_id=1, source_target_pairs={{0,4},{4,0},{8,12},{12,8},{16,20},{20,16},{24,28},{28,24},{32,36},... | collective-permute-start | bytes 786440 | tf_op jit(solution)/shard_map/ppermute | solution.py:323
  20.2 0.0 copy-done.2
  20.2 10.6 %collective-permute-start.2 = (bf16[256,512]{1,0:T(8,128)(2,1)}, bf16[256,512]{1,0:T(8,128)(2,1)S(1)}, u32[]{:S(2)}, u32[]{:S(2)}) collective-permute-start(bf16[256,512]{1,0:T(8,128)(2,1)} %get-tuple-element.36), channel_id=1, source_target_pairs={{8,0},{12,4},{16,8},{20,12},{24,16},{28,20},{32,24},{36,28},{40,32... | collective-permute-start | bytes 786440 | tf_op jit(solution)/shard_map/ppermute | solution.py:321
  30.7 1.9 %collective-permute-start.1 = (bf16[256,512]{1,0:T(8,128)(2,1)}, bf16[256,512]{1,0:T(8,128)(2,1)S(1)}, u32[]{:S(2)}, u32[]{:S(2)}) collective-permute-start(bf16[256,512]{1,0:T(8,128)(2,1)} %get-tuple-element.37), channel_id=1, source_target_pairs={{0,8},{4,12},{8,16},{12,20},{16,24},{20,28},{24,32},{28,36},{32,40... | collective-permute-start | bytes 786440 | tf_op jit(solution)/shard_map/ppermute | solution.py:320
  32.7 0.0 collective-permute-done.4.left
  32.7 2.6 %collective-permute-start = (bf16[128,2048]{1,0:T(8,128)(2,1)}, bf16[128,2048]{1,0:T(8,128)(2,1)}, u32[]{:S(2)}, u32[]{:S(2)}) collective-permute-start(bf16[128,2048]{1,0:T(8,128)(2,1)} %copy-done.2), channel_id=1, source_target_pairs={{0,2},{1,3},{2,0},{3,1},{4,6},{5,7},{6,4},{7,5},{8,10},{9,11},{10,... | collective-permute-start | bytes 1572872 | tf_op jit(solution)/shard_map/ppermute | solution.py:311
  35.3 0.0 collective-permute-done.5.right
  35.3 0.0 collective-permute-done.3.inner
  35.3 1.5 %collective-permute-done.2.down = bf16[256,512]{1,0:T(8,128)(2,1)S(1)} collective-permute-done((bf16[256,512]{1,0:T(8,128)(2,1)}, bf16[256,512]{1,0:T(8,128)(2,1)S(1)}, u32[]{:S(2)}, u32[]{:S(2)}) %collective-permute-start.2) | collective-permute-done | bytes 262176 | tf_op jit(solution)/shard_map/ppermute | solution.py:321
  36.7 7.0 %collective-permute-done.1.up = bf16[256,512]{1,0:T(8,128)(2,1)S(1)} collective-permute-done((bf16[256,512]{1,0:T(8,128)(2,1)}, bf16[256,512]{1,0:T(8,128)(2,1)S(1)}, u32[]{:S(2)}, u32[]{:S(2)}) %collective-permute-start.1) | collective-permute-done | bytes 262176 | tf_op jit(solution)/shard_map/ppermute | solution.py:320
  43.8 3.0 %collective-permute-start.7 = (bf16[256,512]{1,0:T(8,128)(2,1)S(1)}, bf16[256,512]{1,0:T(8,128)(2,1)S(1)}, u32[]{:S(2)}, u32[]{:S(2)}) collective-permute-start(bf16[256,512]{1,0:T(8,128)(2,1)S(1)} %collective-permute-done.1.up), channel_id=1, source_target_pairs={{0,4},{4,0},{8,12},{12,8},{16,20},{20,16},{24,28},{28,24},{32,36},... | collective-permute-start | bytes 786440 | tf_op jit(solution)/shard_map/ppermute | solution.py:326
  46.8 0.1 broadcast_select_fusion
  46.9 1.9 %collective-permute-start.8 = (bf16[256,512]{1,0:T(8,128)(2,1)S(1)}, bf16[256,512]{1,0:T(8,128)(2,1)S(1)}, u32[]{:S(2)}, u32[]{:S(2)}) collective-permute-start(bf16[256,512]{1,0:T(8,128)(2,1)S(1)} %get-tuple-element.33), channel_id=1, source_target_pairs={{0,4},{4,0},{8,12},{12,8},{16,20},{20,16},{24,28},{28,24},{32,36},... | collective-permute-start | bytes 786440 | tf_op jit(solution)/shard_map/ppermute | solution.py:327
  48.8 1.9 %collective-permute-start.6 = (bf16[256,512]{1,0:T(8,128)(2,1)S(1)}, bf16[256,512]{1,0:T(8,128)(2,1)S(1)}, u32[]{:S(2)}, u32[]{:S(2)}) collective-permute-start(bf16[256,512]{1,0:T(8,128)(2,1)S(1)} %get-tuple-element.34), channel_id=1, source_target_pairs={{4,8},{12,16},{20,24},{28,32},{36,40},{44,48},{52,56},{60,64},{68,... | collective-permute-start | bytes 786440 | tf_op jit(solution)/shard_map/ppermute | solution.py:331
  50.7 0.0 collective-permute-done.7.mate_up
  50.7 0.0 collective-permute-done.8.mate_down
  50.7 5.7 %collective-permute-done.6.far = bf16[256,512]{1,0:T(8,128)(2,1)S(1)} collective-permute-done((bf16[256,512]{1,0:T(8,128)(2,1)S(1)}, bf16[256,512]{1,0:T(8,128)(2,1)S(1)}, u32[]{:S(2)}, u32[]{:S(2)}) %collective-permute-start.6) | collective-permute-done | bytes 262176 | tf_op jit(solution)/shard_map/ppermute | solution.py:331
  56.5 41.0 %attention_first.1 = (bf16[512,2048]{1,0:T(8,128)(2,1)}, bf16[2,1024,256]{2,1,0:T(8,128)(2,1)S(1)}, bf16[2,2,144,1024]{3,2,1,0:T(8,128)(2,1)S(1)}) custom-call(s32[2]{0:T(128)S(1)} %pad_add_fusion.place_ref, s32[128,1]{1,0:T(8,128)S(1)} %get-tuple-element.20.starts_ref, bf16[512,512]{1,0:T(8,128)(2,1)S(1)} %bitcast.6, ...), custom_call_target="tpu_custom_call" | custom-call | tf_op jit(solution)/shard_map/attention_first/pallas_call | solution.py:266
  97.5 0.0 collective-permute-done.query
  97.5 4.0 %attention_last.1 = bf16[512,2048]{1,0:T(8,128)(2,1)} custom-call(s32[2]{0:T(128)S(1)} %pad_add_fusion.place_ref, s32[128,1]{1,0:T(8,128)S(1)} %get-tuple-element.20.starts_ref, bf16[128,2048]{1,0:T(8,128)(2,1)} %collective-permute-done.query, bf16[2,1024,256]{2,1,0:T(8,128)(2,1)S(1)} %get-tuple-element.30.keys, ...), custom_call_target="tpu_custom_call", output_to_operand_aliasing={{}: (5, {})} | custom-call | tf_op jit(solution)/shard_map/attention_last/pallas_call | solution.py:287
  (1 shorter events, 0.0 us)
Async XLA Ops:
  0.0 6.1 %copy-start = (bf16[128,8192]{1,0:T(8,128)(2,1)S(1)}, bf16[128,8192]{1,0:T(8,128)(2,1)}, u32[]{:S(2)}) copy-start(bf16[128,8192]{1,0:T(8,128)(2,1)} %queries.1) | copy-start | bytes 6291460
  0.0 6.1 %copy-start.1 = (s32[128]{0:T(128)S(1)}, s32[128]{0:T(128)}, u32[]{:S(2)}) copy-start(s32[128]{0:T(128)} %param.7) | copy-start | bytes 1540
  2.0 12.4 %all-to-all-start = ((bf16[4,128,512]{2,1,0:T(8,128)(2,1)}), bf16[4,128,512]{2,1,0:T(8,128)(2,1)S(1)}, u32[]{:S(2)}, u32[]{:S(2)}) async-start(bf16[4,128,512]{2,1,0:T(8,128)(2,1)} %kv_pack.1), calls=%async_computation | async-start | bytes 1048576 | tf_op jit(solution)/shard_map/all_to_all | solution.py:307
  7.9 12.2 %copy-start.2 = (bf16[128,2048]{1,0:T(8,128)(2,1)}, bf16[128,2048]{1,0:T(8,128)(2,1)S(1)}, u32[]{:S(2)}) copy-start(bf16[128,2048]{1,0:T(8,128)(2,1)S(1)} %get-tuple-element.21) | copy-start | bytes 1572868
  7.9 24.7 %collective-permute-start.4 = (bf16[128,2048]{1,0:T(8,128)(2,1)}, bf16[128,2048]{1,0:T(8,128)(2,1)}, u32[]{:S(2)}, u32[]{:S(2)}) collective-permute-start(bf16[128,2048]{1,0:T(8,128)(2,1)} %get-tuple-element.23), channel_id=1, source_target_pairs={{0,1},{1,2},{2,3},{3,0},{4,5},{5,6},{6,7},{7,4},{8,9},{9,10},{10,1... | collective-permute-start | bytes 1572872 | tf_op jit(solution)/shard_map/ppermute | solution.py:311
  11.3 23.9 %collective-permute-start.5 = (bf16[128,2048]{1,0:T(8,128)(2,1)}, bf16[128,2048]{1,0:T(8,128)(2,1)}, u32[]{:S(2)}, u32[]{:S(2)}) collective-permute-start(bf16[128,2048]{1,0:T(8,128)(2,1)} %get-tuple-element.24), channel_id=1, source_target_pairs={{0,3},{1,0},{2,1},{3,2},{4,7},{5,4},{6,5},{7,6},{8,11},{9,8},{10,9... | collective-permute-start | bytes 1572872 | tf_op jit(solution)/shard_map/ppermute | solution.py:311
  15.4 19.9 %collective-permute-start.3 = (bf16[256,512]{1,0:T(8,128)(2,1)}, bf16[256,512]{1,0:T(8,128)(2,1)S(1)}, u32[]{:S(2)}, u32[]{:S(2)}) collective-permute-start(bf16[256,512]{1,0:T(8,128)(2,1)} %get-tuple-element.35), channel_id=1, source_target_pairs={{0,4},{4,0},{8,12},{12,8},{16,20},{20,16},{24,28},{28,24},{32,36},... | collective-permute-start | bytes 786440 | tf_op jit(solution)/shard_map/ppermute | solution.py:323
  20.2 16.6 %collective-permute-start.2 = (bf16[256,512]{1,0:T(8,128)(2,1)}, bf16[256,512]{1,0:T(8,128)(2,1)S(1)}, u32[]{:S(2)}, u32[]{:S(2)}) collective-permute-start(bf16[256,512]{1,0:T(8,128)(2,1)} %get-tuple-element.36), channel_id=1, source_target_pairs={{8,0},{12,4},{16,8},{20,12},{24,16},{28,20},{32,24},{36,28},{40,32... | collective-permute-start | bytes 786440 | tf_op jit(solution)/shard_map/ppermute | solution.py:321
  30.7 13.0 %collective-permute-start.1 = (bf16[256,512]{1,0:T(8,128)(2,1)}, bf16[256,512]{1,0:T(8,128)(2,1)S(1)}, u32[]{:S(2)}, u32[]{:S(2)}) collective-permute-start(bf16[256,512]{1,0:T(8,128)(2,1)} %get-tuple-element.37), channel_id=1, source_target_pairs={{0,8},{4,12},{8,16},{12,20},{16,24},{20,28},{24,32},{28,36},{32,40... | collective-permute-start | bytes 786440 | tf_op jit(solution)/shard_map/ppermute | solution.py:320
  32.7 64.8 %collective-permute-start = (bf16[128,2048]{1,0:T(8,128)(2,1)}, bf16[128,2048]{1,0:T(8,128)(2,1)}, u32[]{:S(2)}, u32[]{:S(2)}) collective-permute-start(bf16[128,2048]{1,0:T(8,128)(2,1)} %copy-done.2), channel_id=1, source_target_pairs={{0,2},{1,3},{2,0},{3,1},{4,6},{5,7},{6,4},{7,5},{8,10},{9,11},{10,... | collective-permute-start | bytes 1572872 | tf_op jit(solution)/shard_map/ppermute | solution.py:311
  43.8 7.0 %collective-permute-start.7 = (bf16[256,512]{1,0:T(8,128)(2,1)S(1)}, bf16[256,512]{1,0:T(8,128)(2,1)S(1)}, u32[]{:S(2)}, u32[]{:S(2)}) collective-permute-start(bf16[256,512]{1,0:T(8,128)(2,1)S(1)} %collective-permute-done.1.up), channel_id=1, source_target_pairs={{0,4},{4,0},{8,12},{12,8},{16,20},{20,16},{24,28},{28,24},{32,36},... | collective-permute-start | bytes 786440 | tf_op jit(solution)/shard_map/ppermute | solution.py:326
  46.9 3.9 %collective-permute-start.8 = (bf16[256,512]{1,0:T(8,128)(2,1)S(1)}, bf16[256,512]{1,0:T(8,128)(2,1)S(1)}, u32[]{:S(2)}, u32[]{:S(2)}) collective-permute-start(bf16[256,512]{1,0:T(8,128)(2,1)S(1)} %get-tuple-element.33), channel_id=1, source_target_pairs={{0,4},{4,0},{8,12},{12,8},{16,20},{20,16},{24,28},{28,24},{32,36},... | collective-permute-start | bytes 786440 | tf_op jit(solution)/shard_map/ppermute | solution.py:327
  48.8 7.7 %collective-permute-start.6 = (bf16[256,512]{1,0:T(8,128)(2,1)S(1)}, bf16[256,512]{1,0:T(8,128)(2,1)S(1)}, u32[]{:S(2)}, u32[]{:S(2)}) collective-permute-start(bf16[256,512]{1,0:T(8,128)(2,1)S(1)} %get-tuple-element.34), channel_id=1, source_target_pairs={{4,8},{12,16},{20,24},{28,32},{36,40},{44,48},{52,56},{60,64},{68,... | collective-permute-start | bytes 786440 | tf_op jit(solution)/shard_map/ppermute | solution.py:331

commit v6 on v5

--- a/solution.py
+++ b/solution.py
@@ -321,7 +321,7 @@
     down = lax.ppermute(lane1, "ctx", [(i + 2, i) for i in range(count - 2)])
     swap = [(i, i ^ 1) for i in range(count)]
     inner = lax.ppermute(jnp.where(odd, lane1, lane0), "ctx", swap)
-    up, down, inner, left, right = lax.optimization_barrier((up, down, inner, left, right))
+    down, up, inner, left, right = lax.optimization_barrier((down, up, inner, left, right))
     above = jnp.where(last, lane0, down)
     mate_up = lax.ppermute(up, "ctx", swap)
     mate_down = lax.ppermute(above, "ctx", swap)

time: 102 us -> 102 us (level)
  the two profiles are of different devices: /device:TPU:33 before, /device:TPU:408 now
where the time goes in v6:
time: 102 us; the launch traced here: 101 us
  Pallas kernels  59.3 us (58%)
  starting transfers between devices  28.3 us (28%)
  waiting for transfers between devices  12.3 us (12%)
  other arithmetic  1.08 us (1%)
    pallas_call x1, Pallas kernels, attention(): pl.pallas_call(functools.partial(first_kernel, count), in_specs=[SMEM_SPE...  41 us
    pallas_call x1, Pallas kernels, attention(): pl.pallas_call(functools.partial(last_kernel, count), in_specs=[SMEM_SPEC...  14.5 us
    ppermute x3, starting transfers between devices, rotate(): lax.ppermute(block, 'head', [(i, (i + shift) % HEADS) for i in range(HEAD...  9.81 us
    ppermute x1, waiting for transfers between devices, body(): lax.ppermute(jnp.where(odd, jnp.where(last, lane0, up), above), 'ctx', ro...  5.58 us
    all_to_all x1, starting transfers between devices, body(): kv = lax.all_to_all(packed, 'head', split_axis=0, concat_axis=0, tiled=True)  4.3 us
    ppermute x1, starting transfers between devices, body(): up = lax.ppermute(lane0, 'ctx', [(i, i + 2) for i in range(count - 2)])  3.38 us
    ppermute x1, waiting for transfers between devices, body(): down = lax.ppermute(lane1, 'ctx', [(i + 2, i) for i in range(count - 2)])  3.11 us
    ppermute x1, starting transfers between devices, body(): down = lax.ppermute(lane1, 'ctx', [(i + 2, i) for i in range(count - 2)])  2.46 us
  transfers between devices with their start and end apart: 10, of which 5 were waited for; matrix products, arithmetic and copies ran while one was open for 1% of the time, Pallas kernels for 42%

profile of v6, /device:TPU:408, one launch (start us, length us, event | category | flops | bytes accessed | tf_op | source)
XLA Modules:
  0.0 101.1 jit_solution(8260684030726603890)
XLA Ops:
  0.0 0.0 copy-start
  0.0 2.0 %kv_pack.1 = bf16[4,128,512]{2,1,0:T(8,128)(2,1)} custom-call(bf16[128,1024]{1,0:T(8,128)(2,1)} %key_ref.1, bf16[128,1024]{1,0:T(8,128)(2,1)} %value_ref.1), custom_call_target="tpu_custom_call" | custom-call | tf_op jit(solution)/shard_map/kv_pack/pallas_call | solution.py:53
  2.0 4.3 %all-to-all-start = ((bf16[4,128,512]{2,1,0:T(8,128)(2,1)}), bf16[4,128,512]{2,1,0:T(8,128)(2,1)S(1)}, u32[]{:S(2)}, u32[]{:S(2)}) async-start(bf16[4,128,512]{2,1,0:T(8,128)(2,1)} %kv_pack.1), calls=%async_computation | async-start | bytes 1048576 | tf_op jit(solution)/shard_map/all_to_all | solution.py:307
  6.3 0.1 pad_add_fusion.place_ref
  6.4 0.0 copy-done
  6.4 0.0 copy-done.1
  6.4 1.8 %query_pack.1 = (bf16[128,2048]{1,0:T(8,128)(2,1)}, bf16[128,2048]{1,0:T(8,128)(2,1)}, bf16[128,2048]{1,0:T(8,128)(2,1)S(1)}, s32[128,1]{1,0:T(8,128)S(1)}) custom-call(s32[2]{0:T(128)S(1)} %pad_add_fusion.place_ref, s32[1,128]{1,0:T(1,128)S(1)} %bitcast.7, bf16[128,8192]{1,0:T(8,128)(2,1)S(1)} %copy-done), custom_call_target="tpu_custom_call" | custom-call | tf_op jit(solution)/shard_map/query_pack/pallas_call | solution.py:90
  8.2 0.0 copy-start.2
  8.2 3.9 %collective-permute-start.4 = (bf16[128,2048]{1,0:T(8,128)(2,1)}, bf16[128,2048]{1,0:T(8,128)(2,1)}, u32[]{:S(2)}, u32[]{:S(2)}) collective-permute-start(bf16[128,2048]{1,0:T(8,128)(2,1)} %get-tuple-element.23), channel_id=1, source_target_pairs={{0,1},{1,2},{2,3},{3,0},{4,5},{5,6},{6,7},{7,4},{8,9},{9,10},{10,1... | collective-permute-start | bytes 1572872 | tf_op jit(solution)/shard_map/ppermute | solution.py:311
  12.2 3.1 %collective-permute-start.5 = (bf16[128,2048]{1,0:T(8,128)(2,1)}, bf16[128,2048]{1,0:T(8,128)(2,1)}, u32[]{:S(2)}, u32[]{:S(2)}) collective-permute-start(bf16[128,2048]{1,0:T(8,128)(2,1)} %get-tuple-element.24), channel_id=1, source_target_pairs={{0,3},{1,0},{2,1},{3,2},{4,7},{5,4},{6,5},{7,6},{8,11},{9,8},{10,9... | collective-permute-start | bytes 1572872 | tf_op jit(solution)/shard_map/ppermute | solution.py:311
  15.3 1.4 %all-to-all-done = bf16[4,128,512]{2,1,0:T(8,128)(2,1)S(1)} async-done(((bf16[4,128,512]{2,1,0:T(8,128)(2,1)}), bf16[4,128,512]{2,1,0:T(8,128)(2,1)S(1)}, u32[]{:S(2)}, u32[]{:S(2)}) %all-to-all-start) | async-done | bytes 524320 | tf_op jit(solution)/shard_map/all_to_all | solution.py:307
  16.7 0.9 broadcast_select_fusion.1
  17.6 1.9 %collective-permute-start.3 = (bf16[256,512]{1,0:T(8,128)(2,1)}, bf16[256,512]{1,0:T(8,128)(2,1)S(1)}, u32[]{:S(2)}, u32[]{:S(2)}) collective-permute-start(bf16[256,512]{1,0:T(8,128)(2,1)} %get-tuple-element.35), channel_id=1, source_target_pairs={{0,4},{4,0},{8,12},{12,8},{16,20},{20,16},{24,28},{28,24},{32,36},... | collective-permute-start | bytes 786440 | tf_op jit(solution)/shard_map/ppermute | solution.py:323
  19.5 0.0 copy-done.2
  19.5 3.4 %collective-permute-start.2 = (bf16[256,512]{1,0:T(8,128)(2,1)}, bf16[256,512]{1,0:T(8,128)(2,1)S(1)}, u32[]{:S(2)}, u32[]{:S(2)}) collective-permute-start(bf16[256,512]{1,0:T(8,128)(2,1)} %get-tuple-element.36), channel_id=1, source_target_pairs={{0,8},{4,12},{8,16},{12,20},{16,24},{20,28},{24,32},{28,36},{32,40... | collective-permute-start | bytes 786440 | tf_op jit(solution)/shard_map/ppermute | solution.py:320
  22.9 2.5 %collective-permute-start.1 = (bf16[256,512]{1,0:T(8,128)(2,1)}, bf16[256,512]{1,0:T(8,128)(2,1)S(1)}, u32[]{:S(2)}, u32[]{:S(2)}) collective-permute-start(bf16[256,512]{1,0:T(8,128)(2,1)} %get-tuple-element.37), channel_id=1, source_target_pairs={{8,0},{12,4},{16,8},{20,12},{24,16},{28,20},{32,24},{36,28},{40,32... | collective-permute-start | bytes 786440 | tf_op jit(solution)/shard_map/ppermute | solution.py:321
  25.4 1.5 %collective-permute-done.4.left = bf16[128,2048]{1,0:T(8,128)(2,1)} collective-permute-done((bf16[128,2048]{1,0:T(8,128)(2,1)}, bf16[128,2048]{1,0:T(8,128)(2,1)}, u32[]{:S(2)}, u32[]{:S(2)}) %collective-permute-start.4) | collective-permute-done | bytes 524320 | tf_op jit(solution)/shard_map/ppermute | solution.py:311
  26.9 2.7 %collective-permute-start = (bf16[128,2048]{1,0:T(8,128)(2,1)}, bf16[128,2048]{1,0:T(8,128)(2,1)}, u32[]{:S(2)}, u32[]{:S(2)}) collective-permute-start(bf16[128,2048]{1,0:T(8,128)(2,1)} %copy-done.2), channel_id=1, source_target_pairs={{0,2},{1,3},{2,0},{3,1},{4,6},{5,7},{6,4},{7,5},{8,10},{9,11},{10,... | collective-permute-start | bytes 1572872 | tf_op jit(solution)/shard_map/ppermute | solution.py:311
  29.6 0.0 collective-permute-done.5.right
  29.6 0.0 collective-permute-done.3.inner
  29.6 0.7 collective-permute-done.2.up
  30.3 3.1 %collective-permute-done.1.down = bf16[256,512]{1,0:T(8,128)(2,1)S(1)} collective-permute-done((bf16[256,512]{1,0:T(8,128)(2,1)}, bf16[256,512]{1,0:T(8,128)(2,1)S(1)}, u32[]{:S(2)}, u32[]{:S(2)}) %collective-permute-start.1) | collective-permute-done | bytes 262176 | tf_op jit(solution)/shard_map/ppermute | solution.py:321
  33.4 1.9 %collective-permute-start.7 = (bf16[256,512]{1,0:T(8,128)(2,1)S(1)}, bf16[256,512]{1,0:T(8,128)(2,1)S(1)}, u32[]{:S(2)}, u32[]{:S(2)}) collective-permute-start(bf16[256,512]{1,0:T(8,128)(2,1)S(1)} %collective-permute-done.2.up), channel_id=1, source_target_pairs={{0,4},{4,0},{8,12},{12,8},{16,20},{20,16},{24,28},{28,24},{32,36},... | collective-permute-start | bytes 786440 | tf_op jit(solution)/shard_map/ppermute | solution.py:326
  35.4 0.1 broadcast_select_fusion
  35.4 2.4 %collective-permute-start.8 = (bf16[256,512]{1,0:T(8,128)(2,1)S(1)}, bf16[256,512]{1,0:T(8,128)(2,1)S(1)}, u32[]{:S(2)}, u32[]{:S(2)}) collective-permute-start(bf16[256,512]{1,0:T(8,128)(2,1)S(1)} %get-tuple-element.33), channel_id=1, source_target_pairs={{0,4},{4,0},{8,12},{12,8},{16,20},{20,16},{24,28},{28,24},{32,36},... | collective-permute-start | bytes 786440 | tf_op jit(solution)/shard_map/ppermute | solution.py:327
  37.8 2.1 %collective-permute-start.6 = (bf16[256,512]{1,0:T(8,128)(2,1)S(1)}, bf16[256,512]{1,0:T(8,128)(2,1)S(1)}, u32[]{:S(2)}, u32[]{:S(2)}) collective-permute-start(bf16[256,512]{1,0:T(8,128)(2,1)S(1)} %get-tuple-element.34), channel_id=1, source_target_pairs={{4,8},{12,16},{20,24},{28,32},{36,40},{44,48},{52,56},{60,64},{68,... | collective-permute-start | bytes 786440 | tf_op jit(solution)/shard_map/ppermute | solution.py:331
  39.9 0.0 collective-permute-done.7.mate_up
  39.9 0.0 collective-permute-done.8.mate_down
  40.0 5.6 %collective-permute-done.6.far = bf16[256,512]{1,0:T(8,128)(2,1)S(1)} collective-permute-done((bf16[256,512]{1,0:T(8,128)(2,1)S(1)}, bf16[256,512]{1,0:T(8,128)(2,1)S(1)}, u32[]{:S(2)}, u32[]{:S(2)}) %collective-permute-start.6) | collective-permute-done | bytes 262176 | tf_op jit(solution)/shard_map/ppermute | solution.py:331
  45.5 41.0 %attention_first.1 = (bf16[512,2048]{1,0:T(8,128)(2,1)}, bf16[2,1024,256]{2,1,0:T(8,128)(2,1)S(1)}, bf16[2,2,144,1024]{3,2,1,0:T(8,128)(2,1)S(1)}) custom-call(s32[2]{0:T(128)S(1)} %pad_add_fusion.place_ref, s32[128,1]{1,0:T(8,128)S(1)} %get-tuple-element.20.starts_ref, bf16[512,512]{1,0:T(8,128)(2,1)S(1)} %bitcast.6, ...), custom_call_target="tpu_custom_call" | custom-call | tf_op jit(solution)/shard_map/attention_first/pallas_call | solution.py:266
  86.6 0.0 collective-permute-done.query
  86.6 14.5 %attention_last.1 = bf16[512,2048]{1,0:T(8,128)(2,1)} custom-call(s32[2]{0:T(128)S(1)} %pad_add_fusion.place_ref, s32[128,1]{1,0:T(8,128)S(1)} %get-tuple-element.20.starts_ref, bf16[128,2048]{1,0:T(8,128)(2,1)} %collective-permute-done.query, bf16[2,1024,256]{2,1,0:T(8,128)(2,1)S(1)} %get-tuple-element.30.keys, ...), custom_call_target="tpu_custom_call", output_to_operand_aliasing={{}: (5, {})} | custom-call | tf_op jit(solution)/shard_map/attention_last/pallas_call | solution.py:287
  (1 shorter events, 0.0 us)
Async XLA Ops:
  0.0 6.4 %copy-start = (bf16[128,8192]{1,0:T(8,128)(2,1)S(1)}, bf16[128,8192]{1,0:T(8,128)(2,1)}, u32[]{:S(2)}) copy-start(bf16[128,8192]{1,0:T(8,128)(2,1)} %queries.1) | copy-start | bytes 6291460
  0.0 6.4 %copy-start.1 = (s32[128]{0:T(128)S(1)}, s32[128]{0:T(128)}, u32[]{:S(2)}) copy-start(s32[128]{0:T(128)} %param.7) | copy-start | bytes 1540
  2.0 14.7 %all-to-all-start = ((bf16[4,128,512]{2,1,0:T(8,128)(2,1)}), bf16[4,128,512]{2,1,0:T(8,128)(2,1)S(1)}, u32[]{:S(2)}, u32[]{:S(2)}) async-start(bf16[4,128,512]{2,1,0:T(8,128)(2,1)} %kv_pack.1), calls=%async_computation | async-start | bytes 1048576 | tf_op jit(solution)/shard_map/all_to_all | solution.py:307
  8.2 11.3 %copy-start.2 = (bf16[128,2048]{1,0:T(8,128)(2,1)}, bf16[128,2048]{1,0:T(8,128)(2,1)S(1)}, u32[]{:S(2)}) copy-start(bf16[128,2048]{1,0:T(8,128)(2,1)S(1)} %get-tuple-element.21) | copy-start | bytes 1572868
  8.2 18.6 %collective-permute-start.4 = (bf16[128,2048]{1,0:T(8,128)(2,1)}, bf16[128,2048]{1,0:T(8,128)(2,1)}, u32[]{:S(2)}, u32[]{:S(2)}) collective-permute-start(bf16[128,2048]{1,0:T(8,128)(2,1)} %get-tuple-element.23), channel_id=1, source_target_pairs={{0,1},{1,2},{2,3},{3,0},{4,5},{5,6},{6,7},{7,4},{8,9},{9,10},{10,1... | collective-permute-start | bytes 1572872 | tf_op jit(solution)/shard_map/ppermute | solution.py:311
  12.2 17.5 %collective-permute-start.5 = (bf16[128,2048]{1,0:T(8,128)(2,1)}, bf16[128,2048]{1,0:T(8,128)(2,1)}, u32[]{:S(2)}, u32[]{:S(2)}) collective-permute-start(bf16[128,2048]{1,0:T(8,128)(2,1)} %get-tuple-element.24), channel_id=1, source_target_pairs={{0,3},{1,0},{2,1},{3,2},{4,7},{5,4},{6,5},{7,6},{8,11},{9,8},{10,9... | collective-permute-start | bytes 1572872 | tf_op jit(solution)/shard_map/ppermute | solution.py:311
  17.6 12.0 %collective-permute-start.3 = (bf16[256,512]{1,0:T(8,128)(2,1)}, bf16[256,512]{1,0:T(8,128)(2,1)S(1)}, u32[]{:S(2)}, u32[]{:S(2)}) collective-permute-start(bf16[256,512]{1,0:T(8,128)(2,1)} %get-tuple-element.35), channel_id=1, source_target_pairs={{0,4},{4,0},{8,12},{12,8},{16,20},{20,16},{24,28},{28,24},{32,36},... | collective-permute-start | bytes 786440 | tf_op jit(solution)/shard_map/ppermute | solution.py:323
  19.5 10.8 %collective-permute-start.2 = (bf16[256,512]{1,0:T(8,128)(2,1)}, bf16[256,512]{1,0:T(8,128)(2,1)S(1)}, u32[]{:S(2)}, u32[]{:S(2)}) collective-permute-start(bf16[256,512]{1,0:T(8,128)(2,1)} %get-tuple-element.36), channel_id=1, source_target_pairs={{0,8},{4,12},{8,16},{12,20},{16,24},{20,28},{24,32},{28,36},{32,40... | collective-permute-start | bytes 786440 | tf_op jit(solution)/shard_map/ppermute | solution.py:320
  22.9 10.5 %collective-permute-start.1 = (bf16[256,512]{1,0:T(8,128)(2,1)}, bf16[256,512]{1,0:T(8,128)(2,1)S(1)}, u32[]{:S(2)}, u32[]{:S(2)}) collective-permute-start(bf16[256,512]{1,0:T(8,128)(2,1)} %get-tuple-element.37), channel_id=1, source_target_pairs={{8,0},{12,4},{16,8},{20,12},{24,16},{28,20},{32,24},{36,28},{40,32... | collective-permute-start | bytes 786440 | tf_op jit(solution)/shard_map/ppermute | solution.py:321
  26.9 59.7 %collective-permute-start = (bf16[128,2048]{1,0:T(8,128)(2,1)}, bf16[128,2048]{1,0:T(8,128)(2,1)}, u32[]{:S(2)}, u32[]{:S(2)}) collective-permute-start(bf16[128,2048]{1,0:T(8,128)(2,1)} %copy-done.2), channel_id=1, source_target_pairs={{0,2},{1,3},{2,0},{3,1},{4,6},{5,7},{6,4},{7,5},{8,10},{9,11},{10,... | collective-permute-start | bytes 1572872 | tf_op jit(solution)/shard_map/ppermute | solution.py:311
  33.4 6.5 %collective-permute-start.7 = (bf16[256,512]{1,0:T(8,128)(2,1)S(1)}, bf16[256,512]{1,0:T(8,128)(2,1)S(1)}, u32[]{:S(2)}, u32[]{:S(2)}) collective-permute-start(bf16[256,512]{1,0:T(8,128)(2,1)S(1)} %collective-permute-done.2.up), channel_id=1, source_target_pairs={{0,4},{4,0},{8,12},{12,8},{16,20},{20,16},{24,28},{28,24},{32,36},... | collective-permute-start | bytes 786440 | tf_op jit(solution)/shard_map/ppermute | solution.py:326
  35.4 4.5 %collective-permute-start.8 = (bf16[256,512]{1,0:T(8,128)(2,1)S(1)}, bf16[256,512]{1,0:T(8,128)(2,1)S(1)}, u32[]{:S(2)}, u32[]{:S(2)}) collective-permute-start(bf16[256,512]{1,0:T(8,128)(2,1)S(1)} %get-tuple-element.33), channel_id=1, source_target_pairs={{0,4},{4,0},{8,12},{12,8},{16,20},{20,16},{24,28},{28,24},{32,36},... | collective-permute-start | bytes 786440 | tf_op jit(solution)/shard_map/ppermute | solution.py:327
  37.8 7.7 %collective-permute-start.6 = (bf16[256,512]{1,0:T(8,128)(2,1)S(1)}, bf16[256,512]{1,0:T(8,128)(2,1)S(1)}, u32[]{:S(2)}, u32[]{:S(2)}) collective-permute-start(bf16[256,512]{1,0:T(8,128)(2,1)S(1)} %get-tuple-element.34), channel_id=1, source_target_pairs={{4,8},{12,16},{20,24},{28,32},{36,40},{44,48},{52,56},{60,64},{68,... | collective-permute-start | bytes 786440 | tf_op jit(solution)/shard_map/ppermute | solution.py:331

commit v7 on v6

--- a/solution.py
+++ b/solution.py
@@ -317,18 +317,17 @@
 
     lane0, lane1 = kv[:STRETCH], kv[STRETCH:]
     last = ctx == count - 1
+    swap = [(i, i ^ 1) for i in range(count)]
     up = lax.ppermute(lane0, "ctx", [(i, i + 2) for i in range(count - 2)])
     down = lax.ppermute(lane1, "ctx", [(i + 2, i) for i in range(count - 2)])
-    swap = [(i, i ^ 1) for i in range(count)]
+    route = [(i, i + 3) for i in range(1, count - 3, 2)]
+    route += [(i + 3, i) for i in range(1, count - 3, 2)]
+    route += [(count - 1, count - 3)]
+    far = lax.ppermute(jnp.where(odd, lane0, lane1), "ctx", route)
     inner = lax.ppermute(jnp.where(odd, lane1, lane0), "ctx", swap)
-    down, up, inner, left, right = lax.optimization_barrier((down, up, inner, left, right))
-    above = jnp.where(last, lane0, down)
+    inner, far, down, up, left, right = lax.optimization_barrier((inner, far, down, up, left, right))
     mate_up = lax.ppermute(up, "ctx", swap)
-    mate_down = lax.ppermute(above, "ctx", swap)
-    route = [(i, i + 1) for i in range(1, count - 1, 2)]
-    route += [(i, i - 1) for i in range(2, count - 2, 2)]
-    route += [(count - 1, count - 3)]
-    far = lax.ppermute(jnp.where(odd, jnp.where(last, lane0, up), above), "ctx", route)
+    mate_down = lax.ppermute(jnp.where(last, lane0, down), "ctx", swap)
     return attention(
         count, place, starts, kv, up, down, far, inner, mate_up, mate_down, queries, left, right, across
     )

time: 102 us -> 109 us (1.069)
  the two profiles are of different devices: /device:TPU:408 before, /device:TPU:48 now
where the time goes in v7:
time: 109 us; the launch traced here: 108 us
  Pallas kernels  59.8 us (55%)
  starting transfers between devices  39.9 us (37%)
  waiting for transfers between devices  6.3 us (6%)
  other arithmetic  1.13 us (1%)
    pallas_call x1, Pallas kernels, attention(): pl.pallas_call(functools.partial(first_kernel, count), in_specs=[SMEM_SPE...  41.5 us
    pallas_call x1, Pallas kernels, attention(): pl.pallas_call(functools.partial(last_kernel, count), in_specs=[SMEM_SPEC...  14.5 us
    ppermute x1, starting transfers between devices, body(): far = lax.ppermute(jnp.where(odd, lane0, lane1), 'ctx', route)  10.9 us
    ppermute x3, starting transfers between devices, rotate(): lax.ppermute(block, 'head', [(i, (i + shift) % HEADS) for i in range(HEAD...  9.66 us
    ppermute x1, waiting for transfers between devices, body(): down = lax.ppermute(lane1, 'ctx', [(i + 2, i) for i in range(count - 2)])  4.94 us
    ppermute x1, starting transfers between devices, body(): down = lax.ppermute(lane1, 'ctx', [(i + 2, i) for i in range(count - 2)])  4.49 us
    all_to_all x1, starting transfers between devices, body(): kv = lax.all_to_all(packed, 'head', split_axis=0, concat_axis=0, tiled=True)  4.3 us
    ppermute x1, starting transfers between devices, body(): up = lax.ppermute(lane0, 'ctx', [(i, i + 2) for i in range(count - 2)])  4.27 us
  transfers between devices with their start and end apart: 10, of which 2 were waited for; matrix products, arithmetic and copies ran while one was open for 1% of the time, Pallas kernels for 40%

profile of v7, /device:TPU:48, one launch (start us, length us, event | category | flops | bytes accessed | tf_op | source)
XLA Modules:
  0.0 108.1 jit_solution(16080085197064027357)
XLA Ops:
  0.0 0.0 copy-start
  0.0 0.0 copy-start.1
  0.0 2.0 %kv_pack.1 = bf16[4,128,512]{2,1,0:T(8,128)(2,1)} custom-call(bf16[128,1024]{1,0:T(8,128)(2,1)} %key_ref.1, bf16[128,1024]{1,0:T(8,128)(2,1)} %value_ref.1), custom_call_target="tpu_custom_call" | custom-call | tf_op jit(solution)/shard_map/kv_pack/pallas_call | solution.py:53
  2.0 4.3 %all-to-all-start = ((bf16[4,128,512]{2,1,0:T(8,128)(2,1)}), bf16[4,128,512]{2,1,0:T(8,128)(2,1)S(1)}, u32[]{:S(2)}, u32[]{:S(2)}) async-start(bf16[4,128,512]{2,1,0:T(8,128)(2,1)} %kv_pack.1), calls=%async_computation | async-start | bytes 1048576 | tf_op jit(solution)/shard_map/all_to_all | solution.py:307
  6.3 0.1 pad_add_fusion.place_ref
  6.4 0.0 copy-done
  6.4 0.0 copy-done.1
  6.4 1.8 %query_pack.1 = (bf16[128,2048]{1,0:T(8,128)(2,1)}, bf16[128,2048]{1,0:T(8,128)(2,1)}, bf16[128,2048]{1,0:T(8,128)(2,1)S(1)}, s32[128,1]{1,0:T(8,128)S(1)}) custom-call(s32[2]{0:T(128)S(1)} %pad_add_fusion.place_ref, s32[1,128]{1,0:T(1,128)S(1)} %bitcast.7, bf16[128,8192]{1,0:T(8,128)(2,1)S(1)} %copy-done), custom_call_target="tpu_custom_call" | custom-call | tf_op jit(solution)/shard_map/query_pack/pallas_call | solution.py:90
  8.2 0.0 copy-start.2
  8.2 0.8 copy-done.2
  9.0 3.9 %collective-permute-start.5 = (bf16[128,2048]{1,0:T(8,128)(2,1)}, bf16[128,2048]{1,0:T(8,128)(2,1)S(1)}, u32[]{:S(2)}, u32[]{:S(2)}) collective-permute-start(bf16[128,2048]{1,0:T(8,128)(2,1)} %get-tuple-element.24), channel_id=1, source_target_pairs={{0,1},{1,2},{2,3},{3,0},{4,5},{5,6},{6,7},{7,4},{8,9},{9,10},{10,1... | collective-permute-start | bytes 1572872 | tf_op jit(solution)/shard_map/ppermute | solution.py:311
  12.9 3.1 %collective-permute-start.6 = (bf16[128,2048]{1,0:T(8,128)(2,1)}, bf16[128,2048]{1,0:T(8,128)(2,1)}, u32[]{:S(2)}, u32[]{:S(2)}) collective-permute-start(bf16[128,2048]{1,0:T(8,128)(2,1)} %get-tuple-element.25), channel_id=1, source_target_pairs={{0,3},{1,0},{2,1},{3,2},{4,7},{5,4},{6,5},{7,6},{8,11},{9,8},{10,9... | collective-permute-start | bytes 1572872 | tf_op jit(solution)/shard_map/ppermute | solution.py:311
  16.1 0.0 all-to-all-done
  16.1 1.0 fusion
  17.1 4.3 %collective-permute-start.4 = (bf16[256,512]{1,0:T(8,128)(2,1)}, bf16[256,512]{1,0:T(8,128)(2,1)}, u32[]{:S(2)}, u32[]{:S(2)}) collective-permute-start(bf16[256,512]{1,0:T(8,128)(2,1)} %get-tuple-element.35), channel_id=1, source_target_pairs={{0,8},{4,12},{8,16},{12,20},{16,24},{20,28},{24,32},{28,36},{32,40... | collective-permute-start | bytes 786440 | tf_op jit(solution)/shard_map/ppermute | solution.py:321
  21.4 1.9 %collective-permute-start.1 = (bf16[256,512]{1,0:T(8,128)(2,1)}, bf16[256,512]{1,0:T(8,128)(2,1)}, u32[]{:S(2)}, u32[]{:S(2)}) collective-permute-start(bf16[256,512]{1,0:T(8,128)(2,1)} %get-tuple-element.36), channel_id=1, source_target_pairs={{0,4},{4,0},{8,12},{12,8},{16,20},{20,16},{24,28},{28,24},{32,36},... | collective-permute-start | bytes 786440 | tf_op jit(solution)/shard_map/ppermute | solution.py:327
  23.3 10.9 %collective-permute-start.2 = (bf16[256,512]{1,0:T(8,128)(2,1)}, bf16[256,512]{1,0:T(8,128)(2,1)}, u32[]{:S(2)}, u32[]{:S(2)}) collective-permute-start(bf16[256,512]{1,0:T(8,128)(2,1)} %get-tuple-element.37), channel_id=1, source_target_pairs={{4,16},{12,24},{20,32},{28,40},{36,48},{44,56},{52,64},{60,72},{68... | collective-permute-start | bytes 786440 | tf_op jit(solution)/shard_map/ppermute | solution.py:326
  34.3 0.0 collective-permute-done.5.left
  34.3 4.5 %collective-permute-start.3 = (bf16[256,512]{1,0:T(8,128)(2,1)}, bf16[256,512]{1,0:T(8,128)(2,1)S(1)}, u32[]{:S(2)}, u32[]{:S(2)}) collective-permute-start(bf16[256,512]{1,0:T(8,128)(2,1)} %get-tuple-element.38), channel_id=1, source_target_pairs={{8,0},{12,4},{16,8},{20,12},{24,16},{28,20},{32,24},{36,28},{40,32... | collective-permute-start | bytes 786440 | tf_op jit(solution)/shard_map/ppermute | solution.py:322
  38.8 0.0 collective-permute-done.6.right
  38.8 2.6 %collective-permute-start = (bf16[128,2048]{1,0:T(8,128)(2,1)}, bf16[128,2048]{1,0:T(8,128)(2,1)}, u32[]{:S(2)}, u32[]{:S(2)}) collective-permute-start(bf16[128,2048]{1,0:T(8,128)(2,1)} %copy-done.2), channel_id=1, source_target_pairs={{0,2},{1,3},{2,0},{3,1},{4,6},{5,7},{6,4},{7,5},{8,10},{9,11},{10,... | collective-permute-start | bytes 1572872 | tf_op jit(solution)/shard_map/ppermute | solution.py:311
  41.4 0.0 collective-permute-done.4.up
  41.4 0.0 collective-permute-done.1.inner
  41.4 0.0 collective-permute-done.2.far
  41.4 4.9 %collective-permute-done.3.down = bf16[256,512]{1,0:T(8,128)(2,1)S(1)} collective-permute-done((bf16[256,512]{1,0:T(8,128)(2,1)}, bf16[256,512]{1,0:T(8,128)(2,1)S(1)}, u32[]{:S(2)}, u32[]{:S(2)}) %collective-permute-start.3) | collective-permute-done | bytes 262176 | tf_op jit(solution)/shard_map/ppermute | solution.py:322
  46.4 1.9 %collective-permute-start.8 = (bf16[256,512]{1,0:T(8,128)(2,1)S(1)}, bf16[256,512]{1,0:T(8,128)(2,1)S(1)}, u32[]{:S(2)}, u32[]{:S(2)}) collective-permute-start(bf16[256,512]{1,0:T(8,128)(2,1)S(1)} %broadcast_select_fusion), channel_id=1, source_target_pairs={{0,4},{4,0},{8,12},{12,8},{16,20},{20,16},{24,28},{28,24},{32,36},... | collective-permute-start | bytes 786440 | tf_op jit(solution)/shard_map/ppermute | solution.py:330
  48.3 2.4 %collective-permute-start.7 = (bf16[256,512]{1,0:T(8,128)(2,1)}, bf16[256,512]{1,0:T(8,128)(2,1)S(1)}, u32[]{:S(2)}, u32[]{:S(2)}) collective-permute-start(bf16[256,512]{1,0:T(8,128)(2,1)} %collective-permute-done.4.up), channel_id=1, source_target_pairs={{0,4},{4,0},{8,12},{12,8},{16,20},{20,16},{24,28},{28,24},{32,36},... | collective-permute-start | bytes 786440 | tf_op jit(solution)/shard_map/ppermute | solution.py:329
  50.7 0.0 collective-permute-done.8.mate_down
  50.8 1.3 %collective-permute-done.7.mate_up = bf16[256,512]{1,0:T(8,128)(2,1)S(1)} collective-permute-done((bf16[256,512]{1,0:T(8,128)(2,1)}, bf16[256,512]{1,0:T(8,128)(2,1)S(1)}, u32[]{:S(2)}, u32[]{:S(2)}) %collective-permute-start.7) | collective-permute-done | bytes 262176 | tf_op jit(solution)/shard_map/ppermute | solution.py:329
  52.1 41.5 %attention_first.1 = (bf16[512,2048]{1,0:T(8,128)(2,1)}, bf16[2,1024,256]{2,1,0:T(8,128)(2,1)S(1)}, bf16[2,2,144,1024]{3,2,1,0:T(8,128)(2,1)S(1)}) custom-call(s32[2]{0:T(128)S(1)} %pad_add_fusion.place_ref, s32[128,1]{1,0:T(8,128)S(1)} %get-tuple-element.21.starts_ref, bf16[512,512]{1,0:T(8,128)(2,1)S(1)} %bitcast.6, ...), custom_call_target="tpu_custom_call" | custom-call | tf_op jit(solution)/shard_map/attention_first/pallas_call | solution.py:266
  93.6 0.0 collective-permute-done.query
  93.6 14.5 %attention_last.1 = bf16[512,2048]{1,0:T(8,128)(2,1)} custom-call(s32[2]{0:T(128)S(1)} %pad_add_fusion.place_ref, s32[128,1]{1,0:T(8,128)S(1)} %get-tuple-element.21.starts_ref, bf16[128,2048]{1,0:T(8,128)(2,1)} %collective-permute-done.query, bf16[2,1024,256]{2,1,0:T(8,128)(2,1)S(1)} %get-tuple-element.32.keys, ...), custom_call_target="tpu_custom_call", output_to_operand_aliasing={{}: (5, {})} | custom-call | tf_op jit(solution)/shard_map/attention_last/pallas_call | solution.py:287
  (1 shorter events, 0.0 us)
Async XLA Ops:
  0.0 6.4 %copy-start = (bf16[128,8192]{1,0:T(8,128)(2,1)S(1)}, bf16[128,8192]{1,0:T(8,128)(2,1)}, u32[]{:S(2)}) copy-start(bf16[128,8192]{1,0:T(8,128)(2,1)} %queries.1) | copy-start | bytes 6291460
  0.0 6.4 %copy-start.1 = (s32[128]{0:T(128)S(1)}, s32[128]{0:T(128)}, u32[]{:S(2)}) copy-start(s32[128]{0:T(128)} %param.7) | copy-start | bytes 1540
  2.0 14.1 %all-to-all-start = ((bf16[4,128,512]{2,1,0:T(8,128)(2,1)}), bf16[4,128,512]{2,1,0:T(8,128)(2,1)S(1)}, u32[]{:S(2)}, u32[]{:S(2)}) async-start(bf16[4,128,512]{2,1,0:T(8,128)(2,1)} %kv_pack.1), calls=%async_computation | async-start | bytes 1048576 | tf_op jit(solution)/shard_map/all_to_all | solution.py:307
  8.2 0.8 copy-start.2
  9.0 25.2 %collective-permute-start.5 = (bf16[128,2048]{1,0:T(8,128)(2,1)}, bf16[128,2048]{1,0:T(8,128)(2,1)S(1)}, u32[]{:S(2)}, u32[]{:S(2)}) collective-permute-start(bf16[128,2048]{1,0:T(8,128)(2,1)} %get-tuple-element.24), channel_id=1, source_target_pairs={{0,1},{1,2},{2,3},{3,0},{4,5},{5,6},{6,7},{7,4},{8,9},{9,10},{10,1... | collective-permute-start | bytes 1572872 | tf_op jit(solution)/shard_map/ppermute | solution.py:311
  12.9 25.8 %collective-permute-start.6 = (bf16[128,2048]{1,0:T(8,128)(2,1)}, bf16[128,2048]{1,0:T(8,128)(2,1)}, u32[]{:S(2)}, u32[]{:S(2)}) collective-permute-start(bf16[128,2048]{1,0:T(8,128)(2,1)} %get-tuple-element.25), channel_id=1, source_target_pairs={{0,3},{1,0},{2,1},{3,2},{4,7},{5,4},{6,5},{7,6},{8,11},{9,8},{10,9... | collective-permute-start | bytes 1572872 | tf_op jit(solution)/shard_map/ppermute | solution.py:311
  17.1 24.3 %collective-permute-start.4 = (bf16[256,512]{1,0:T(8,128)(2,1)}, bf16[256,512]{1,0:T(8,128)(2,1)}, u32[]{:S(2)}, u32[]{:S(2)}) collective-permute-start(bf16[256,512]{1,0:T(8,128)(2,1)} %get-tuple-element.35), channel_id=1, source_target_pairs={{0,8},{4,12},{8,16},{12,20},{16,24},{20,28},{24,32},{28,36},{32,40... | collective-permute-start | bytes 786440 | tf_op jit(solution)/shard_map/ppermute | solution.py:321
  21.4 20.0 %collective-permute-start.1 = (bf16[256,512]{1,0:T(8,128)(2,1)}, bf16[256,512]{1,0:T(8,128)(2,1)}, u32[]{:S(2)}, u32[]{:S(2)}) collective-permute-start(bf16[256,512]{1,0:T(8,128)(2,1)} %get-tuple-element.36), channel_id=1, source_target_pairs={{0,4},{4,0},{8,12},{12,8},{16,20},{20,16},{24,28},{28,24},{32,36},... | collective-permute-start | bytes 786440 | tf_op jit(solution)/shard_map/ppermute | solution.py:327
  23.3 18.1 %collective-permute-start.2 = (bf16[256,512]{1,0:T(8,128)(2,1)}, bf16[256,512]{1,0:T(8,128)(2,1)}, u32[]{:S(2)}, u32[]{:S(2)}) collective-permute-start(bf16[256,512]{1,0:T(8,128)(2,1)} %get-tuple-element.37), channel_id=1, source_target_pairs={{4,16},{12,24},{20,32},{28,40},{36,48},{44,56},{52,64},{60,72},{68... | collective-permute-start | bytes 786440 | tf_op jit(solution)/shard_map/ppermute | solution.py:326
  34.3 12.1 %collective-permute-start.3 = (bf16[256,512]{1,0:T(8,128)(2,1)}, bf16[256,512]{1,0:T(8,128)(2,1)S(1)}, u32[]{:S(2)}, u32[]{:S(2)}) collective-permute-start(bf16[256,512]{1,0:T(8,128)(2,1)} %get-tuple-element.38), channel_id=1, source_target_pairs={{8,0},{12,4},{16,8},{20,12},{24,16},{28,20},{32,24},{36,28},{40,32... | collective-permute-start | bytes 786440 | tf_op jit(solution)/shard_map/ppermute | solution.py:322
  38.8 54.8 %collective-permute-start = (bf16[128,2048]{1,0:T(8,128)(2,1)}, bf16[128,2048]{1,0:T(8,128)(2,1)}, u32[]{:S(2)}, u32[]{:S(2)}) collective-permute-start(bf16[128,2048]{1,0:T(8,128)(2,1)} %copy-done.2), channel_id=1, source_target_pairs={{0,2},{1,3},{2,0},{3,1},{4,6},{5,7},{6,4},{7,5},{8,10},{9,11},{10,... | collective-permute-start | bytes 1572872 | tf_op jit(solution)/shard_map/ppermute | solution.py:311
  46.4 4.3 %collective-permute-start.8 = (bf16[256,512]{1,0:T(8,128)(2,1)S(1)}, bf16[256,512]{1,0:T(8,128)(2,1)S(1)}, u32[]{:S(2)}, u32[]{:S(2)}) collective-permute-start(bf16[256,512]{1,0:T(8,128)(2,1)S(1)} %broadcast_select_fusion), channel_id=1, source_target_pairs={{0,4},{4,0},{8,12},{12,8},{16,20},{20,16},{24,28},{28,24},{32,36},... | collective-permute-start | bytes 786440 | tf_op jit(solution)/shard_map/ppermute | solution.py:330
  48.3 3.8 %collective-permute-start.7 = (bf16[256,512]{1,0:T(8,128)(2,1)}, bf16[256,512]{1,0:T(8,128)(2,1)S(1)}, u32[]{:S(2)}, u32[]{:S(2)}) collective-permute-start(bf16[256,512]{1,0:T(8,128)(2,1)} %collective-permute-done.4.up), channel_id=1, source_target_pairs={{0,4},{4,0},{8,12},{12,8},{16,20},{20,16},{24,28},{28,24},{32,36},... | collective-permute-start | bytes 786440 | tf_op jit(solution)/shard_map/ppermute | solution.py:329

commit v8 on v7

--- a/solution.py
+++ b/solution.py
@@ -146,22 +146,55 @@
     return wait
 
 
-def attend(block, ctx, count, starts, query, keys, values_t, bias, out):
-    lane = block // 2
-    half = lax.rem(block, 2)
-    stretch = jnp.where(lane == 0, ctx, 2 * count - 1 - ctx)
-    first = stretch * STRETCH + half * ROWS
-    row_pos = first + lax.broadcasted_iota(jnp.int32, (1, ROWS), 1)
-    row_start = jnp.max(jnp.where(starts <= row_pos, starts, 0), axis=0, keepdims=True)
-    key_pos = first - REACH * STRETCH + lax.broadcasted_iota(jnp.int32, (KEYS, ROWS), 0)
-    allowed = (key_pos >= row_start) & (key_pos <= row_pos)
-    bias[...] = jnp.where(allowed, 0.0, -jnp.inf).astype(jnp.float32)
-    window = pl.ds(pl.multiple_of(half * ROWS, ROWS), KEYS)
+def attention_kernel(
+    count, place_ref, starts_ref, own, up, down, far, inner, mate_up, mate_down,
+    queries, left, right, across,
+    out_ref, keys, values, values_t, query, result, bias, flags, sems, load_sems, store_sems,
+):
+    ctx, head = place_ref[0], place_ref[1]
+    width = query.shape[2]
     kv_local = keys.shape[2] // HEAD_DIM
-
-    def part(kv_head, base, heads, raise_by):
+    part_width = width // kv_local
+    wait = load_windows(
+        ctx, count, own, up, down, far, inner, mate_up, mate_down, keys, values, sems
+    )
+
+    def load(shift, source):
+        block = lax.rem(head + HEADS - shift, HEADS)
+        return pltpu.make_async_copy(source, query.at[block], load_sems.at[shift])
+
+    own_cols = pl.ds(pl.multiple_of(head * width, width), width)
+    loads = [
+        load(shift, source)
+        for shift, source in enumerate((queries.at[:, own_cols], left, across, right))
+    ]
+    for copy in loads:
+        copy.start()
+    flags[...] = jnp.zeros_like(flags)
+
+    def store(block, kv_head):
+        rows = pl.ds(pl.multiple_of(block * ROWS, ROWS), ROWS)
+        cols = pl.ds(kv_head * part_width, part_width)
+        return pltpu.make_async_copy(
+            result.at[block, :, cols], out_ref.at[rows, cols], store_sems.at[block, kv_head]
+        )
+
+    def set_bias(block):
+        lane, half = block // 2, lax.rem(block, 2)
+        stretch = jnp.where(lane == 0, ctx, 2 * count - 1 - ctx)
+        first = stretch * STRETCH + half * ROWS
+        starts = starts_ref[...]
+        row_pos = first + lax.broadcasted_iota(jnp.int32, (1, ROWS), 1)
+        row_start = jnp.max(jnp.where(starts <= row_pos, starts, 0), axis=0, keepdims=True)
+        key_pos = first - REACH * STRETCH + lax.broadcasted_iota(jnp.int32, (KEYS, ROWS), 0)
+        allowed = (key_pos >= row_start) & (key_pos <= row_pos)
+        bias[...] = jnp.where(allowed, 0.0, -jnp.inf).astype(jnp.float32)
+
+    def part(block, kv_head, base, heads, raise_by):
+        lane, half = block // 2, lax.rem(block, 2)
+        window = pl.ds(pl.multiple_of(half * ROWS, ROWS), KEYS)
         cols = [pl.ds(base + at * HEAD_DIM, HEAD_DIM) for at in range(heads)]
-        stacked = jnp.concatenate([query[:, col] for col in cols], axis=0)
+        stacked = jnp.concatenate([query[block, :, col] for col in cols], axis=0)
         key = keys[lane, window, kv_head * HEAD_DIM : (kv_head + 1) * HEAD_DIM]
         scores = lax.dot_general(
             key, stacked, (((1,), (1,)), ((), ())), preferred_element_type=jnp.float32
@@ -172,46 +205,11 @@
             values_t[lane, kv_head, :, window], weights, preferred_element_type=jnp.float32
         )
         total = mixed[HEAD_DIM : HEAD_DIM + 1]
-        result = (mixed[:HEAD_DIM] / total).astype(out.dtype)
+        part_result = (mixed[:HEAD_DIM] / total).astype(out_ref.dtype)
         for at, col in enumerate(cols):
-            out[:, col] = result[:, at * HEAD_DIM : (at + 1) * HEAD_DIM].T
-        return jnp.where((total >= SMALL) & (total <= LARGE), 0, 1)
-
-    outside = [
-        part(kv_head, kv_head * GROUP * HEAD_DIM, GROUP, lambda s, m: s * EXPONENT_SCALE + m)
-        for kv_head in range(kv_local)
-    ]
-
-    @pl.when(jnp.max(functools.reduce(jnp.maximum, outside)) > 0)
-    def _():
-        def shifted(scores, masks):
-            scores = scores + masks
-            return (scores - jnp.max(scores, axis=0, keepdims=True)) * EXPONENT_SCALE
-
-        for kv_head in range(kv_local):
-
-            @pl.loop(0, GROUP)
-            def _(head):
-                base = pl.multiple_of((kv_head * GROUP + head) * HEAD_DIM, HEAD_DIM)
-                part(kv_head, base, 1, shifted)
-
-
-def first_kernel(
-    count, place_ref, starts_ref, own, up, down, far, inner, mate_up, mate_down, queries, left, right,
-    out_ref, keys, values_t, values, query, result, bias, sems, load_sems, store_sems,
-):
-    ctx, head = place_ref[0], place_ref[1]
-    width = query.shape[2]
-    wait = load_windows(ctx, count, own, up, down, far, inner, mate_up, mate_down, keys, values, sems)
-    own_cols = pl.ds(pl.multiple_of(head * width, width), width)
-    sources = (queries.at[:, own_cols], left, right)
-    loads = [
-        pltpu.make_async_copy(source, query.at[at], load_sems.at[at])
-        for at, source in enumerate(sources)
-    ]
-    for load in loads:
-        load.start()
-    kv_local = keys.shape[2] // HEAD_DIM
+            result[block, :, col] = part_result[:, at * HEAD_DIM : (at + 1) * HEAD_DIM].T
+        return total
+
     for lane in range(LANES):
         wait(0, lane)
         for kv_head in range(kv_local):
@@ -223,77 +221,77 @@
             )
     for lane in range(LANES):
         wait(1, lane)
-    for load in loads:
-        load.wait()
-
-    def store(at):
-        shift = jnp.where(at == 0, 0, jnp.where(at == 1, 3, 1))
-        block = lax.rem(head + shift, HEADS)
-        rows = pl.ds(pl.multiple_of(block * ROWS, ROWS), ROWS)
-        return block, pltpu.make_async_copy(result.at[at], out_ref.at[rows, :], store_sems.at[at])
-
-    @pl.loop(0, 3)
-    def _(at):
-        block, copy = store(at)
-        attend(
-            block, ctx, count, starts_ref[...], query.at[at], keys, values_t, bias, result.at[at]
-        )
-        copy.start()
-
-    for at in range(3):
-        store(at)[1].wait()
-
-
-def last_kernel(
-    count, place_ref, starts_ref, query, keys, values_t, partial, out_ref, result, bias, sem
+    for copy in loads:
+        copy.wait()
+
+    @pl.loop(0, HEADS)
+    def _(block):
+        set_bias(block)
+        for kv_head in range(kv_local):
+            total = part(
+                block, kv_head, kv_head * part_width, GROUP,
+                lambda scores, masks: scores * EXPONENT_SCALE + masks,
+            )
+            inside = (total >= SMALL) & (total <= LARGE)
+            flags[...] = jnp.maximum(flags[...], jnp.where(inside, 0.0, 1.0))
+            store(block, kv_head).start()
+
+    for block in range(HEADS):
+        for kv_head in range(kv_local):
+            store(block, kv_head).wait()
+
+    @pl.when(jnp.max(flags[...]) > 0)
+    def _():
+        def shifted(scores, masks):
+            scores = scores + masks
+            return (scores - jnp.max(scores, axis=0, keepdims=True)) * EXPONENT_SCALE
+
+        @pl.loop(0, HEADS)
+        def _(block):
+            set_bias(block)
+            for kv_head in range(kv_local):
+
+                @pl.loop(0, GROUP)
+                def _(head):
+                    base = pl.multiple_of(kv_head * part_width + head * HEAD_DIM, HEAD_DIM)
+                    part(block, kv_head, base, 1, shifted)
+
+                copy = store(block, kv_head)
+                copy.start()
+                copy.wait()
+
+
+def attention(
+    count, place, starts, own, up, down, far, inner, mate_up, mate_down,
+    queries, left, right, across,
 ):
-    ctx, head = place_ref[0], place_ref[1]
-    block = lax.rem(head + 2, HEADS)
-    attend(block, ctx, count, starts_ref[...], query, keys, values_t, bias, result)
-    rows = pl.ds(pl.multiple_of(block * ROWS, ROWS), ROWS)
-    copy = pltpu.make_async_copy(result, out_ref.at[rows, :], sem)
-    copy.start()
-    copy.wait()
-
-
-def attention(count, place, starts, own, up, down, far, inner, mate_up, mate_down, queries, left, right, across):
     rows, width = left.shape
     kv_width = own.shape[1] // 2
     kv_local = kv_width // HEAD_DIM
     dtype = queries.dtype
-    out_shape = jax.ShapeDtypeStruct((HEADS * rows, width), dtype)
-    bias = pltpu.VMEM((KEYS, ROWS), jnp.float32)
-    partial, keys, values_t = pl.pallas_call(
-        functools.partial(first_kernel, count),
-        in_specs=[SMEM_SPEC, VMEM_SPEC] + [VMEM_SPEC] * 7 + [ANY_SPEC] * 3,
-        out_specs=[ANY_SPEC, VMEM_SPEC, VMEM_SPEC],
-        out_shape=[
-            out_shape,
-            jax.ShapeDtypeStruct((LANES, WINDOW, kv_width), dtype),
-            jax.ShapeDtypeStruct((LANES, kv_local, PADDED, WINDOW), dtype),
-        ],
+    return pl.pallas_call(
+        functools.partial(attention_kernel, count),
+        in_specs=[SMEM_SPEC, VMEM_SPEC] + [VMEM_SPEC] * 7 + [ANY_SPEC] * 4,
+        out_specs=ANY_SPEC,
+        out_shape=jax.ShapeDtypeStruct((HEADS * rows, width), dtype),
         scratch_shapes=[
             pltpu.VMEM((LANES, WINDOW, kv_width), dtype),
-            pltpu.VMEM((3, rows, width), dtype),
-            pltpu.VMEM((3, rows, width), dtype),
-            bias,
+            pltpu.VMEM((LANES, WINDOW, kv_width), dtype),
+            pltpu.VMEM((LANES, kv_local, PADDED, WINDOW), dtype),
+            pltpu.VMEM((HEADS, rows, width), dtype),
+            pltpu.VMEM((HEADS, rows, width), dtype),
+            pltpu.VMEM((KEYS, ROWS), jnp.float32),
+            pltpu.VMEM((1, GROUP * ROWS), jnp.float32),
             pltpu.SemaphoreType.DMA((2, LANES, REACH + 1)),
-            pltpu.SemaphoreType.DMA((3,)),
-            pltpu.SemaphoreType.DMA((3,)),
+            pltpu.SemaphoreType.DMA((HEADS,)),
+            pltpu.SemaphoreType.DMA((HEADS, kv_local)),
         ],
         compiler_params=PARAMS,
-        name="attention_first",
-    )(place, starts, own, up, down, far, inner, mate_up, mate_down, queries, left, right)
-    return pl.pallas_call(
-        functools.partial(last_kernel, count),
-        in_specs=[SMEM_SPEC] + [VMEM_SPEC] * 4 + [ANY_SPEC],
-        out_specs=ANY_SPEC,
-        out_shape=out_shape,
-        scratch_shapes=[pltpu.VMEM((rows, width), dtype), bias, pltpu.SemaphoreType.DMA],
-        input_output_aliases={5: 0},
-        compiler_params=PARAMS,
-        name="attention_last",
-    )(place, starts, across, keys, values_t, partial)
+        name="attention",
+    )(
+        place, starts, own, up, down, far, inner, mate_up, mate_down,
+        queries, left, right, across,
+    )
 
 
 def body(queries, key_rows, value_rows, doc_lengths):
@@ -325,7 +323,7 @@
     route += [(count - 1, count - 3)]
     far = lax.ppermute(jnp.where(odd, lane0, lane1), "ctx", route)
     inner = lax.ppermute(jnp.where(odd, lane1, lane0), "ctx", swap)
-    inner, far, down, up, left, right = lax.optimization_barrier((inner, far, down, up, left, right))
+    down, far, up, left, right = lax.optimization_barrier((down, far, up, left, right))
     mate_up = lax.ppermute(up, "ctx", swap)
     mate_down = lax.ppermute(jnp.where(last, lane0, down), "ctx", swap)
     return attention(

time: 109 us -> 111 us (1.018)
  the two profiles are of different devices: /device:TPU:48 before, /device:TPU:1 now
where the time goes in v8:
time: 111 us; the launch traced here: 109 us
  Pallas kernels  63.9 us (58%)
  starting transfers between devices  34.3 us (31%)
  waiting for transfers between devices  9.28 us (8%)
    pallas_call x1, Pallas kernels, attention(): pl.pallas_call(functools.partial(attention_kernel, count), in_specs=[SMEM...  60.1 us
    ppermute x3, starting transfers between devices, rotate(): lax.ppermute(block, 'head', [(i, (i + shift) % HEADS) for i in range(HEAD...  10.4 us
    ppermute x1, waiting for transfers between devices, body(): down = lax.ppermute(lane1, 'ctx', [(i + 2, i) for i in range(count - 2)])  7.79 us
    ppermute x1, starting transfers between devices, body(): far = lax.ppermute(jnp.where(odd, lane0, lane1), 'ctx', route)  6.78 us
    all_to_all x1, starting transfers between devices, body(): kv = lax.all_to_all(packed, 'head', split_axis=0, concat_axis=0, tiled=True)  4.85 us
    ppermute x1, starting transfers between devices, body(): up = lax.ppermute(lane0, 'ctx', [(i, i + 2) for i in range(count - 2)])  4.71 us
    ppermute x1, starting transfers between devices, body(): mate_down = lax.ppermute(jnp.where(last, lane0, down), 'ctx', swap)  2.41 us
  transfers between devices with their start and end apart: 10, of which 2 were waited for; matrix products, arithmetic and copies ran while one was open for 1% of the time, Pallas kernels for 2%

profile of v8, /device:TPU:1, one launch (start us, length us, event | category | flops | bytes accessed | tf_op | source)
XLA Modules:
  0.0 109.4 jit_solution(845245131080783610)
XLA Ops:
  0.0 0.0 copy-start
  0.0 0.0 copy-start.1
  0.0 2.0 %kv_pack.1 = bf16[4,128,512]{2,1,0:T(8,128)(2,1)} custom-call(bf16[128,1024]{1,0:T(8,128)(2,1)} %key_ref.1, bf16[128,1024]{1,0:T(8,128)(2,1)} %value_ref.1), custom_call_target="tpu_custom_call" | custom-call | tf_op jit(solution)/shard_map/kv_pack/pallas_call | solution.py:53
  2.0 4.9 %all-to-all-start = ((bf16[4,128,512]{2,1,0:T(8,128)(2,1)}), bf16[4,128,512]{2,1,0:T(8,128)(2,1)S(1)}, u32[]{:S(2)}, u32[]{:S(2)}) async-start(bf16[4,128,512]{2,1,0:T(8,128)(2,1)} %kv_pack.1), calls=%async_computation | async-start | bytes 1048576 | tf_op jit(solution)/shard_map/all_to_all | solution.py:305
  6.9 0.1 pad_add_fusion.place_ref
  6.9 0.0 copy-done
  6.9 0.0 copy-done.1
  6.9 1.8 %query_pack.1 = (bf16[128,2048]{1,0:T(8,128)(2,1)}, bf16[128,2048]{1,0:T(8,128)(2,1)}, bf16[128,2048]{1,0:T(8,128)(2,1)S(1)}, s32[128,1]{1,0:T(8,128)S(1)}) custom-call(s32[2]{0:T(128)S(1)} %pad_add_fusion.place_ref, s32[1,128]{1,0:T(1,128)S(1)} %bitcast.7, bf16[128,8192]{1,0:T(8,128)(2,1)S(1)} %copy-done), custom_call_target="tpu_custom_call" | custom-call | tf_op jit(solution)/shard_map/query_pack/pallas_call | solution.py:90
  8.8 0.0 copy-start.2
  8.8 0.8 copy-done.2
  9.6 3.4 %collective-permute-start.3 = (bf16[128,2048]{1,0:T(8,128)(2,1)}, bf16[128,2048]{1,0:T(8,128)(2,1)S(1)}, u32[]{:S(2)}, u32[]{:S(2)}) collective-permute-start(bf16[128,2048]{1,0:T(8,128)(2,1)} %get-tuple-element.19), channel_id=1, source_target_pairs={{0,1},{1,2},{2,3},{3,0},{4,5},{5,6},{6,7},{7,4},{8,9},{9,10},{10,1... | collective-permute-start | bytes 1572872 | tf_op jit(solution)/shard_map/ppermute | solution.py:309
  12.9 3.1 %collective-permute-start.4 = (bf16[128,2048]{1,0:T(8,128)(2,1)}, bf16[128,2048]{1,0:T(8,128)(2,1)}, u32[]{:S(2)}, u32[]{:S(2)}) collective-permute-start(bf16[128,2048]{1,0:T(8,128)(2,1)} %get-tuple-element.20), channel_id=1, source_target_pairs={{0,3},{1,0},{2,1},{3,2},{4,7},{5,4},{6,5},{7,6},{8,11},{9,8},{10,9... | collective-permute-start | bytes 1572872 | tf_op jit(solution)/shard_map/ppermute | solution.py:309
  16.1 0.0 all-to-all-done
  16.1 0.9 fusion
  17.0 4.7 %collective-permute-start.2 = (bf16[256,512]{1,0:T(8,128)(2,1)}, bf16[256,512]{1,0:T(8,128)(2,1)}, u32[]{:S(2)}, u32[]{:S(2)}) collective-permute-start(bf16[256,512]{1,0:T(8,128)(2,1)} %get-tuple-element.29), channel_id=1, source_target_pairs={{0,8},{4,12},{8,16},{12,20},{16,24},{20,28},{24,32},{28,36},{32,40... | collective-permute-start | bytes 786440 | tf_op jit(solution)/shard_map/ppermute | solution.py:319
  21.7 6.8 %collective-permute-start.1 = (bf16[256,512]{1,0:T(8,128)(2,1)}, bf16[256,512]{1,0:T(8,128)(2,1)}, u32[]{:S(2)}, u32[]{:S(2)}) collective-permute-start(bf16[256,512]{1,0:T(8,128)(2,1)} %get-tuple-element.30), channel_id=1, source_target_pairs={{4,16},{12,24},{20,32},{28,40},{36,48},{44,56},{52,64},{60,72},{68... | collective-permute-start | bytes 786440 | tf_op jit(solution)/shard_map/ppermute | solution.py:324
  28.5 1.3 %collective-permute-start = (bf16[256,512]{1,0:T(8,128)(2,1)}, bf16[256,512]{1,0:T(8,128)(2,1)S(1)}, u32[]{:S(2)}, u32[]{:S(2)}) collective-permute-start(bf16[256,512]{1,0:T(8,128)(2,1)} %get-tuple-element.31), channel_id=1, source_target_pairs={{8,0},{12,4},{16,8},{20,12},{24,16},{28,20},{32,24},{36,28},{40,32... | collective-permute-start | bytes 786440 | tf_op jit(solution)/shard_map/ppermute | solution.py:320
  29.8 0.0 collective-permute-done.3.left
  29.8 3.9 %collective-permute-start.8 = (bf16[128,2048]{1,0:T(8,128)(2,1)}, bf16[128,2048]{1,0:T(8,128)(2,1)}, u32[]{:S(2)}, u32[]{:S(2)}) collective-permute-start(bf16[128,2048]{1,0:T(8,128)(2,1)} %copy-done.2), channel_id=1, source_target_pairs={{0,2},{1,3},{2,0},{3,1},{4,6},{5,7},{6,4},{7,5},{8,10},{9,11},{10,... | collective-permute-start | bytes 1572872 | tf_op jit(solution)/shard_map/ppermute | solution.py:309
  33.7 0.0 collective-permute-done.4.right
  33.8 0.0 collective-permute-done.2.up
  33.8 0.0 collective-permute-done.1.far
  33.8 7.8 %collective-permute-done.down = bf16[256,512]{1,0:T(8,128)(2,1)S(1)} collective-permute-done((bf16[256,512]{1,0:T(8,128)(2,1)}, bf16[256,512]{1,0:T(8,128)(2,1)S(1)}, u32[]{:S(2)}, u32[]{:S(2)}) %collective-permute-start) | collective-permute-done | bytes 262176 | tf_op jit(solution)/shard_map/ppermute | solution.py:320
  41.6 1.9 %collective-permute-start.6 = (bf16[256,512]{1,0:T(8,128)(2,1)}, bf16[256,512]{1,0:T(8,128)(2,1)S(1)}, u32[]{:S(2)}, u32[]{:S(2)}) collective-permute-start(bf16[256,512]{1,0:T(8,128)(2,1)} %collective-permute-done.2.up), channel_id=1, source_target_pairs={{0,4},{4,0},{8,12},{12,8},{16,20},{20,16},{24,28},{28,24},{32,36},... | collective-permute-start | bytes 786440 | tf_op jit(solution)/shard_map/ppermute | solution.py:327
  43.5 0.1 broadcast_select_fusion
  43.5 2.4 %collective-permute-start.7 = (bf16[256,512]{1,0:T(8,128)(2,1)S(1)}, bf16[256,512]{1,0:T(8,128)(2,1)S(1)}, u32[]{:S(2)}, u32[]{:S(2)}) collective-permute-start(bf16[256,512]{1,0:T(8,128)(2,1)S(1)} %get-tuple-element.27), channel_id=1, source_target_pairs={{0,4},{4,0},{8,12},{12,8},{16,20},{20,16},{24,28},{28,24},{32,36},... | collective-permute-start | bytes 786440 | tf_op jit(solution)/shard_map/ppermute | solution.py:328
  46.0 1.9 %collective-permute-start.5 = (bf16[256,512]{1,0:T(8,128)(2,1)S(1)}, bf16[256,512]{1,0:T(8,128)(2,1)S(1)}, u32[]{:S(2)}, u32[]{:S(2)}) collective-permute-start(bf16[256,512]{1,0:T(8,128)(2,1)S(1)} %get-tuple-element.28), channel_id=1, source_target_pairs={{0,4},{4,0},{8,12},{12,8},{16,20},{20,16},{24,28},{28,24},{32,36},... | collective-permute-start | bytes 786440 | tf_op jit(solution)/shard_map/ppermute | solution.py:325
  47.9 0.0 collective-permute-done.8.across
  47.9 0.0 collective-permute-done.6.mate_up
  47.9 0.0 collective-permute-done.7.mate_down
  47.9 1.5 %collective-permute-done.5.inner = bf16[256,512]{1,0:T(8,128)(2,1)S(1)} collective-permute-done((bf16[256,512]{1,0:T(8,128)(2,1)S(1)}, bf16[256,512]{1,0:T(8,128)(2,1)S(1)}, u32[]{:S(2)}, u32[]{:S(2)}) %collective-permute-start.5) | collective-permute-done | bytes 262176 | tf_op jit(solution)/shard_map/ppermute | solution.py:325
  49.4 60.1 %attention.1 = bf16[512,2048]{1,0:T(8,128)(2,1)} custom-call(s32[2]{0:T(128)S(1)} %pad_add_fusion.place_ref, s32[128,1]{1,0:T(8,128)S(1)} %get-tuple-element.17.starts_ref, bf16[512,512]{1,0:T(8,128)(2,1)S(1)} %bitcast.6, bf16[256,512]{1,0:T(8,128)(2,1)} %collective-permute-done.2.up, bf16[256,512]{1,0:T(8,128)(2,1)S(1)} %collective-permute-done.down, ...), custom_call_target="tpu_custom_call" | custom-call | tf_op jit(solution)/shard_map/attention/pallas_call | solution.py:272
Async XLA Ops:
  0.0 6.9 %copy-start = (bf16[128,8192]{1,0:T(8,128)(2,1)S(1)}, bf16[128,8192]{1,0:T(8,128)(2,1)}, u32[]{:S(2)}) copy-start(bf16[128,8192]{1,0:T(8,128)(2,1)} %queries.1) | copy-start | bytes 6291460
  0.0 6.9 %copy-start.1 = (s32[128]{0:T(128)S(1)}, s32[128]{0:T(128)}, u32[]{:S(2)}) copy-start(s32[128]{0:T(128)} %param.7) | copy-start | bytes 1540
  2.0 14.1 %all-to-all-start = ((bf16[4,128,512]{2,1,0:T(8,128)(2,1)}), bf16[4,128,512]{2,1,0:T(8,128)(2,1)S(1)}, u32[]{:S(2)}, u32[]{:S(2)}) async-start(bf16[4,128,512]{2,1,0:T(8,128)(2,1)} %kv_pack.1), calls=%async_computation | async-start | bytes 1048576 | tf_op jit(solution)/shard_map/all_to_all | solution.py:305
  8.8 0.8 copy-start.2
  9.6 20.2 %collective-permute-start.3 = (bf16[128,2048]{1,0:T(8,128)(2,1)}, bf16[128,2048]{1,0:T(8,128)(2,1)S(1)}, u32[]{:S(2)}, u32[]{:S(2)}) collective-permute-start(bf16[128,2048]{1,0:T(8,128)(2,1)} %get-tuple-element.19), channel_id=1, source_target_pairs={{0,1},{1,2},{2,3},{3,0},{4,5},{5,6},{6,7},{7,4},{8,9},{9,10},{10,1... | collective-permute-start | bytes 1572872 | tf_op jit(solution)/shard_map/ppermute | solution.py:309
  12.9 20.8 %collective-permute-start.4 = (bf16[128,2048]{1,0:T(8,128)(2,1)}, bf16[128,2048]{1,0:T(8,128)(2,1)}, u32[]{:S(2)}, u32[]{:S(2)}) collective-permute-start(bf16[128,2048]{1,0:T(8,128)(2,1)} %get-tuple-element.20), channel_id=1, source_target_pairs={{0,3},{1,0},{2,1},{3,2},{4,7},{5,4},{6,5},{7,6},{8,11},{9,8},{10,9... | collective-permute-start | bytes 1572872 | tf_op jit(solution)/shard_map/ppermute | solution.py:309
  17.0 16.8 %collective-permute-start.2 = (bf16[256,512]{1,0:T(8,128)(2,1)}, bf16[256,512]{1,0:T(8,128)(2,1)}, u32[]{:S(2)}, u32[]{:S(2)}) collective-permute-start(bf16[256,512]{1,0:T(8,128)(2,1)} %get-tuple-element.29), channel_id=1, source_target_pairs={{0,8},{4,12},{8,16},{12,20},{16,24},{20,28},{24,32},{28,36},{32,40... | collective-permute-start | bytes 786440 | tf_op jit(solution)/shard_map/ppermute | solution.py:319
  21.7 12.1 %collective-permute-start.1 = (bf16[256,512]{1,0:T(8,128)(2,1)}, bf16[256,512]{1,0:T(8,128)(2,1)}, u32[]{:S(2)}, u32[]{:S(2)}) collective-permute-start(bf16[256,512]{1,0:T(8,128)(2,1)} %get-tuple-element.30), channel_id=1, source_target_pairs={{4,16},{12,24},{20,32},{28,40},{36,48},{44,56},{52,64},{60,72},{68... | collective-permute-start | bytes 786440 | tf_op jit(solution)/shard_map/ppermute | solution.py:324
  28.5 13.1 %collective-permute-start = (bf16[256,512]{1,0:T(8,128)(2,1)}, bf16[256,512]{1,0:T(8,128)(2,1)S(1)}, u32[]{:S(2)}, u32[]{:S(2)}) collective-permute-start(bf16[256,512]{1,0:T(8,128)(2,1)} %get-tuple-element.31), channel_id=1, source_target_pairs={{8,0},{12,4},{16,8},{20,12},{24,16},{28,20},{32,24},{36,28},{40,32... | collective-permute-start | bytes 786440 | tf_op jit(solution)/shard_map/ppermute | solution.py:320
  29.8 18.1 %collective-permute-start.8 = (bf16[128,2048]{1,0:T(8,128)(2,1)}, bf16[128,2048]{1,0:T(8,128)(2,1)}, u32[]{:S(2)}, u32[]{:S(2)}) collective-permute-start(bf16[128,2048]{1,0:T(8,128)(2,1)} %copy-done.2), channel_id=1, source_target_pairs={{0,2},{1,3},{2,0},{3,1},{4,6},{5,7},{6,4},{7,5},{8,10},{9,11},{10,... | collective-permute-start | bytes 1572872 | tf_op jit(solution)/shard_map/ppermute | solution.py:309
  41.6 6.3 %collective-permute-start.6 = (bf16[256,512]{1,0:T(8,128)(2,1)}, bf16[256,512]{1,0:T(8,128)(2,1)S(1)}, u32[]{:S(2)}, u32[]{:S(2)}) collective-permute-start(bf16[256,512]{1,0:T(8,128)(2,1)} %collective-permute-done.2.up), channel_id=1, source_target_pairs={{0,4},{4,0},{8,12},{12,8},{16,20},{20,16},{24,28},{28,24},{32,36},... | collective-permute-start | bytes 786440 | tf_op jit(solution)/shard_map/ppermute | solution.py:327
  43.5 4.4 %collective-permute-start.7 = (bf16[256,512]{1,0:T(8,128)(2,1)S(1)}, bf16[256,512]{1,0:T(8,128)(2,1)S(1)}, u32[]{:S(2)}, u32[]{:S(2)}) collective-permute-start(bf16[256,512]{1,0:T(8,128)(2,1)S(1)} %get-tuple-element.27), channel_id=1, source_target_pairs={{0,4},{4,0},{8,12},{12,8},{16,20},{20,16},{24,28},{28,24},{32,36},... | collective-permute-start | bytes 786440 | tf_op jit(solution)/shard_map/ppermute | solution.py:328
  46.0 3.4 %collective-permute-start.5 = (bf16[256,512]{1,0:T(8,128)(2,1)S(1)}, bf16[256,512]{1,0:T(8,128)(2,1)S(1)}, u32[]{:S(2)}, u32[]{:S(2)}) collective-permute-start(bf16[256,512]{1,0:T(8,128)(2,1)S(1)} %get-tuple-element.28), channel_id=1, source_target_pairs={{0,4},{4,0},{8,12},{12,8},{16,20},{20,16},{24,28},{28,24},{32,36},... | collective-permute-start | bytes 786440 | tf_op jit(solution)/shard_map/ppermute | solution.py:325
